TPU v7x, 32 devices: a whole 2x2x4 slice. The times are simulated.
32 devices in a mesh: cand: 8 (over y, x, core), ref: 4 (over z).
Axes of the slice: x: 2, y: 2, z: 4, core: 2. Of those that a mesh axis runs over, the one named last changes fastest.
Arguments:
- cand_factor: float32 [8192, 512], P('cand'), may hold values from -6 to 6
- ref_factor: float32 [2048, 512], P('ref'), may hold values from -6 to 6
- cand_plan: float32 [8192, 128], P('cand'), may hold values from 0.0625 to 16
- ref_plan: float32 [2048, 128], P('ref'), may hold values from 0.0625 to 16
- weights: float32 [128], replicated, may hold values from 0.5 to 2
Outputs:
- new_cand_plan: float32 [8192, 128], P('cand')
- new_ref_plan: float32 [2048, 128], P('ref')
- new_weights: float32 [128], replicated
All inputs are finite; a program needn't handle non-finite values. Where the computation divides by a largest or mean magnitude, that divisor is 1e-20 or more.
Results may differ from a plain program's by a relative error of at most 0.00019.
Values sent between devices are 32-bit elements; how exact they have to be, the bound alone decides.
No kernel may reach another device: no remote copies, remote signals or barrier semaphores. Data moves between devices by JAX's collectives and lax.ppermute only.
A program may use at most 64 MiB of HBM per device.

v0:
```python
import jax
import jax.numpy as jnp
from jax import lax
from jax.sharding import PartitionSpec as P

ITERS = 3


step_size = 3.0
tiny_value = 1e-06


def contract_rows(left, right):
    return lax.dot_general(
        left,
        right,
        (((0,), (0,)), ((), ())),
        precision=lax.Precision.HIGHEST,
        preferred_element_type=jnp.float32,
    )


def on_device(cand_factor, ref_factor, cand_plan, ref_plan, weights):
    cand_count = lax.axis_size("cand")
    ref_count = lax.axis_size("ref")
    cand_total = cand_factor.shape[0] * cand_count
    ref_total = ref_factor.shape[0] * ref_count
    rank_width = weights.shape[0]
    cand_block, cand_local = (cand_factor, cand_plan)
    ref_block, ref_local = (ref_factor, ref_plan)
    cand_partial = contract_rows(cand_block, cand_local) / cand_total
    ref_partial = contract_rows(ref_block, ref_local) / ref_total
    cand_moment = lax.psum(cand_partial, "cand")
    ref_moment = lax.psum(ref_partial, "ref")
    grad_cand = jnp.dot(cand_block, ref_moment, precision=lax.Precision.HIGHEST) / weights[None, :]
    grad_ref = jnp.dot(ref_block, cand_moment, precision=lax.Precision.HIGHEST) / weights[None, :]
    grad_weights = -jnp.sum(cand_moment * ref_moment, axis=0) / (weights * weights)
    local_top = jnp.maximum(jnp.max(jnp.abs(grad_cand)), jnp.max(jnp.abs(grad_ref)))
    global_top = lax.pmax(local_top, ("cand", "ref"))
    top = jnp.maximum(global_top, jnp.max(jnp.abs(grad_weights))) + tiny_value
    kernel_cand = cand_local * jnp.exp(-step_size * grad_cand / top)
    kernel_ref = ref_local * jnp.exp(-step_size * grad_ref / top)
    kernel_weights = weights * jnp.exp(-step_size * grad_weights / top)
    scale_cand = jnp.ones((rank_width,), jnp.float32)
    scale_ref = jnp.ones((rank_width,), jnp.float32)
    for repeat_index in range(ITERS):
        row_cand = rank_width / jnp.dot(kernel_cand, scale_cand, precision=lax.Precision.HIGHEST)
        row_ref = rank_width / jnp.dot(kernel_ref, scale_ref, precision=lax.Precision.HIGHEST)
        cand_mass_part = (
            jnp.dot(row_cand, kernel_cand, precision=lax.Precision.HIGHEST) / cand_total
        )
        ref_mass_part = jnp.dot(row_ref, kernel_ref, precision=lax.Precision.HIGHEST) / ref_total
        mass_cand = lax.psum(cand_mass_part, "cand")
        mass_ref = lax.psum(ref_mass_part, "ref")
        new_weights = jnp.cbrt(kernel_weights * scale_cand * mass_cand * scale_ref * mass_ref)
        scale_cand = new_weights / mass_cand
        scale_ref = new_weights / mass_ref
    new_cand_plan = row_cand[:, None] * kernel_cand * scale_cand[None, :]
    new_ref_plan = row_ref[:, None] * kernel_ref * scale_ref[None, :]
    return (new_cand_plan, new_ref_plan, new_weights)


def solution(mesh):
    in_specs = (P("cand", None), P("ref", None), P("cand", None), P("ref", None), P())
    out_specs = (P("cand", None), P("ref", None), P())
    return jax.shard_map(
        on_device, mesh=mesh, in_specs=in_specs, out_specs=out_specs, check_vma=False
    )
```

profile of v0, /device:TPU:0, one launch (start us, length us, event | category | flops | bytes accessed | tf_op | source)
XLA Modules:
  0.0 237.8 jit_solution(1407843614711286646)
XLA Ops:
  7.3 1.5 copy-done
  8.8 5.2 %convolution_multiply_fusion = f32[512,128]{1,0:T(8,128)} fusion(f32[1024,512]{1,0:T(8,128)S(1)} %copy-done, f32[1024,128]{1,0:T(8,128)} %param.7), kind=kOutput, calls=%fused_computation.1 | convolution fusion | flops 805371904 | bytes 2883584 | tf_op jit(solution)/shard_map/dot_general | solution.py:14
  14.0 2.5 %convolution_multiply_fusion.1 = f32[512,128]{1,0:T(8,128)} fusion(f32[512,512]{1,0:T(8,128)S(1)} %copy-done.1, f32[512,128]{1,0:T(8,128)S(1)} %copy-done.4), kind=kOutput, calls=%fused_computation.3 | convolution fusion | flops 402718720 | bytes 1572864 | tf_op jit(solution)/shard_map/dot_general | solution.py:14
  16.6 0.8 copy.9
  17.4 53.3 %all-reduce.5.cloned.1.call-done = f32[512,128]{1,0:T(8,128)} async-done(((f32[512,128]{1,0:T(8,128)}), f32[512,128]{1,0:T(8,128)}) %all-reduce.5.cloned.1.call-update) | async-done | bytes 262160 | tf_op jit(solution)/shard_map/psum | solution.py:33
  70.7 3.4 %abs_reduce_fusion.1 = (f32[]{:T(128)}, f32[128,512]{1,0:T(8,128)}) fusion(f32[128]{0:T(128)S(1)} %copy-done.5, f32[512,128]{1,0:T(8,128)} %all-reduce.5.cloned.1.call-done, f32[512,512]{1,0:T(8,128)S(1)} %copy-done.1), kind=kOutput, calls=%fused_computation.22 | convolution fusion | flops 402849792 | bytes 1573380 | tf_op jit(solution)/shard_map/dot_general | solution.py:36
  74.1 34.3 %all-reduce.3.cloned.1.call-done = f32[512,128]{1,0:T(8,128)} async-done(((f32[512,128]{1,0:T(8,128)}), f32[512,128]{1,0:T(8,128)}) %all-reduce.3.cloned.1.call-update) | async-done | bytes 262160 | tf_op jit(solution)/shard_map/psum | solution.py:34
  108.4 4.2 %abs_reduce_fusion = (f32[]{:T(128)}, f32[128,1024]{1,0:T(8,128)}) fusion(f32[128]{0:T(128)S(1)} %copy-done.5, f32[512,128]{1,0:T(8,128)} %all-reduce.3.cloned.1.call-done, f32[1024,512]{1,0:T(8,128)S(1)} %copy-done), kind=kOutput, calls=%fused_computation.18 | convolution fusion | flops 805699584 | bytes 2884100 | tf_op jit(solution)/shard_map/dot_general | solution.py:35
  114.2 40.2 %pmax.7 = f32[]{:T(128)} all-reduce(f32[]{:T(128)S(6)} %max.8), channel_id=1, replica_groups=mesh['cand'=8,'ref'=4] {'cand','ref'}, use_global_device_ids=true, to_apply=%region_4.0 | all-reduce | flops 1 | bytes 8 | tf_op jit(solution)/shard_map/pmax | solution.py:39
  154.4 1.0 multiply_reduce_fusion
  155.4 0.6 abs_reduce_fusion.2
  157.3 1.1 bitcast_multiply_fusion.1
  158.7 0.3 fusion
  158.9 10.4 %psum.59 = f32[128]{0:T(128)S(1)} all-reduce(f32[128]{0:T(128)S(1)} %fusion), channel_id=1, replica_groups=mesh['cand'=8,'ref'=4] {'ref'}, use_global_device_ids=true, to_apply=%region_8.0 | all-reduce | flops 128 | bytes 1024 | tf_op jit(solution)/shard_map/psum | solution.py:54
  169.4 1.1 bitcast_multiply_fusion
  170.5 0.4 fusion.16
  170.9 0.5 fusion.5
  171.4 11.8 %psum.58 = f32[128]{0:T(128)S(1)} all-reduce(f32[128]{0:T(128)S(1)} %fusion.5), channel_id=1, replica_groups=mesh['cand'=8,'ref'=4] {'cand'}, use_global_device_ids=true, to_apply=%region_7.0 | all-reduce | flops 128 | bytes 1024 | tf_op jit(solution)/shard_map/psum | solution.py:53
  183.2 0.3 fusion.10
  183.5 0.4 fusion.12
  183.9 0.3 fusion.1
  184.2 8.4 %psum.61 = f32[128]{0:T(128)S(1)} all-reduce(f32[128]{0:T(128)S(1)} %fusion.1), channel_id=1, replica_groups=mesh['cand'=8,'ref'=4] {'ref'}, use_global_device_ids=true, to_apply=%region_10.0 | all-reduce | flops 128 | bytes 1024 | tf_op jit(solution)/shard_map/psum | solution.py:54
  192.6 0.5 fusion.4
  193.1 11.8 %psum.60 = f32[128]{0:T(128)S(1)} all-reduce(f32[128]{0:T(128)S(1)} %fusion.4), channel_id=1, replica_groups=mesh['cand'=8,'ref'=4] {'cand'}, use_global_device_ids=true, to_apply=%region_9.0 | all-reduce | flops 128 | bytes 1024 | tf_op jit(solution)/shard_map/psum | solution.py:53
  205.0 0.4 fusion.8
  205.4 0.5 fusion.3
  205.9 12.1 %psum.62 = f32[128]{0:T(128)S(1)} all-reduce(f32[128]{0:T(128)S(1)} %fusion.3), channel_id=1, replica_groups=mesh['cand'=8,'ref'=4] {'cand'}, use_global_device_ids=true, to_apply=%region_11.0 | all-reduce | flops 128 | bytes 1024 | tf_op jit(solution)/shard_map/psum | solution.py:53
  217.9 0.3 fusion.6
  218.2 0.3 fusion.2
  218.5 10.4 %psum.63 = f32[128]{0:T(128)S(1)} all-reduce(f32[128]{0:T(128)S(1)} %fusion.2), channel_id=1, replica_groups=mesh['cand'=8,'ref'=4] {'ref'}, use_global_device_ids=true, to_apply=%region_12.0 | all-reduce | flops 128 | bytes 1024 | tf_op jit(solution)/shard_map/psum | solution.py:54
  229.0 0.8 copy.11
  230.0 1.0 copy.10
  (32 shorter events, 0.9 us)
Async XLA Ops:
  7.2 1.6 copy-start
  7.2 6.8 %copy-start.1 = (f32[512,512]{1,0:T(8,128)S(1)}, f32[512,512]{1,0:T(8,128)}, u32[]{:S(2)}) copy-start(f32[512,512]{1,0:T(8,128)} %param.6) | copy-start | bytes 3145732
  7.2 6.8 %copy-start.4 = (f32[512,128]{1,0:T(8,128)S(1)}, f32[512,128]{1,0:T(8,128)}, u32[]{:S(2)}) copy-start(f32[512,128]{1,0:T(8,128)} %param.8) | copy-start | bytes 786436
  7.2 63.5 %copy-start.5 = (f32[128]{0:T(128)S(1)}, f32[128]{0:T(128)}, u32[]{:S(2)}) copy-start(f32[128]{0:T(128)} %param.9) | copy-start | bytes 1540
  7.2 63.5 %all-reduce.5.cloned.1.call-start = ((), (), s32[]{:S(2)}) async-start(), calls=%async_computation.1 | async-start | bytes 524288 | tf_op jit(solution)/shard_map/psum | solution.py:33
  14.0 94.5 %all-reduce.3.cloned.1.call-start = ((), (), s32[]{:S(2)}) async-start(), calls=%async_computation | async-start | bytes 524288 | tf_op jit(solution)/shard_map/psum | solution.py:34
  74.1 39.9 %copy-start.2 = (f32[1024,128]{1,0:T(8,128)S(1)}, f32[1024,128]{1,0:T(8,128)}, u32[]{:S(2)}) copy-start(f32[1024,128]{1,0:T(8,128)} %param.7) | copy-start | bytes 1572868
  74.1 80.3 %copy-start.3 = (f32[512,128]{1,0:T(8,128)S(1)}, f32[512,128]{1,0:T(8,128)}, u32[]{:S(2)}) copy-start(f32[512,128]{1,0:T(8,128)} %all-reduce.5.cloned.1.call-done) | copy-start | bytes 786436
  228.9 2.1 copy-start.6
Sparse Core Ops, SparseCore 0:
  14.1 56.5 all-reduce.4
  73.6 34.7 all-reduce.2
where the time goes:
time: 238 us
  blocking collectives  105 us (44%)
  waiting for transfers between devices  87.7 us (37%)
  matrix products  19.6 us (8%)
  between operations  16.8 us (7%)
  local copies, waits for them, and re-layouts  4.4 us (2%)
  other arithmetic  4.18 us (2%)
    psum x1, waiting for transfers between devices, on_device(): cand_moment = lax.psum(cand_partial, 'cand')  53.3 us
    pmax x1, blocking collectives, on_device(): global_top = lax.pmax(local_top, ('cand', 'ref'))  40.2 us
    psum x3, blocking collectives, on_device(): mass_cand = lax.psum(cand_mass_part, 'cand')  35.7 us
    psum x1, waiting for transfers between devices, on_device(): ref_moment = lax.psum(ref_partial, 'ref')  34.3 us
    psum x3, blocking collectives, on_device(): mass_ref = lax.psum(ref_mass_part, 'ref')  29.2 us
    dot_general x2, matrix products, contract_rows(): lax.dot_general(left, right, (((0,), (0,)), ((), ())), precision=lax.Prec...  7.68 us
  transfers between devices with their start and end apart: 2, of which 2 were waited for; matrix products, arithmetic and copies ran while one was open for 3% of the time, Pallas kernels for 0%

commit v1 on v0

v1 whole, which is shorter than its diff:
```python
import jax
import jax.numpy as jnp
from jax import lax
from jax.sharding import Mesh, PartitionSpec as P

ITERS = 3

step_size = 3.0
tiny_value = 1e-06

HIGH = lax.Precision.HIGH
f32 = jnp.float32


def dot_nt(left, right):
    return lax.dot_general(
        left, right, (((1,), (1,)), ((), ())), precision=HIGH, preferred_element_type=f32
    )


def dot_tn(left, right):
    return lax.dot_general(
        left, right, (((0,), (0,)), ((), ())), precision=HIGH, preferred_element_type=f32
    )


def partner_lists(count):
    if count & (count - 1) == 0:
        return [[(i, i ^ k) for i in range(count)] for k in range(1, count)]
    return [[(i, (i + k) % count) for i in range(count)] for k in range(1, count)]


def swap_core(array, core_count):
    if core_count == 1:
        return None
    return lax.ppermute(array, "core", [(0, 1), (1, 0)])


def share(array, axes, count):
    pieces = jnp.broadcast_to(array[None], (count,) + array.shape)
    return lax.all_to_all(pieces, axes, 0, 0)


def on_device(cand_factor, ref_factor, cand_plan, ref_plan, weights):
    chips, cores, refs = (lax.axis_size(a) for a in ("chip", "core", "ref"))
    chip, core, ref = (lax.axis_index(a) for a in ("chip", "core", "ref"))
    cand_rows, width = cand_factor.shape
    ref_rows = ref_factor.shape[0]
    rank = weights.shape[0]
    cand_total = cand_rows * chips * cores
    ref_total = ref_rows * refs
    half = width // cores
    cand_cols, ref_cols = rank // chips, rank // refs

    ref_half = lax.dynamic_slice_in_dim(ref_factor, core * half, half, 1)
    ref_part = dot_tn(ref_plan, ref_half) / ref_total
    blocks = ref_part.reshape(refs, ref_cols, half)
    ref_block = lax.dynamic_index_in_dim(blocks, ref, 0, False)
    arrived = []
    for pairs in partner_lists(refs):
        goes_to = jnp.array([b for _, b in pairs], jnp.int32)[ref]
        arrived.append(lax.ppermute(lax.dynamic_index_in_dim(blocks, goes_to, 0, False), "ref", pairs))

    cand_part = dot_tn(cand_plan, cand_factor) / cand_total
    mine = lax.dynamic_slice_in_dim(cand_part, core * half, half, 1)
    if cores > 1:
        mine = mine + swap_core(lax.dynamic_slice_in_dim(cand_part, (1 - core) * half, half, 1), cores)
    pieces = lax.all_to_all(mine.reshape(chips, cand_cols, half), "chip", 0, 0)
    cand_block = jnp.sum(pieces, axis=0)
    for piece in arrived:
        ref_block = ref_block + piece

    def whole_width(part):
        if cores == 1:
            return part
        other = swap_core(part, cores)
        low = jnp.where(core == 0, part, other)
        high = jnp.where(core == 0, other, part)
        return jnp.concatenate([low, high], axis=-1)

    both = whole_width(jnp.concatenate([cand_block, ref_block], axis=0))
    cand_cols_moment, ref_cols_moment = both[:cand_cols], both[cand_cols:]
    w_ref = lax.dynamic_slice_in_dim(weights, ref * ref_cols, ref_cols, 0)
    w_cand = lax.dynamic_slice_in_dim(weights, chip * cand_cols, cand_cols, 0)
    ref_share = lax.dynamic_slice_in_dim(ref_factor, core * (ref_rows // cores), ref_rows // cores, 0)
    local_top = jnp.maximum(
        jnp.max(jnp.abs(dot_nt(cand_factor, ref_cols_moment) / w_ref[None, :])),
        jnp.max(jnp.abs(dot_nt(ref_share, cand_cols_moment) / w_cand[None, :])),
    )

    if cand_cols % refs == 0 and ref_cols % chips == 0:
        a, b = cand_cols // refs, ref_cols // chips
        cand_piece = lax.dynamic_slice_in_dim(cand_block, ref * a, a, 0)
        ref_piece = lax.dynamic_slice_in_dim(ref_block, chip * b, b, 0)
        piece = jnp.concatenate([cand_piece, ref_piece, jnp.broadcast_to(local_top, (8, half))], axis=0)
        got = share(piece, ("chip", "ref"), chips * refs).reshape(chips, refs, a + b + 8, half)
        cand_m = got[:, :, :a].reshape(rank, half)
        ref_m = jnp.swapaxes(got[:, :, a : a + b], 0, 1).reshape(rank, half)
        tops = got[:, :, a + b :, :]
    else:
        a, b = half // refs, half // chips
        cand_piece = lax.dynamic_slice_in_dim(cand_block, ref * a, a, 1).reshape(-1)
        ref_piece = lax.dynamic_slice_in_dim(ref_block, chip * b, b, 1).reshape(-1)
        piece = jnp.concatenate([cand_piece, ref_piece, local_top[None]])
        got = share(piece, ("chip", "ref"), chips * refs).reshape(chips, refs, -1)
        n = cand_piece.shape[0]
        cand_m = got[:, :, :n].reshape(chips, refs, cand_cols, a).transpose(0, 2, 1, 3).reshape(rank, half)
        ref_m = got[:, :, n:-1].reshape(chips, refs, ref_cols, b).transpose(1, 2, 0, 3).reshape(rank, half)
        tops = got[:, :, -1:]
    top_here = jnp.max(tops)
    both = whole_width(jnp.concatenate([cand_m, ref_m, jnp.broadcast_to(top_here, (8, half))], axis=0))
    cand_moment, ref_moment = both[:rank], both[rank : 2 * rank]
    global_top = jnp.max(both[2 * rank :])

    grad_weights = -jnp.sum(cand_moment * ref_moment, axis=1) / (weights * weights)
    top = jnp.maximum(global_top, jnp.max(jnp.abs(grad_weights))) + tiny_value
    kernel_weights = weights * jnp.exp(-step_size * grad_weights / top)
    kernel_cand = cand_plan * jnp.exp(-step_size * (dot_nt(cand_factor, ref_moment) / weights[None, :]) / top)
    kernel_ref = ref_plan * jnp.exp(-step_size * (dot_nt(ref_factor, cand_moment) / weights[None, :]) / top)

    cand_sub = cand_rows // refs
    ref_sub = ref_rows // (chips * cores)
    mine_cand = lax.dynamic_slice_in_dim(kernel_cand, ref * cand_sub, cand_sub, 0)
    mine_ref = lax.dynamic_slice_in_dim(kernel_ref, (chip * cores + core) * ref_sub, ref_sub, 0)
    scale_cand = jnp.ones((rank,), f32)
    scale_ref = jnp.ones((rank,), f32)
    for _ in range(ITERS):
        last_cand, last_ref = scale_cand, scale_ref
        row_cand = rank / jnp.sum(mine_cand * scale_cand[None, :], axis=1, keepdims=True)
        row_ref = rank / jnp.sum(mine_ref * scale_ref[None, :], axis=1, keepdims=True)
        part = jnp.stack(
            [jnp.sum(row_cand * mine_cand, axis=0) / cand_total, jnp.sum(row_ref * mine_ref, axis=0) / ref_total]
        )
        mass = jnp.sum(share(part, ("chip", "core", "ref"), chips * cores * refs), axis=0)
        mass_cand, mass_ref = mass[0], mass[1]
        new_weights = jnp.cbrt(kernel_weights * scale_cand * mass_cand * scale_ref * mass_ref)
        scale_cand = new_weights / mass_cand
        scale_ref = new_weights / mass_ref
    row_cand = rank / jnp.sum(kernel_cand * last_cand[None, :], axis=1, keepdims=True)
    row_ref = rank / jnp.sum(kernel_ref * last_ref[None, :], axis=1, keepdims=True)
    new_cand_plan = row_cand * kernel_cand * scale_cand[None, :]
    new_ref_plan = row_ref * kernel_ref * scale_ref[None, :]
    return (new_cand_plan, new_ref_plan, new_weights)


def solution(mesh):
    cand, ref = mesh.shape["cand"], mesh.shape["ref"]
    cores = 2 if cand % 2 == 0 else 1
    finer = Mesh(mesh.devices.reshape(cand // cores, cores, ref), ("chip", "core", "ref"))
    rows = ("chip", "core")
    in_specs = (P(rows, None), P("ref", None), P(rows, None), P("ref", None), P())
    out_specs = (P(rows, None), P("ref", None), P())
    return jax.shard_map(on_device, mesh=finer, in_specs=in_specs, out_specs=out_specs, check_vma=False)
```

time: 238 us -> 103 us (0.43)
  waiting for transfers between devices: 87.7 us -> 16.2 us
  blocking collectives: 105 us -> 34.6 us
  starting transfers between devices: 0.08 us -> 12 us
  matrix products: 19.6 us -> 8.99 us
  between operations: 16.8 us -> 9.54 us
  local copies, waits for them, and re-layouts: 4.4 us -> 11.1 us
  other arithmetic: 4.18 us -> 10 us
    psum x2 -> x0, waiting for transfers between devices: 87.6 us -> none  [the longest x1 53.3 us: on_device(): cand_moment = lax.psum(cand_partial, 'cand')]
    psum x6 -> x0, blocking collectives: 64.9 us -> none  [the longest x3 35.7 us: on_device(): mass_cand = lax.psum(cand_mass_part, 'cand')]
    pmax x1 -> x0, blocking collectives: 40.2 us -> none  [on_device(): global_top = lax.pmax(local_top, ('cand', 'ref'))]
    all_to_all x0 -> x3, blocking collectives: none -> 34.6 us  [share(): return lax.all_to_all(pieces, axes, 0, 0)]
    all_to_all x0 -> x2, waiting for transfers between devices: none -> 11.6 us  [the longest x1 7.27 us: share(): return lax.all_to_all(pieces, axes, 0, 0)]
    dot_general x16 -> x6, matrix products: 19.6 us -> 8.99 us  [the longest x4 5.63 us: dot_nt(): lax.dot_general(left, right, (((1,), (1,)), ((), ())), precision=HIGH, pr...]
    all_to_all x0 -> x2, starting transfers between devices: none -> 6.28 us  [the longest x1 3.72 us: on_device(): pieces = lax.all_to_all(mine.reshape(chips, cand_cols, half), 'chip', 0, 0)]
    ppermute x0 -> x6, starting transfers between devices: none -> 5.72 us  [the longest x3 5.64 us: on_device(): lax.ppermute(lax.dynamic_index_in_dim(blocks, goes_to, 0, False), 'ref',...]
  transfers between devices with their start and end apart: 2 -> 8, of which waited for: 2 -> 5; matrix products, arithmetic and copies ran while one was open for 3% -> 6% of each run, Pallas kernels for 0% -> 0%
where the time goes in v1:
time: 103 us
  blocking collectives  34.6 us (34%)
  waiting for transfers between devices  16.2 us (16%)
  starting transfers between devices  12 us (12%)
  local copies, waits for them, and re-layouts  11.1 us (11%)
  other arithmetic  10 us (10%)
  between operations  9.54 us (9%)
  matrix products  8.99 us (9%)
    all_to_all x3, blocking collectives, share(): return lax.all_to_all(pieces, axes, 0, 0)  34.6 us
    all_to_all x1, waiting for transfers between devices, share(): return lax.all_to_all(pieces, axes, 0, 0)  7.27 us
    ppermute x3, starting transfers between devices, on_device(): lax.ppermute(lax.dynamic_index_in_dim(blocks, goes_to, 0, False), 'ref',...  5.64 us
    dot_general x4, matrix products, dot_nt(): lax.dot_general(left, right, (((1,), (1,)), ((), ())), precision=HIGH, pr...  5.63 us
    all_to_all x1, waiting for transfers between devices, on_device(): pieces = lax.all_to_all(mine.reshape(chips, cand_cols, half), 'chip', 0, 0)  4.32 us
    dynamic_slice x3, local copies, waits for them, and re-layouts, on_device(): goes_to = jnp.array([b for _, b in pairs], jnp.int32)[ref]  3.88 us
    all_to_all x1, starting transfers between devices, on_device(): pieces = lax.all_to_all(mine.reshape(chips, cand_cols, half), 'chip', 0, 0)  3.72 us
    unnamed x20, local copies, waits for them, and re-layouts  3.71 us
  transfers between devices with their start and end apart: 8, of which 5 were waited for; matrix products, arithmetic and copies ran while one was open for 6% of the time, Pallas kernels for 0%

profile of v1, /device:TPU:0, one launch (start us, length us, event | category | flops | bytes accessed | tf_op | source)
XLA Modules:
  0.0 102.6 jit_solution(18039699166120383845)
XLA Ops:
  0.6 1.4 %dynamic_slice.57 = s32[1]{0:T(128)} dynamic-slice(s32[4]{0:T(128)} %constant.79.clone, s32[]{:T(128)S(6)} %select_n.70), dynamic_slice_sizes={1} | dynamic-slice | bytes 12 | tf_op jit(solution)/shard_map/dynamic_slice | solution.py:61
  3.3 1.2 %dynamic_slice.59 = s32[1]{0:T(128)} dynamic-slice(s32[4]{0:T(128)} %constant.80.clone, s32[]{:T(128)S(6)} %select_n.70), dynamic_slice_sizes={1} | dynamic-slice | bytes 12 | tf_op jit(solution)/shard_map/dynamic_slice | solution.py:61
  5.9 1.2 %dynamic_slice.61 = s32[1]{0:T(128)} dynamic-slice(s32[4]{0:T(128)} %constant.81.clone, s32[]{:T(128)S(6)} %select_n.70), dynamic_slice_sizes={1} | dynamic-slice | bytes 12 | tf_op jit(solution)/shard_map/dynamic_slice | solution.py:61
  10.4 1.5 %convolution_multiply_fusion.1 = f32[256,128]{0,1:T(8,128)S(1)} fusion(f32[512,128]{1,0:T(8,128)} %param.11, f32[512,512]{1,0:T(8,128)} %param.9, s32[]{:T(128)S(6)} %select_n.67), kind=kOutput, calls=%fused_computation.13 | convolution fusion | flops 100696064 | bytes 917508 | tf_op jit(solution)/shard_map/dot_general | solution.py:22
  12.5 3.1 %collective-permute-start.1 = (f32[32,256]{1,0:T(8,128)}, f32[32,256]{1,0:T(8,128)}, u32[]{:S(2)}, u32[]{:S(2)}) collective-permute-start(f32[32,256]{1,0:T(8,128)} %get-tuple-element.34), channel_id=1, source_target_pairs={{0,1},{1,0},{2,3},{3,2},{4,5},{5,4},{6,7},{7,6},{8,9},{9,8},{10,11... | collective-permute-start | bytes 98312 | tf_op jit(solution)/shard_map/ppermute | solution.py:62
  15.6 2.6 %collective-permute-start.2 = (f32[32,256]{1,0:T(8,128)}, f32[32,256]{1,0:T(8,128)}, u32[]{:S(2)}, u32[]{:S(2)}) collective-permute-start(f32[32,256]{1,0:T(8,128)} %get-tuple-element.36), channel_id=1, source_target_pairs={{0,2},{1,3},{2,0},{3,1},{4,6},{5,7},{6,4},{7,5},{8,10},{9,11},{10,... | collective-permute-start | bytes 98312 | tf_op jit(solution)/shard_map/ppermute | solution.py:62
  18.2 1.9 %convolution_multiply_fusion = f32[128,512]{1,0:T(8,128)S(1)} fusion(f32[1024,128]{1,0:T(8,128)} %param.10, f32[1024,512]{1,0:T(8,128)S(1)} %copy-done), kind=kOutput, calls=%fused_computation.6 | convolution fusion | flops 402718720 | bytes 2883584 | tf_op jit(solution)/shard_map/dot_general | solution.py:22
  20.1 0.7 constant_dynamic-slice_fusion.2
  21.3 2.9 %collective-permute-done.3 = f32[32,256]{1,0:T(8,128)} collective-permute-done((f32[32,256]{1,0:T(8,128)}, f32[32,256]{1,0:T(8,128)}, u32[]{:S(2)}, u32[]{:S(2)}) %collective-permute-start.3) | collective-permute-done | bytes 32800 | tf_op jit(solution)/shard_map/ppermute | solution.py:62
  24.2 1.4 %fusion.21 = f32[32,256]{1,0:T(8,128)} fusion(f32[32,256]{1,0:T(8,128)} %collective-permute-done.3, f32[32,256]{1,0:T(8,128)} %collective-permute-done.2, f32[32,256]{1,0:T(8,128)} %collective-permute-done.1, f32[4,32,256]{2,1,0:T(8,128)S(1)} %bitcast.96, s32[]{:T(128)S(6)} %select_n.70), kind=kLoop, calls=%fused_computation.59 | loop fusion | flops 24576 | bytes 163844 | tf_op jit(solution)/shard_map/add | solution.py:71
  25.6 1.6 %dynamic-slice_add_fusion = f32[128,256]{1,0:T(8,128)} fusion(f32[128,256]{1,0:T(8,128)} %collective-permute-done, f32[128,512]{1,0:T(8,128)S(1)} %convolution_multiply_fusion, s32[]{:T(128)S(6)} %select_n.67), kind=kLoop, calls=%fused_computation.45 | loop fusion | flops 32768 | bytes 393220 | tf_op jit(solution)/shard_map/add | solution.py:67
  27.2 3.7 %all-to-all-start = ((f32[4,32,256]{2,1,0:T(8,128)}), f32[4,32,256]{2,1,0:T(8,128)S(1)}, u32[]{:S(2)}, u32[]{:S(2)}) async-start(f32[4,32,256]{2,1,0:T(8,128)} %bitcast.97), calls=%async_computation | async-start | bytes 262144 | tf_op jit(solution)/shard_map/all_to_all | solution.py:68
  30.9 0.7 constant_dynamic-slice_fusion
  31.6 4.3 %all-to-all-done = f32[4,32,256]{2,1,0:T(8,128)S(1)} async-done(((f32[4,32,256]{2,1,0:T(8,128)}), f32[4,32,256]{2,1,0:T(8,128)S(1)}, u32[]{:S(2)}, u32[]{:S(2)}) %all-to-all-start) | async-done | bytes 131104 | tf_op jit(solution)/shard_map/all_to_all | solution.py:68
  36.0 0.8 pad_maximum_fusion.4
  36.7 1.2 %collective-permute-done.4 = f32[64,256]{1,0:T(8,128)S(1)} collective-permute-done((f32[64,256]{1,0:T(8,128)S(1)}, f32[64,256]{1,0:T(8,128)S(1)}, u32[]{:S(2)}, u32[]{:S(2)}) %collective-permute-start.4) | collective-permute-done | bytes 65568 | tf_op jit(solution)/shard_map/ppermute | solution.py:36
  38.0 0.8 broadcast_select_fusion.2
  38.8 1.0 fusion.13
  39.7 1.6 %fusion.12 = f32[]{:T(128)} fusion(f32[1024,512]{1,0:T(8,128)S(1)} %copy-done, f32[64,256]{1,0:T(8,128)S(1)} %get-tuple-element.33, f32[64,256]{1,0:T(8,128)S(1)} %get-tuple-element.32, f32[32]{0:T(128)S(1)} %get-tuple-element.38), kind=kOutput, calls=%fused_computation.22 | convolution fusion | flops 100777984 | bytes 2228356 | tf_op jit(solution)/shard_map/dot_general | solution.py:16
  42.9 16.6 %all_to_all.25 = f32[16,24,256]{2,1,0:T(8,128)S(1)} all-to-all(f32[16,24,256]{2,1,0:T(8,128)S(1)} %broadcast_in_dim.13), channel_id=1, replica_groups=mesh['chip'=4,'core'=2,'ref'=4] {'chip','ref'}, dimensions={0} | all-to-all | bytes 786432 | tf_op jit(solution)/shard_map/all_to_all | solution.py:41
  61.0 1.0 copy.31
  62.0 0.8 copy.32
  62.8 1.1 %broadcast_select_fusion.1 = (f32[264,256]{1,0:T(8,128)S(1)}, f32[264,256]{1,0:T(8,128)S(1)}) fusion(f32[264,256]{1,0:T(8,128)} %collective-permute-done.5, pred[]{:T(512)S(6)} %eq.2, f32[264]{0:T(512)S(1)} %pad.10.clone, f32[128,256]{1,0:T(8,128)S(1)} %bitcast.92, f32[128,256]{1,0:T(8,128)S(1)} %bitcast.94), kind=kLoop, calls=%fused_computation.35 | loop fusion | flops 270336 | bytes 1074209 | tf_op jit(solution)/shard_map/jit(_where)/select_n | solution.py:77
  64.6 0.7 abs_reduce_fusion
  66.7 2.4 %fusion.4 = f32[1024,128]{0,1:T(8,128)S(1)} fusion(f32[1024,128]{0,1:T(8,128)} %copy.31, f32[1024,512]{1,0:T(8,128)S(1)} %copy-done, f32[]{:T(128)S(6)} %add.74, f32[128]{0:T(128)S(1)} %copy-done.6, f32[264,256]{1,0:T(8,128)S(1)} %get-tuple-element.27, f32[264,256]{1,0:T(8,128)S(1)} %get-tuple-element.28), kind=kOutput, calls=%fused_computation.5 | convolution fusion | flops 403243008 | bytes 3686916 | tf_op jit(solution)/shard_map/dot_general | solution.py:16
  69.2 0.7 fusion.9
  70.3 9.1 %all_to_all.26 = f32[32,2,128]{2,1,0:T(2,128)S(1)} all-to-all(f32[32,2,128]{2,1,0:T(2,128)S(1)} %broadcast_in_dim.15), channel_id=1, replica_groups=mesh['chip'=4,'core'=2,'ref'=4] {'chip','core','ref'}, dimensions={0} | all-to-all | bytes 65536 | tf_op jit(solution)/shard_map/all_to_all | solution.py:41
  80.0 9.0 %all_to_all.27 = f32[32,2,128]{2,1,0:T(2,128)S(1)} all-to-all(f32[32,2,128]{2,1,0:T(2,128)S(1)} %broadcast_in_dim.16), channel_id=1, replica_groups=mesh['chip'=4,'core'=2,'ref'=4] {'chip','core','ref'}, dimensions={0} | all-to-all | bytes 65536 | tf_op jit(solution)/shard_map/all_to_all | solution.py:41
  90.6 2.6 %all-to-all-start.4 = ((f32[32,2,128]{2,1,0:T(2,128)}), f32[32,2,128]{2,1,0:T(2,128)S(1)}, u32[]{:S(2)}, u32[]{:S(2)}) async-start(f32[32,2,128]{2,1,0:T(2,128)} %broadcast_in_dim.17), calls=%async_computation.4 | async-start | bytes 65536 | tf_op jit(solution)/shard_map/all_to_all | solution.py:41
  93.2 7.3 %all-to-all-done.4 = f32[32,2,128]{2,1,0:T(2,128)S(1)} async-done(((f32[32,2,128]{2,1,0:T(2,128)}), f32[32,2,128]{2,1,0:T(2,128)S(1)}, u32[]{:S(2)}, u32[]{:S(2)}) %all-to-all-start.4) | async-done | bytes 32800 | tf_op jit(solution)/shard_map/all_to_all | solution.py:41
  100.6 0.8 copy.37
  101.6 1.0 copy.36
  (83 shorter events, 6.5 us)
Async XLA Ops:
  0.6 17.6 %copy-start = (f32[1024,512]{1,0:T(8,128)S(1)}, f32[1024,512]{1,0:T(8,128)}, u32[]{:S(2)}) copy-start(f32[1024,512]{1,0:T(8,128)} %param.8) | copy-start | bytes 6291460
  10.4 10.4 %copy-start.6 = (f32[128]{0:T(128)S(1)}, f32[128]{0:T(128)}, u32[]{:S(2)}) copy-start(f32[128]{0:T(128)} %param.12) | copy-start | bytes 1540
  12.5 8.3 %collective-permute-start.1 = (f32[32,256]{1,0:T(8,128)}, f32[32,256]{1,0:T(8,128)}, u32[]{:S(2)}, u32[]{:S(2)}) collective-permute-start(f32[32,256]{1,0:T(8,128)} %get-tuple-element.34), channel_id=1, source_target_pairs={{0,1},{1,0},{2,3},{3,2},{4,5},{5,4},{6,7},{7,6},{8,9},{9,8},{10,11... | collective-permute-start | bytes 98312 | tf_op jit(solution)/shard_map/ppermute | solution.py:62
  15.6 5.7 %collective-permute-start.2 = (f32[32,256]{1,0:T(8,128)}, f32[32,256]{1,0:T(8,128)}, u32[]{:S(2)}, u32[]{:S(2)}) collective-permute-start(f32[32,256]{1,0:T(8,128)} %get-tuple-element.36), channel_id=1, source_target_pairs={{0,2},{1,3},{2,0},{3,1},{4,6},{5,7},{6,4},{7,5},{8,10},{9,11},{10,... | collective-permute-start | bytes 98312 | tf_op jit(solution)/shard_map/ppermute | solution.py:62
  18.2 6.0 %collective-permute-start.3 = (f32[32,256]{1,0:T(8,128)}, f32[32,256]{1,0:T(8,128)}, u32[]{:S(2)}, u32[]{:S(2)}) collective-permute-start(f32[32,256]{1,0:T(8,128)} %get-tuple-element.35), channel_id=1, source_target_pairs={{0,3},{1,2},{2,1},{3,0},{4,7},{5,6},{6,5},{7,4},{8,11},{9,10},{10,... | collective-permute-start | bytes 98312 | tf_op jit(solution)/shard_map/ppermute | solution.py:62
  18.2 20.6 %copy-start.3 = (f32[512,512]{1,0:T(8,128)S(1)}, f32[512,512]{1,0:T(8,128)}, u32[]{:S(2)}) copy-start(f32[512,512]{1,0:T(8,128)} %param.9) | copy-start | bytes 3145732
  20.7 4.9 %collective-permute-start = (f32[128,256]{1,0:T(8,128)}, f32[128,256]{1,0:T(8,128)}, u32[]{:S(2)}, u32[]{:S(2)}) collective-permute-start(f32[128,256]{1,0:T(8,128)} %constant_dynamic-slice_fusion.2), channel_id=1, source_target_pairs={{0,4},{4,0},{1,5},{5,1},{2,6},{6,2},{3,7},{7,3},{8,12},{12,8},{9,1... | collective-permute-start | bytes 393224 | tf_op jit(solution)/shard_map/ppermute | solution.py:36
  27.2 8.7 %all-to-all-start = ((f32[4,32,256]{2,1,0:T(8,128)}), f32[4,32,256]{2,1,0:T(8,128)S(1)}, u32[]{:S(2)}, u32[]{:S(2)}) async-start(f32[4,32,256]{2,1,0:T(8,128)} %bitcast.97), calls=%async_computation | async-start | bytes 262144 | tf_op jit(solution)/shard_map/all_to_all | solution.py:68
  36.7 1.3 %collective-permute-start.4 = (f32[64,256]{1,0:T(8,128)S(1)}, f32[64,256]{1,0:T(8,128)S(1)}, u32[]{:S(2)}, u32[]{:S(2)}) collective-permute-start(f32[64,256]{1,0:T(8,128)S(1)} %pad_maximum_fusion.4), channel_id=1, source_target_pairs={{0,4},{4,0},{1,5},{5,1},{2,6},{6,2},{3,7},{7,3},{8,12},{12,8},{9,1... | collective-permute-start | bytes 196616 | tf_op jit(solution)/shard_map/ppermute | solution.py:36
  39.7 21.3 %copy-start.1 = (f32[1024,128]{1,0:T(8,128)S(1)}, f32[1024,128]{1,0:T(8,128)}, u32[]{:S(2)}) copy-start(f32[1024,128]{1,0:T(8,128)} %param.10) | copy-start | bytes 1572868
  41.3 20.6 %copy-start.2 = (f32[512,128]{1,0:T(8,128)S(1)}, f32[512,128]{1,0:T(8,128)}, u32[]{:S(2)}) copy-start(f32[512,128]{1,0:T(8,128)} %param.11) | copy-start | bytes 786436
  60.9 1.9 %collective-permute-start.5 = (f32[264,256]{1,0:T(8,128)S(1)}, f32[264,256]{1,0:T(8,128)}, u32[]{:S(2)}, u32[]{:S(2)}) collective-permute-start(f32[264,256]{1,0:T(8,128)S(1)} %maximum_maximum_fusion), channel_id=1, source_target_pairs={{0,4},{4,0},{1,5},{5,1},{2,6},{6,2},{3,7},{7,3},{8,12},{12,8},{9,1... | collective-permute-start | bytes 811016 | tf_op jit(solution)/shard_map/ppermute | solution.py:36
  66.7 2.6 %copy-start.4 = (f32[512,512]{1,0:T(8,128)S(1)}, f32[512,512]{1,0:T(8,128)}, u32[]{:S(2)}) copy-start(f32[512,512]{1,0:T(8,128)} %param.9) | copy-start | bytes 3145732
  66.7 2.6 %copy-start.5 = (f32[512,128]{0,1:T(8,128)S(1)}, f32[512,128]{0,1:T(8,128)}, u32[]{:S(2)}) copy-start(f32[512,128]{0,1:T(8,128)} %copy.32) | copy-start | bytes 786436
  90.6 9.9 %all-to-all-start.4 = ((f32[32,2,128]{2,1,0:T(2,128)}), f32[32,2,128]{2,1,0:T(2,128)S(1)}, u32[]{:S(2)}, u32[]{:S(2)}) async-start(f32[32,2,128]{2,1,0:T(2,128)} %broadcast_in_dim.17), calls=%async_computation.4 | async-start | bytes 65536 | tf_op jit(solution)/shard_map/all_to_all | solution.py:41
  100.5 2.1 %copy-start.7 = (f32[128]{0:T(128)}, f32[128]{0:T(128)S(1)}, u32[]{:S(2)}) copy-start(f32[128]{0:T(128)S(1)} %get-tuple-element.19) | copy-start | bytes 1540

commit v2 on v1

--- a/solution.py
+++ b/solution.py
@@ -1,6 +1,8 @@
 import jax
 import jax.numpy as jnp
 from jax import lax
+from jax.experimental import pallas as pl
+from jax.experimental.pallas import tpu as pltpu
 from jax.sharding import Mesh, PartitionSpec as P
 
 ITERS = 3
@@ -41,7 +43,7 @@
     return lax.all_to_all(pieces, axes, 0, 0)
 
 
-def on_device(cand_factor, ref_factor, cand_plan, ref_plan, weights):
+def on_device_any(cand_factor, ref_factor, cand_plan, ref_plan, weights):
     chips, cores, refs = (lax.axis_size(a) for a in ("chip", "core", "ref"))
     chip, core, ref = (lax.axis_index(a) for a in ("chip", "core", "ref"))
     cand_rows, width = cand_factor.shape
@@ -143,6 +145,266 @@
     return (new_cand_plan, new_ref_plan, new_weights)
 
 
+bf16 = jnp.bfloat16
+
+
+def split(x):
+    high = x.astype(bf16)
+    return high, (x - high.astype(f32)).astype(bf16)
+
+
+def mxu(left, right, dims):
+    return lax.dot_general(left, right, (dims, ((), ())), preferred_element_type=f32)
+
+
+def rows_by_cols(left, right):
+    lh, ll = split(left)
+    rh, rl = split(right)
+    nn = ((1,), (0,))
+    return mxu(lh, rh, nn) + (mxu(lh, rl, nn) + mxu(ll, rh, nn))
+
+
+def rows_by_rows(left, right):
+    n = right.shape[0]
+    lh, ll = split(left)
+    rh, rl = split(right)
+    nt = ((1,), (1,))
+    wide = mxu(lh, jnp.concatenate([rh, rl], axis=0), nt)
+    return wide[:, :n] + (wide[:, n:] + mxu(ll, rh, nt))
+
+
+def call(body, out_shapes, *args, scratch=()):
+    outs = [jax.ShapeDtypeStruct(s, f32) for s in out_shapes]
+    return pl.pallas_call(
+        body,
+        out_shape=outs,
+        in_specs=[pl.BlockSpec(memory_space=pltpu.VMEM) for _ in args],
+        out_specs=[pl.BlockSpec(memory_space=pltpu.VMEM) for _ in outs],
+        scratch_shapes=[pltpu.VMEM(s, f32) for s in scratch],
+        compiler_params=pltpu.CompilerParams(vmem_limit_bytes=40 << 20),
+    )(*args)
+
+
+def largest(x):
+    return jnp.max(jnp.max(jnp.abs(x), axis=0, keepdims=True), axis=1, keepdims=True)
+
+
+def cube_root(x):
+    return jnp.exp(jnp.log(x) * (1.0 / 3.0))
+
+
+def on_device_tiled(cand_factor, ref_factor, cand_plan, ref_plan, weights):
+    chips, cores, refs = (lax.axis_size(a) for a in ("chip", "core", "ref"))
+    cand_rows, width = cand_factor.shape
+    ref_rows = ref_factor.shape[0]
+    rank = weights.shape[0]
+    cand_total = cand_rows * chips * cores
+    ref_total = ref_rows * refs
+    half = width // cores
+    ca, ra = rank // chips, rank // refs
+    cb, rb = ca // refs, ra // chips
+    lanes = half // 128
+    cand_sub = cand_rows // refs
+    ref_sub = ref_rows // (chips * cores)
+    everyone = chips * cores * refs
+    pairs = partner_lists(refs)
+    xor = refs & (refs - 1) == 0
+    weights_row = weights[None, :]
+
+    def moment_parts(factor_ref, plan_ref, *rest):
+        outs, full = rest[:-1], rest[-1]
+        core, ref = lax.axis_index("core"), lax.axis_index("ref")
+        here = factor_ref[:, pl.ds(pl.multiple_of(core * half, half), half)]
+        full[...] = rows_by_cols(plan_ref[...].T, here) / ref_total
+        for k in range(refs):
+            to = ref ^ k if xor else (ref + k) % refs
+            outs[k][...] = full[pl.ds(pl.multiple_of(to * ra, ra), ra), :]
+
+    blocks = call(
+        moment_parts, [(ra, half)] * refs, ref_factor, ref_plan, scratch=[(rank, half)]
+    )
+    arrived = [lax.ppermute(b, "ref", p) for b, p in zip(blocks[1:], pairs)]
+
+    def cand_parts(factor_ref, plan_ref, out):
+        whole = rows_by_cols(plan_ref[...].T, factor_ref[...]) / cand_total
+        for i in range(chips):
+            for j in range(cores):
+                out[i * cores + j] = whole[i * ca : (i + 1) * ca, j * half : (j + 1) * half]
+
+    (parts,) = call(cand_parts, [(chips * cores, ca, half)], cand_factor, cand_plan)
+    pieces = lax.all_to_all(parts, ("chip", "core"), 0, 0)
+
+    def own_blocks(pieces_ref, *rest):
+        out = rest[-1]
+        out[:ca, :] = jnp.sum(pieces_ref[...], axis=0)
+        total = rest[0][...]
+        for other in rest[1:-1]:
+            total = total + other[...]
+        out[ca:, :] = total
+
+    (mine,) = call(own_blocks, [(ca + ra, half)], pieces, blocks[0], *arrived)
+    other = swap_core(mine, cores)
+
+    def column_tops(mine_ref, other_ref, cand_ref, ref_ref, w_ref, out, ref_cols, cand_cols):
+        chip, core, ref = (lax.axis_index(a) for a in ("chip", "core", "ref"))
+        here, there = mine_ref[...], other_ref[...]
+        low = jnp.where(core == 0, here, there)
+        high = jnp.where(core == 0, there, here)
+        ref_cols[...] = jnp.zeros_like(ref_cols)
+        cand_cols[...] = jnp.zeros_like(cand_cols)
+        at_ref = pl.ds(pl.multiple_of(ref * ra, ra), ra)
+        at_cand = pl.ds(pl.multiple_of(chip * ca, ca), ca)
+        ref_cols[at_ref, :half] = low[ca:]
+        ref_cols[at_ref, half:] = high[ca:]
+        cand_cols[at_cand, :half] = low[:ca]
+        cand_cols[at_cand, half:] = high[:ca]
+        w = w_ref[...]
+        grad_cand = rows_by_rows(cand_ref[...], ref_cols[...])
+        share_rows = ref_rows // cores
+        ref_share = ref_ref[pl.ds(pl.multiple_of(core * share_rows, share_rows), share_rows), :]
+        grad_ref = rows_by_rows(ref_share, cand_cols[...])
+        tall = jnp.maximum(
+            jnp.max(jnp.abs(grad_cand), axis=0, keepdims=True), jnp.max(jnp.abs(grad_ref), axis=0, keepdims=True)
+        )
+        top = jnp.broadcast_to(tall / w, (8, rank))
+        cand_piece = mine_ref[pl.ds(pl.multiple_of(ref * cb, cb), cb), :]
+        ref_piece = mine_ref[pl.ds(pl.multiple_of(ca + chip * rb, rb), rb), :]
+        for to in range(chips * refs):
+            for lane in range(lanes):
+                at = slice(lane * 128, (lane + 1) * 128)
+                out[to, lane * cb : (lane + 1) * cb, :] = cand_piece[:, at]
+                out[to, lanes * cb + lane * rb : lanes * cb + (lane + 1) * rb, :] = ref_piece[:, at]
+            out[to, lanes * (cb + rb) :, :] = top
+
+    tall_piece = lanes * (cb + rb) + 8
+    (to_all,) = call(
+        column_tops,
+        [(chips * refs, tall_piece, 128)],
+        mine,
+        other,
+        cand_factor,
+        ref_factor,
+        weights_row,
+        scratch=[(rank, width), (rank, width)],
+    )
+    got = lax.all_to_all(to_all, ("chip", "ref"), 0, 0)
+    got_other = swap_core(got, cores)
+
+    def mass_part(kernel_cand, kernel_ref, scale_cand, scale_ref, out):
+        row_cand = rank / jnp.sum(kernel_cand * scale_cand, axis=1, keepdims=True)
+        row_ref = rank / jnp.sum(kernel_ref * scale_ref, axis=1, keepdims=True)
+        mass_cand = jnp.sum(row_cand * kernel_cand, axis=0, keepdims=True) / cand_total
+        mass_ref = jnp.sum(row_ref * kernel_ref, axis=0, keepdims=True) / ref_total
+        both = jnp.concatenate([mass_cand, mass_ref], axis=0)
+        out[...] = jnp.broadcast_to(both[None], (everyone, 2, rank))
+
+    def first_kernels(
+        got_ref, got_other_ref, cand_ref, cand_plan_ref, ref_ref, ref_plan_ref, w_ref,
+        cand_moment, ref_moment, state, sub_cand, sub_ref, out,
+    ):
+        chip, core, ref = (lax.axis_index(a) for a in ("chip", "core", "ref"))
+        tops = None
+        for i in range(chips):
+            for k in range(refs):
+                here, there = got_ref[i * refs + k], got_other_ref[i * refs + k]
+                low = jnp.where(core == 0, here, there)
+                high = jnp.where(core == 0, there, here)
+                for part, side in enumerate((low, high)):
+                    for lane in range(lanes):
+                        at = slice(part * half + lane * 128, part * half + (lane + 1) * 128)
+                        row = i * ca + k * cb
+                        cand_moment[row : row + cb, at] = side[lane * cb : (lane + 1) * cb]
+                        row = k * ra + i * rb
+                        start = lanes * cb + lane * rb
+                        ref_moment[row : row + rb, at] = side[start : start + rb]
+                    top = side[lanes * (cb + rb) :]
+                    tops = top if tops is None else jnp.maximum(tops, top)
+        w = w_ref[...]
+        product = cand_moment[...] * ref_moment[...]
+        folded = product[:, :128]
+        for lane in range(1, width // 128):
+            folded = folded + product[:, lane * 128 : (lane + 1) * 128]
+        grad_weights = -jnp.sum(folded.T, axis=0, keepdims=True) / (w * w)
+        top = jnp.maximum(jnp.max(tops[:1], axis=1, keepdims=True), largest(grad_weights)) + tiny_value
+        kernel_weights = w * jnp.exp(-step_size * grad_weights / top)
+        state[0:1, :] = kernel_weights
+        state[1:2, :] = jnp.broadcast_to(top, (1, rank))
+        state[2:8, :] = jnp.ones((6, rank), f32)
+        at = pl.ds(pl.multiple_of(ref * cand_sub, cand_sub), cand_sub)
+        grad = rows_by_rows(cand_ref[at, :], ref_moment[...]) / w
+        kernel_cand = cand_plan_ref[at, :] * jnp.exp(-step_size * grad / top)
+        at = pl.ds(pl.multiple_of((chip * cores + core) * ref_sub, ref_sub), ref_sub)
+        grad = rows_by_rows(ref_ref[at, :], cand_moment[...]) / w
+        kernel_ref = ref_plan_ref[at, :] * jnp.exp(-step_size * grad / top)
+        sub_cand[...] = kernel_cand
+        sub_ref[...] = kernel_ref
+        ones = jnp.ones((1, rank), f32)
+        mass_part(kernel_cand, kernel_ref, ones, ones, out)
+
+    cand_moment, ref_moment, state, sub_cand, sub_ref, out = call(
+        first_kernels,
+        [(rank, width), (rank, width), (8, rank), (cand_sub, rank), (ref_sub, rank), (everyone, 2, rank)],
+        got, got_other, cand_factor, cand_plan, ref_factor, ref_plan, weights_row,
+    )
+
+    def update(mass_ref, state):
+        mass = jnp.sum(mass_ref[...], axis=0)
+        mass_cand, mass_ref = mass[0:1], mass[1:2]
+        kernel_weights, scale_cand, scale_ref = state[0:1, :], state[2:3, :], state[3:4, :]
+        new_weights = cube_root(kernel_weights * scale_cand * mass_cand * scale_ref * mass_ref)
+        return new_weights, new_weights / mass_cand, new_weights / mass_ref
+
+    def next_masses(mass_ref, state_ref, sub_cand_ref, sub_ref_ref, new_state, out):
+        _, scale_cand, scale_ref = update(mass_ref, state_ref)
+        new_state[...] = state_ref[...]
+        new_state[2:3, :] = scale_cand
+        new_state[3:4, :] = scale_ref
+        mass_part(sub_cand_ref[...], sub_ref_ref[...], scale_cand, scale_ref, out)
+
+    for _ in range(ITERS - 1):
+        mass = lax.all_to_all(out, ("chip", "core", "ref"), 0, 0)
+        state, out = call(next_masses, [(8, rank), (everyone, 2, rank)], mass, state, sub_cand, sub_ref)
+    mass = lax.all_to_all(out, ("chip", "core", "ref"), 0, 0)
+
+    def scaled_rows(
+        cand_moment_ref, ref_moment_ref, state_ref, cand_ref, cand_plan_ref, ref_ref, ref_plan_ref, w_ref,
+        cand_out, ref_out,
+    ):
+        w = w_ref[...]
+        top = state_ref[1:2, :]
+        grad = rows_by_rows(cand_ref[...], ref_moment_ref[...]) / w
+        kernel_cand = cand_plan_ref[...] * jnp.exp(-step_size * grad / top)
+        cand_out[...] = kernel_cand * (rank / jnp.sum(kernel_cand * state_ref[2:3, :], axis=1, keepdims=True))
+        grad = rows_by_rows(ref_ref[...], cand_moment_ref[...]) / w
+        kernel_ref = ref_plan_ref[...] * jnp.exp(-step_size * grad / top)
+        ref_out[...] = kernel_ref * (rank / jnp.sum(kernel_ref * state_ref[3:4, :], axis=1, keepdims=True))
+
+    rows_cand, rows_ref = call(
+        scaled_rows, [(cand_rows, rank), (ref_rows, rank)],
+        cand_moment, ref_moment, state, cand_factor, cand_plan, ref_factor, ref_plan, weights_row,
+    )
+
+    def finish(mass_ref, state_ref, rows_cand_ref, rows_ref_ref, cand_out, ref_out, w_out):
+        new_weights, scale_cand, scale_ref = update(mass_ref, state_ref)
+        cand_out[...] = rows_cand_ref[...] * scale_cand
+        ref_out[...] = rows_ref_ref[...] * scale_ref
+        w_out[...] = new_weights
+
+    new_cand_plan, new_ref_plan, new_weights = call(
+        finish, [(cand_rows, rank), (ref_rows, rank), (1, rank)], mass, state, rows_cand, rows_ref
+    )
+    return new_cand_plan, new_ref_plan, new_weights.reshape(rank)
+
+
+def on_device(*args):
+    chips, cores, refs = (lax.axis_size(a) for a in ("chip", "core", "ref"))
+    rank, width = args[4].shape[0], args[0].shape[1]
+    rows = (args[0].shape[0] // refs, args[1].shape[0] // (chips * cores))
+    tiled = cores == 2 and rank == 128 and rank % (8 * chips * refs) == 0 and width % (128 * cores) == 0
+    tiled = tiled and all(n % 8 == 0 for n in rows)
+    return (on_device_tiled if tiled else on_device_any)(*args)
+
+
 def solution(mesh):
     cand, ref = mesh.shape["cand"], mesh.shape["ref"]
     cores = 2 if cand % 2 == 0 else 1

time: 103 us -> 74.7 us (0.73)
  other arithmetic: 10 us -> 0 us
  matrix products: 8.99 us -> 0 us
  between operations: 9.54 us -> 0.77 us
  Pallas kernels: 0 us -> 6.49 us
  waiting for transfers between devices: 16.2 us -> 10.3 us
  local copies, waits for them, and re-layouts: 11.1 us -> 9.77 us
    all_to_all x2, waiting for transfers between devices: 11.6 us -> 1.74 us  [the longest x1 1.74 us: on_device_tiled(): mass = lax.all_to_all(out, ('chip', 'core', 'ref'), 0, 0)]
    dot_general x6 -> x0, matrix products: 8.99 us -> none  [the longest x4 5.63 us: dot_nt(): lax.dot_general(left, right, (((1,), (1,)), ((), ())), precision=HIGH, pr...]
    pallas_call x0 -> x9, Pallas kernels: none -> 6.49 us  [call(): pl.pallas_call(body, out_shape=outs, in_specs=[pl.BlockSpec(memory_space=...]
    unnamed x20 -> x34, local copies, waits for them, and re-layouts: 3.71 us -> 9.77 us
    dynamic_slice x7 -> x0, local copies, waits for them, and re-layouts: 5.33 us -> none  [the longest x3 3.88 us: on_device(): goes_to = jnp.array([b for _, b in pairs], jnp.int32)[ref]]
    add x2 -> x0, other arithmetic: 2.99 us -> none  [the longest x1 1.57 us: on_device(): mine + swap_core(lax.dynamic_slice_in_dim(cand_part, (1 - core) * half, h...]
    ppermute x3, waiting for transfers between devices: 3.39 us -> 5.71 us  [on_device_tiled(): arrived = [lax.ppermute(b, 'ref', p) for b, p in zip(blocks[1:], pairs)]]
    reduce_sum x19 -> x0, other arithmetic: 1.97 us -> none  [the longest x3 0.55 us: on_device(): jnp.sum(row_ref * mine_ref, axis=0) / ref_total]
  transfers between devices with their start and end apart: 8 -> 7, of which waited for: 5 -> 5; matrix products, arithmetic and copies ran while one was open for 6% -> 0% of each run, Pallas kernels for 0% -> 2%
where the time goes in v2:
time: 74.7 us; the launch traced here: 74 us
  blocking collectives  34.3 us (46%)
  starting transfers between devices  12.4 us (17%)
  waiting for transfers between devices  10.3 us (14%)
  local copies, waits for them, and re-layouts  9.77 us (13%)
  Pallas kernels  6.49 us (9%)
  between operations  0.77 us (1%)
    all_to_all x2, blocking collectives, on_device_tiled(): mass = lax.all_to_all(out, ('chip', 'core', 'ref'), 0, 0)  18 us
    all_to_all x1, blocking collectives, on_device_tiled(): got = lax.all_to_all(to_all, ('chip', 'ref'), 0, 0)  16.3 us
    unnamed x34, local copies, waits for them, and re-layouts  9.77 us
    pallas_call x9, Pallas kernels, call(): pl.pallas_call(body, out_shape=outs, in_specs=[pl.BlockSpec(memory_space=...  6.49 us
    ppermute x3, waiting for transfers between devices, on_device_tiled(): arrived = [lax.ppermute(b, 'ref', p) for b, p in zip(blocks[1:], pairs)]  5.71 us
    all_to_all x1, starting transfers between devices, on_device_tiled(): pieces = lax.all_to_all(parts, ('chip', 'core'), 0, 0)  5.2 us
    ppermute x3, starting transfers between devices, on_device_tiled(): arrived = [lax.ppermute(b, 'ref', p) for b, p in zip(blocks[1:], pairs)]  4.57 us
    ppermute x2, waiting for transfers between devices, swap_core(): return lax.ppermute(array, 'core', [(0, 1), (1, 0)])  2.87 us
  transfers between devices with their start and end apart: 7, of which 5 were waited for; matrix products, arithmetic and copies ran while one was open for 0% of the time, Pallas kernels for 2%

profile of v2, /device:TPU:0, one launch (start us, length us, event | category | flops | bytes accessed | tf_op | source)
XLA Modules:
  0.0 74.0 jit_solution(17951309951070363932)
XLA Ops:
  0.6 1.6 %copy-done = f32[1024,512]{1,0:T(8,128)S(1)} copy-done((f32[1024,512]{1,0:T(8,128)S(1)}, f32[1024,512]{1,0:T(8,128)}, u32[]{:S(2)}) %copy-start) | copy-done | bytes 2097176
  2.2 1.0 %copy-done.3 = f32[1024,128]{1,0:T(8,128)S(1)} copy-done((f32[1024,128]{1,0:T(8,128)S(1)}, f32[1024,128]{1,0:T(8,128)}, u32[]{:S(2)}) %copy-start.3) | copy-done | bytes 524312
  3.3 0.7 shard_map.76
  4.0 0.7 copy-done.7
  4.7 5.2 %all-to-all-start = ((f32[8,32,256]{2,1,0:T(8,128)}), f32[8,32,256]{2,1,0:T(8,128)}, u32[]{:S(2)}, u32[]{:S(2)}) async-start(f32[8,32,256]{2,1,0:T(8,128)} %copy-done.7), calls=%async_computation | async-start | bytes 524288 | tf_op jit(solution)/shard_map/all_to_all | solution.py:235
  9.9 0.3 shard_map.77
  10.3 2.0 %collective-permute-start = (f32[32,256]{1,0:T(8,128)S(1)}, f32[32,256]{1,0:T(8,128)S(1)}, u32[]{:S(2)}, u32[]{:S(2)}) collective-permute-start(f32[32,256]{1,0:T(8,128)S(1)} %get-tuple-element.23), channel_id=1, source_target_pairs={{0,1},{1,0},{2,3},{3,2},{4,5},{5,4},{6,7},{7,6},{8,9},{9,8},{10,11... | collective-permute-start | bytes 98312 | tf_op jit(solution)/shard_map/ppermute | solution.py:226
  12.2 2.6 %collective-permute-start.1 = (f32[32,256]{1,0:T(8,128)S(1)}, f32[32,256]{1,0:T(8,128)S(1)}, u32[]{:S(2)}, u32[]{:S(2)}) collective-permute-start(f32[32,256]{1,0:T(8,128)S(1)} %get-tuple-element.24), channel_id=1, source_target_pairs={{0,2},{1,3},{2,0},{3,1},{4,6},{5,7},{6,4},{7,5},{8,10},{9,11},{10,... | collective-permute-start | bytes 98312 | tf_op jit(solution)/shard_map/ppermute | solution.py:226
  14.8 2.9 %collective-permute-done.1.rest_2_ = f32[32,256]{1,0:T(8,128)S(1)} collective-permute-done((f32[32,256]{1,0:T(8,128)S(1)}, f32[32,256]{1,0:T(8,128)S(1)}, u32[]{:S(2)}, u32[]{:S(2)}) %collective-permute-start.1) | collective-permute-done | bytes 32800 | tf_op jit(solution)/shard_map/ppermute | solution.py:226
  17.7 2.9 %collective-permute-done.2.rest_3_ = f32[32,256]{1,0:T(8,128)S(1)} collective-permute-done((f32[32,256]{1,0:T(8,128)S(1)}, f32[32,256]{1,0:T(8,128)S(1)}, u32[]{:S(2)}, u32[]{:S(2)}) %collective-permute-start.2) | collective-permute-done | bytes 32800 | tf_op jit(solution)/shard_map/ppermute | solution.py:226
  20.5 1.0 %shard_map.78.mine_ref = f32[64,256]{1,0:T(8,128)S(1)} custom-call(f32[8,32,256]{2,1,0:T(8,128)} %all-to-all-done.pieces_ref, f32[32,256]{1,0:T(8,128)S(1)} %get-tuple-element.22.rest_0_, f32[32,256]{1,0:T(8,128)S(1)} %collective-permute-done.rest_1_, f32[32,256]{1,0:T(8,128)S(1)} %collective-permute-done.1.rest_2_, f32[32,256]{1,0:T(8,128)S(1)} %collective-permute-done.2.rest_3_), custom_call_target="tpu_custom_call" | custom-call | tf_op jit(solution)/shard_map/pallas_call | solution.py:178
  21.5 0.1 collective-permute-start.3
  21.6 1.2 %collective-permute-done.3.other_ref = f32[64,256]{1,0:T(8,128)S(1)} collective-permute-done((f32[64,256]{1,0:T(8,128)S(1)}, f32[64,256]{1,0:T(8,128)S(1)}, u32[]{:S(2)}, u32[]{:S(2)}) %collective-permute-start.3) | collective-permute-done | bytes 65568 | tf_op jit(solution)/shard_map/ppermute | solution.py:38
  22.8 0.9 %shard_map.79 = f32[16,40,128]{2,1,0:T(8,128)S(1)} custom-call(f32[64,256]{1,0:T(8,128)S(1)} %shard_map.78.mine_ref, f32[64,256]{1,0:T(8,128)S(1)} %collective-permute-done.3.other_ref, f32[1024,512]{1,0:T(8,128)S(1)} %copy-done.1, f32[512,512]{1,0:T(8,128)S(1)} %copy-done.2, f32[1,128]{1,0:T(1,128)S(1)} %bitcast.2), custom_call_target="tpu_custom_call" | custom-call | tf_op jit(solution)/shard_map/pallas_call | solution.py:178
  23.8 16.3 %all_to_all.25.got_ref = f32[16,40,128]{2,1,0:T(8,128)S(1)} all-to-all(f32[16,40,128]{2,1,0:T(8,128)S(1)} %shard_map.79), channel_id=1, replica_groups=mesh['chip'=4,'core'=2,'ref'=4] {'chip','ref'}, dimensions={0} | all-to-all | bytes 655360 | tf_op jit(solution)/shard_map/all_to_all | solution.py:290
  40.1 1.6 %collective-permute-done.4.got_other_ref = f32[16,40,128]{2,1,0:T(8,128)S(1)} collective-permute-done((f32[16,40,128]{2,1,0:T(8,128)S(1)}, f32[16,40,128]{2,1,0:T(8,128)S(1)}, u32[]{:S(2)}, u32[]{:S(2)}) %collective-permute-start.4) | collective-permute-done | bytes 327712 | tf_op jit(solution)/shard_map/ppermute | solution.py:38
  41.7 0.5 shard_map.80
  42.2 9.0 %all_to_all.26.mass_ref = f32[32,2,128]{2,1,0:T(2,128)S(1)} all-to-all(f32[32,2,128]{2,1,0:T(2,128)S(1)} %get-tuple-element.26), channel_id=1, replica_groups=mesh['chip'=4,'core'=2,'ref'=4] {'chip','core','ref'}, dimensions={0} | all-to-all | bytes 65536 | tf_op jit(solution)/shard_map/all_to_all | solution.py:365
  51.2 0.2 shard_map.81
  51.4 9.0 %all_to_all.27.mass_ref = f32[32,2,128]{2,1,0:T(2,128)S(1)} all-to-all(f32[32,2,128]{2,1,0:T(2,128)S(1)} %get-tuple-element.30), channel_id=1, replica_groups=mesh['chip'=4,'core'=2,'ref'=4] {'chip','core','ref'}, dimensions={0} | all-to-all | bytes 65536 | tf_op jit(solution)/shard_map/all_to_all | solution.py:365
  60.4 0.8 %shard_map.82 = (f32[8,128]{1,0:T(8,128)S(1)}, f32[32,2,128]{2,1,0:T(2,128)}) custom-call(f32[32,2,128]{2,1,0:T(2,128)S(1)} %all_to_all.27.mass_ref, f32[8,128]{1,0:T(8,128)S(1)} %get-tuple-element.31.state_ref, f32[256,128]{1,0:T(8,128)S(1)} %get-tuple-element.28.sub_cand_ref, f32[64,128]{1,0:T(8,128)S(1)} %get-tuple-element.29.sub_ref_ref), custom_call_target="tpu_custom_call" | custom-call | tf_op jit(solution)/shard_map/pallas_call | solution.py:178
  61.2 2.6 %all-to-all-start.4 = ((f32[32,2,128]{2,1,0:T(2,128)}), f32[32,2,128]{2,1,0:T(2,128)S(1)}, u32[]{:S(2)}, u32[]{:S(2)}) async-start(f32[32,2,128]{2,1,0:T(2,128)} %get-tuple-element.32), calls=%async_computation.4 | async-start | bytes 65536 | tf_op jit(solution)/shard_map/all_to_all | solution.py:367
  63.8 1.0 %copy-done.5 = f32[1024,128]{1,0:T(8,128)S(1)} copy-done((f32[1024,128]{1,0:T(8,128)S(1)}, f32[1024,128]{1,0:T(8,128)}, u32[]{:S(2)}) %copy-start.5) | copy-done | bytes 524312
  64.8 0.9 %copy-done.13 = f32[128,512]{1,0:T(8,128)S(1)} copy-done((f32[128,512]{1,0:T(8,128)S(1)}, f32[128,512]{1,0:T(8,128)}, u32[]{:S(2)}) %copy-start.13) | copy-done | bytes 262168
  65.8 0.9 %copy-done.15 = f32[128,512]{1,0:T(8,128)S(1)} copy-done((f32[128,512]{1,0:T(8,128)S(1)}, f32[128,512]{1,0:T(8,128)}, u32[]{:S(2)}) %copy-start.15) | copy-done | bytes 262168
  66.7 1.1 %shard_map.83 = (f32[1024,128]{1,0:T(8,128)S(1)}, f32[512,128]{1,0:T(8,128)S(1)}) custom-call(f32[128,512]{1,0:T(8,128)S(1)} %copy-done.13, f32[128,512]{1,0:T(8,128)S(1)} %copy-done.15, f32[8,128]{1,0:T(8,128)S(1)} %get-tuple-element.33.state_ref, f32[1024,512]{1,0:T(8,128)S(1)} %copy-done.1, f32[1024,128]{1,0:T(8,128)S(1)} %copy-done.5, ...), custom_call_target="tpu_custom_call" | custom-call | tf_op jit(solution)/shard_map/pallas_call | solution.py:178
  67.9 0.8 %copy-done.8 = f32[1024,128]{1,0:T(8,128)} copy-done((f32[1024,128]{1,0:T(8,128)}, f32[1024,128]{1,0:T(8,128)S(1)}, u32[]{:S(2)}) %copy-start.8) | copy-done | bytes 524312
  68.7 0.7 copy-done.10
  69.4 1.7 %all-to-all-done.4.mass_ref = f32[32,2,128]{2,1,0:T(2,128)S(1)} async-done(((f32[32,2,128]{2,1,0:T(2,128)}), f32[32,2,128]{2,1,0:T(2,128)S(1)}, u32[]{:S(2)}, u32[]{:S(2)}) %all-to-all-start.4) | async-done | bytes 32800 | tf_op jit(solution)/shard_map/all_to_all | solution.py:367
  71.1 1.0 %copy-done.9 = f32[1024,128]{1,0:T(8,128)S(1)} copy-done((f32[1024,128]{1,0:T(8,128)S(1)}, f32[1024,128]{1,0:T(8,128)}, u32[]{:S(2)}) %copy-start.9) | copy-done | bytes 524312
  72.1 0.9 %copy-done.11 = f32[512,128]{1,0:T(8,128)S(1)} copy-done((f32[512,128]{1,0:T(8,128)S(1)}, f32[512,128]{1,0:T(8,128)}, u32[]{:S(2)}) %copy-start.11) | copy-done | bytes 262168
  73.1 1.0 %shard_map.84 = (f32[1024,128]{1,0:T(8,128)}, f32[512,128]{1,0:T(8,128)}, f32[1,128]{1,0:T(1,128)}) custom-call(f32[32,2,128]{2,1,0:T(2,128)S(1)} %all-to-all-done.4.mass_ref, f32[8,128]{1,0:T(8,128)S(1)} %get-tuple-element.33.state_ref, f32[1024,128]{1,0:T(8,128)S(1)} %copy-done.9, f32[512,128]{1,0:T(8,128)S(1)} %copy-done.11), custom_call_target="tpu_custom_call" | custom-call | tf_op jit(solution)/shard_map/pallas_call | solution.py:178
  (28 shorter events, 0.1 us)
Async XLA Ops:
  0.6 1.6 %copy-start = (f32[1024,512]{1,0:T(8,128)S(1)}, f32[1024,512]{1,0:T(8,128)}, u32[]{:S(2)}) copy-start(f32[1024,512]{1,0:T(8,128)} %cand_ref.5) | copy-start | bytes 6291460
  2.2 1.0 %copy-start.3 = (f32[1024,128]{1,0:T(8,128)S(1)}, f32[1024,128]{1,0:T(8,128)}, u32[]{:S(2)}) copy-start(f32[1024,128]{1,0:T(8,128)} %cand_plan_ref.3) | copy-start | bytes 1572868
  3.3 6.6 %copy-start.2 = (f32[512,512]{1,0:T(8,128)S(1)}, f32[512,512]{1,0:T(8,128)}, u32[]{:S(2)}) copy-start(f32[512,512]{1,0:T(8,128)} %ref_ref.5) | copy-start | bytes 3145732
  3.3 6.6 %copy-start.6 = (f32[512,128]{1,0:T(8,128)S(1)}, f32[512,128]{1,0:T(8,128)}, u32[]{:S(2)}) copy-start(f32[512,128]{1,0:T(8,128)} %ref_plan_ref.3) | copy-start | bytes 786436
  3.3 19.6 %copy-start.1 = (f32[1024,512]{1,0:T(8,128)S(1)}, f32[1024,512]{1,0:T(8,128)}, u32[]{:S(2)}) copy-start(f32[1024,512]{1,0:T(8,128)} %cand_ref.5) | copy-start | bytes 6291460
  3.3 19.6 %copy-start.16 = (f32[128]{0:T(128)S(1)}, f32[128]{0:T(128)}, u32[]{:S(2)}) copy-start(f32[128]{0:T(128)} %param.9) | copy-start | bytes 1540
  4.0 0.7 copy-start.7
  4.7 15.9 %all-to-all-start = ((f32[8,32,256]{2,1,0:T(8,128)}), f32[8,32,256]{2,1,0:T(8,128)}, u32[]{:S(2)}, u32[]{:S(2)}) async-start(f32[8,32,256]{2,1,0:T(8,128)} %copy-done.7), calls=%async_computation | async-start | bytes 524288 | tf_op jit(solution)/shard_map/all_to_all | solution.py:235
  10.3 4.6 %collective-permute-start = (f32[32,256]{1,0:T(8,128)S(1)}, f32[32,256]{1,0:T(8,128)S(1)}, u32[]{:S(2)}, u32[]{:S(2)}) collective-permute-start(f32[32,256]{1,0:T(8,128)S(1)} %get-tuple-element.23), channel_id=1, source_target_pairs={{0,1},{1,0},{2,3},{3,2},{4,5},{5,4},{6,7},{7,6},{8,9},{9,8},{10,11... | collective-permute-start | bytes 98312 | tf_op jit(solution)/shard_map/ppermute | solution.py:226
  12.2 5.5 %collective-permute-start.1 = (f32[32,256]{1,0:T(8,128)S(1)}, f32[32,256]{1,0:T(8,128)S(1)}, u32[]{:S(2)}, u32[]{:S(2)}) collective-permute-start(f32[32,256]{1,0:T(8,128)S(1)} %get-tuple-element.24), channel_id=1, source_target_pairs={{0,2},{1,3},{2,0},{3,1},{4,6},{5,7},{6,4},{7,5},{8,10},{9,11},{10,... | collective-permute-start | bytes 98312 | tf_op jit(solution)/shard_map/ppermute | solution.py:226
  14.8 5.7 %collective-permute-start.2 = (f32[32,256]{1,0:T(8,128)S(1)}, f32[32,256]{1,0:T(8,128)S(1)}, u32[]{:S(2)}, u32[]{:S(2)}) collective-permute-start(f32[32,256]{1,0:T(8,128)S(1)} %get-tuple-element.25), channel_id=1, source_target_pairs={{0,3},{1,2},{2,1},{3,0},{4,7},{5,6},{6,5},{7,4},{8,11},{9,10},{10,... | collective-permute-start | bytes 98312 | tf_op jit(solution)/shard_map/ppermute | solution.py:226
  21.5 1.3 %collective-permute-start.3 = (f32[64,256]{1,0:T(8,128)S(1)}, f32[64,256]{1,0:T(8,128)S(1)}, u32[]{:S(2)}, u32[]{:S(2)}) collective-permute-start(f32[64,256]{1,0:T(8,128)S(1)} %shard_map.78.mine_ref), channel_id=1, source_target_pairs={{0,4},{4,0},{1,5},{5,1},{2,6},{6,2},{3,7},{7,3},{8,12},{12,8},{9,1... | collective-permute-start | bytes 196616 | tf_op jit(solution)/shard_map/ppermute | solution.py:38
  22.8 18.8 %copy-start.4 = (f32[1024,128]{1,0:T(8,128)S(1)}, f32[1024,128]{1,0:T(8,128)}, u32[]{:S(2)}) copy-start(f32[1024,128]{1,0:T(8,128)} %cand_plan_ref.3) | copy-start | bytes 1572868
  40.1 1.6 %collective-permute-start.4 = (f32[16,40,128]{2,1,0:T(8,128)S(1)}, f32[16,40,128]{2,1,0:T(8,128)S(1)}, u32[]{:S(2)}, u32[]{:S(2)}) collective-permute-start(f32[16,40,128]{2,1,0:T(8,128)S(1)} %all_to_all.25.got_ref), channel_id=1, source_target_pairs={{0,4},{4,0},{1,5},{5,1},{2,6},{6,2},{3,7},{7,3},{8,12},{12,8},{9,1... | collective-permute-start | bytes 983048 | tf_op jit(solution)/shard_map/ppermute | solution.py:38
  42.2 19.0 %copy-start.12 = (f32[128,512]{1,0:T(8,128)}, f32[128,512]{1,0:T(8,128)S(1)}, u32[]{:S(2)}) copy-start(f32[128,512]{1,0:T(8,128)S(1)} %get-tuple-element.34.cand_moment_ref) | copy-start | bytes 786436
  42.2 19.0 %copy-start.14 = (f32[128,512]{1,0:T(8,128)}, f32[128,512]{1,0:T(8,128)S(1)}, u32[]{:S(2)}) copy-start(f32[128,512]{1,0:T(8,128)S(1)} %get-tuple-element.35.ref_moment_ref) | copy-start | bytes 786436
  61.2 9.9 %all-to-all-start.4 = ((f32[32,2,128]{2,1,0:T(2,128)}), f32[32,2,128]{2,1,0:T(2,128)S(1)}, u32[]{:S(2)}, u32[]{:S(2)}) async-start(f32[32,2,128]{2,1,0:T(2,128)} %get-tuple-element.32), calls=%async_computation.4 | async-start | bytes 65536 | tf_op jit(solution)/shard_map/all_to_all | solution.py:367
  63.8 1.0 %copy-start.5 = (f32[1024,128]{1,0:T(8,128)S(1)}, f32[1024,128]{1,0:T(8,128)}, u32[]{:S(2)}) copy-start(f32[1024,128]{1,0:T(8,128)} %cand_plan_ref.3) | copy-start | bytes 1572868
  64.8 0.9 %copy-start.13 = (f32[128,512]{1,0:T(8,128)S(1)}, f32[128,512]{1,0:T(8,128)}, u32[]{:S(2)}) copy-start(f32[128,512]{1,0:T(8,128)} %copy-done.12) | copy-start | bytes 786436
  65.8 0.9 %copy-start.15 = (f32[128,512]{1,0:T(8,128)S(1)}, f32[128,512]{1,0:T(8,128)}, u32[]{:S(2)}) copy-start(f32[128,512]{1,0:T(8,128)} %copy-done.14) | copy-start | bytes 786436
  67.9 0.8 %copy-start.8 = (f32[1024,128]{1,0:T(8,128)}, f32[1024,128]{1,0:T(8,128)S(1)}, u32[]{:S(2)}) copy-start(f32[1024,128]{1,0:T(8,128)S(1)} %get-tuple-element.36.rows_cand_ref) | copy-start | bytes 1572868
  68.7 0.7 copy-start.10
  71.1 1.0 %copy-start.9 = (f32[1024,128]{1,0:T(8,128)S(1)}, f32[1024,128]{1,0:T(8,128)}, u32[]{:S(2)}) copy-start(f32[1024,128]{1,0:T(8,128)} %copy-done.8) | copy-start | bytes 1572868
  72.1 0.9 %copy-start.11 = (f32[512,128]{1,0:T(8,128)S(1)}, f32[512,128]{1,0:T(8,128)}, u32[]{:S(2)}) copy-start(f32[512,128]{1,0:T(8,128)} %copy-done.10) | copy-start | bytes 786436

commit v3 on v2

--- a/solution.py
+++ b/solution.py
@@ -145,6 +145,8 @@
     return (new_cand_plan, new_ref_plan, new_weights)
 
 
+ORDER = 1
+STEPS = 2
 bf16 = jnp.bfloat16
 
 
@@ -166,23 +168,37 @@
 
 def rows_by_rows(left, right):
     n = right.shape[0]
-    lh, ll = split(left)
+    lh, ll = left
     rh, rl = split(right)
     nt = ((1,), (1,))
     wide = mxu(lh, jnp.concatenate([rh, rl], axis=0), nt)
     return wide[:, :n] + (wide[:, n:] + mxu(ll, rh, nt))
 
 
-def call(body, out_shapes, *args, scratch=()):
-    outs = [jax.ShapeDtypeStruct(s, f32) for s in out_shapes]
+FAST = pl.BlockSpec(memory_space=pltpu.VMEM)
+SLOW = pl.BlockSpec(memory_space=pltpu.HBM)
+
+
+def call(body, outs, *args, scratch=(), slow=(), slow_outs=(), short_outs=(), room=4):
+    args = [pltpu.with_memory_space_constraint(a, pltpu.HBM) if i in slow else a for i, a in enumerate(args)]
     return pl.pallas_call(
         body,
-        out_shape=outs,
-        in_specs=[pl.BlockSpec(memory_space=pltpu.VMEM) for _ in args],
-        out_specs=[pl.BlockSpec(memory_space=pltpu.VMEM) for _ in outs],
-        scratch_shapes=[pltpu.VMEM(s, f32) for s in scratch],
-        compiler_params=pltpu.CompilerParams(vmem_limit_bytes=40 << 20),
+        out_shape=[
+            pltpu.HBM(s, f32) if i in slow_outs else jax.ShapeDtypeStruct(s, bf16 if i in short_outs else f32)
+            for i, s in enumerate(outs)
+        ],
+        in_specs=[SLOW if i in slow else FAST for i in range(len(args))],
+        out_specs=[SLOW if i in slow_outs else FAST for i in range(len(outs))],
+        scratch_shapes=[pltpu.VMEM(s, f32) if isinstance(s, tuple) else s for s in scratch],
+        compiler_params=pltpu.CompilerParams(vmem_limit_bytes=room << 20),
     )(*args)
+
+
+def copies(pairs, sems):
+    made = [pltpu.make_async_copy(src, dst, sems.at[i]) for i, (src, dst) in enumerate(pairs)]
+    for c in made:
+        c.start()
+    return made
 
 
 def largest(x):
@@ -211,41 +227,91 @@
     xor = refs & (refs - 1) == 0
     weights_row = weights[None, :]
 
-    def moment_parts(factor_ref, plan_ref, *rest):
-        outs, full = rest[:-1], rest[-1]
+    steps = STEPS
+    step = cand_rows // steps
+    dma = pltpu.SemaphoreType.DMA
+
+    share_rows = ref_rows // cores
+
+    def parts(
+        cand_hbm, cand_plan_hbm, ref_hbm, ref_plan_hbm,
+        out, cand_high, cand_low, share_high, share_low, *rest,
+    ):
+        blocks = rest[:refs]
+        cand, cand_plan, ref_in, ref_plan, whole, ref_whole, sems, ref_sems, out_sems = rest[refs:]
         core, ref = lax.axis_index("core"), lax.axis_index("ref")
-        here = factor_ref[:, pl.ds(pl.multiple_of(core * half, half), half)]
-        full[...] = rows_by_cols(plan_ref[...].T, here) / ref_total
+        loads = copies(
+            [(cand_plan_hbm, cand_plan)]
+            + [(cand_hbm.at[pl.ds(i * step, step)], cand.at[pl.ds(i * step, step)]) for i in range(steps)],
+            sems,
+        )
+        loads[0].wait()
+        plan_high, plan_low = split(cand_plan[...].T)
+        nn = ((1,), (0,))
+        total = None
+        for i in range(steps):
+            loads[1 + i].wait()
+            if i == 0:
+                ref_loads = copies([(ref_plan_hbm, ref_plan), (ref_hbm, ref_in)], ref_sems)
+            rows = slice(i * step, (i + 1) * step)
+            high, low = split(cand[rows, :])
+            cand_high[rows, :], cand_low[rows, :] = high, low
+            part = mxu(plan_high[:, rows], high, nn) + (
+                mxu(plan_high[:, rows], low, nn) + mxu(plan_low[:, rows], high, nn)
+            )
+            total = part if total is None else total + part
+        total = total / cand_total
+        for i in range(chips):
+            for j in range(cores):
+                whole[i * cores + j] = total[i * ca : (i + 1) * ca, j * half : (j + 1) * half]
+        stores = copies([(whole, out)], out_sems)
+        for c in ref_loads:
+            c.wait()
+        here = ref_in[:, pl.ds(pl.multiple_of(core * half, half), half)]
+        ref_whole[...] = rows_by_cols(ref_plan[...].T, here) / ref_total
         for k in range(refs):
             to = ref ^ k if xor else (ref + k) % refs
-            outs[k][...] = full[pl.ds(pl.multiple_of(to * ra, ra), ra), :]
-
-    blocks = call(
-        moment_parts, [(ra, half)] * refs, ref_factor, ref_plan, scratch=[(rank, half)]
-    )
-    arrived = [lax.ppermute(b, "ref", p) for b, p in zip(blocks[1:], pairs)]
-
-    def cand_parts(factor_ref, plan_ref, out):
-        whole = rows_by_cols(plan_ref[...].T, factor_ref[...]) / cand_total
-        for i in range(chips):
-            for j in range(cores):
-                out[i * cores + j] = whole[i * ca : (i + 1) * ca, j * half : (j + 1) * half]
-
-    (parts,) = call(cand_parts, [(chips * cores, ca, half)], cand_factor, cand_plan)
-    pieces = lax.all_to_all(parts, ("chip", "core"), 0, 0)
+            blocks[k][...] = ref_whole[pl.ds(pl.multiple_of(to * ra, ra), ra), :]
+        share = ref_in[pl.ds(pl.multiple_of(core * share_rows, share_rows), share_rows), :]
+        share_high[...], share_low[...] = split(share)
+        for c in stores:
+            c.wait()
+
+    to_plane, cand_high, cand_low, share_high, share_low, *blocks = call(
+        parts,
+        [(chips * cores, ca, half), (cand_rows, width), (cand_rows, width), (share_rows, width), (share_rows, width)]
+        + [(ra, half)] * refs,
+        cand_factor, cand_plan, ref_factor, ref_plan,
+        scratch=[
+            (cand_rows, width), (cand_rows, rank), (ref_rows, width), (ref_rows, rank), (chips * cores, ca, half),
+            (rank, half), dma((steps + 1,)), dma((2,)), dma((1,)),
+        ],
+        slow=(0, 1, 2, 3),
+        slow_outs=(0,),
+        short_outs=(1, 2, 3, 4),
+        room=16,
+    )
+    pieces = lax.all_to_all(to_plane, ("chip", "core"), 0, 0)
+    order = list(range(1, refs))[::ORDER]
+    blocks = [blocks[0]] + [lax.ppermute(blocks[k], "ref", pairs[k - 1]) for k in order]
 
     def own_blocks(pieces_ref, *rest):
         out = rest[-1]
         out[:ca, :] = jnp.sum(pieces_ref[...], axis=0)
-        total = rest[0][...]
-        for other in rest[1:-1]:
-            total = total + other[...]
-        out[ca:, :] = total
-
-    (mine,) = call(own_blocks, [(ca + ra, half)], pieces, blocks[0], *arrived)
+        if len(rest) == 2:
+            out[ca:, :] = jnp.sum(rest[0][...], axis=0)
+        else:
+            total = rest[0][...]
+            for other in rest[1:-1]:
+                total = total + other[...]
+            out[ca:, :] = total
+
+    (mine,) = call(own_blocks, [(ca + ra, half)], pieces, *blocks)
     other = swap_core(mine, cores)
 
-    def column_tops(mine_ref, other_ref, cand_ref, ref_ref, w_ref, out, ref_cols, cand_cols):
+    def column_tops(
+        mine_ref, other_ref, cand_high, cand_low, share_high, share_low, w_ref, out, ref_cols, cand_cols
+    ):
         chip, core, ref = (lax.axis_index(a) for a in ("chip", "core", "ref"))
         here, there = mine_ref[...], other_ref[...]
         low = jnp.where(core == 0, here, there)
@@ -259,10 +325,8 @@
         cand_cols[at_cand, :half] = low[:ca]
         cand_cols[at_cand, half:] = high[:ca]
         w = w_ref[...]
-        grad_cand = rows_by_rows(cand_ref[...], ref_cols[...])
-        share_rows = ref_rows // cores
-        ref_share = ref_ref[pl.ds(pl.multiple_of(core * share_rows, share_rows), share_rows), :]
-        grad_ref = rows_by_rows(ref_share, cand_cols[...])
+        grad_cand = rows_by_rows((cand_high[...], cand_low[...]), ref_cols[...])
+        grad_ref = rows_by_rows((share_high[...], share_low[...]), cand_cols[...])
         tall = jnp.maximum(
             jnp.max(jnp.abs(grad_cand), axis=0, keepdims=True), jnp.max(jnp.abs(grad_ref), axis=0, keepdims=True)
         )
@@ -282,10 +346,13 @@
         [(chips * refs, tall_piece, 128)],
         mine,
         other,
-        cand_factor,
-        ref_factor,
+        cand_high,
+        cand_low,
+        share_high,
+        share_low,
         weights_row,
         scratch=[(rank, width), (rank, width)],
+        room=12,
     )
     got = lax.all_to_all(to_all, ("chip", "ref"), 0, 0)
     got_other = swap_core(got, cores)
@@ -299,8 +366,8 @@
         out[...] = jnp.broadcast_to(both[None], (everyone, 2, rank))
 
     def first_kernels(
-        got_ref, got_other_ref, cand_ref, cand_plan_ref, ref_ref, ref_plan_ref, w_ref,
-        cand_moment, ref_moment, state, sub_cand, sub_ref, out,
+        got_ref, got_other_ref, cand_high, cand_low, cand_plan_ref, share_high, share_low, ref_plan_ref, w_ref,
+        cand_moment, full_cand, state, sub_cand, sub_ref, out, ref_moment,
     ):
         chip, core, ref = (lax.axis_index(a) for a in ("chip", "core", "ref"))
         tops = None
@@ -330,21 +397,24 @@
         state[0:1, :] = kernel_weights
         state[1:2, :] = jnp.broadcast_to(top, (1, rank))
         state[2:8, :] = jnp.ones((6, rank), f32)
-        at = pl.ds(pl.multiple_of(ref * cand_sub, cand_sub), cand_sub)
-        grad = rows_by_rows(cand_ref[at, :], ref_moment[...]) / w
-        kernel_cand = cand_plan_ref[at, :] * jnp.exp(-step_size * grad / top)
-        at = pl.ds(pl.multiple_of((chip * cores + core) * ref_sub, ref_sub), ref_sub)
-        grad = rows_by_rows(ref_ref[at, :], cand_moment[...]) / w
+        grad = rows_by_rows((cand_high[...], cand_low[...]), ref_moment[...]) / w
+        full_cand[...] = cand_plan_ref[...] * jnp.exp(-step_size * grad / top)
+        kernel_cand = full_cand[pl.ds(pl.multiple_of(ref * cand_sub, cand_sub), cand_sub), :]
+        at = pl.ds(pl.multiple_of(chip * ref_sub, ref_sub), ref_sub)
+        grad = rows_by_rows((share_high[at, :], share_low[at, :]), cand_moment[...]) / w
+        at = pl.ds(pl.multiple_of(core * share_rows + chip * ref_sub, ref_sub), ref_sub)
         kernel_ref = ref_plan_ref[at, :] * jnp.exp(-step_size * grad / top)
         sub_cand[...] = kernel_cand
         sub_ref[...] = kernel_ref
         ones = jnp.ones((1, rank), f32)
         mass_part(kernel_cand, kernel_ref, ones, ones, out)
 
-    cand_moment, ref_moment, state, sub_cand, sub_ref, out = call(
+    cand_moment, full_cand, state, sub_cand, sub_ref, out = call(
         first_kernels,
-        [(rank, width), (rank, width), (8, rank), (cand_sub, rank), (ref_sub, rank), (everyone, 2, rank)],
-        got, got_other, cand_factor, cand_plan, ref_factor, ref_plan, weights_row,
+        [(rank, width), (cand_rows, rank), (8, rank), (cand_sub, rank), (ref_sub, rank), (everyone, 2, rank)],
+        got, got_other, cand_high, cand_low, cand_plan, share_high, share_low, ref_plan, weights_row,
+        scratch=[(rank, width)],
+        room=12,
     )
 
     def update(mass_ref, state):
@@ -366,32 +436,36 @@
         state, out = call(next_masses, [(8, rank), (everyone, 2, rank)], mass, state, sub_cand, sub_ref)
     mass = lax.all_to_all(out, ("chip", "core", "ref"), 0, 0)
 
-    def scaled_rows(
-        cand_moment_ref, ref_moment_ref, state_ref, cand_ref, cand_plan_ref, ref_ref, ref_plan_ref, w_ref,
-        cand_out, ref_out,
+    def finish(
+        mass_ref, cand_moment, state_ref, full_cand, ref_ref, ref_plan_ref, w_ref,
+        cand_out, ref_out, w_out, cand_done, ref_done, w_done, sems,
     ):
-        w = w_ref[...]
+        new_weights, scale_cand, scale_ref = update(mass_ref, state_ref)
         top = state_ref[1:2, :]
-        grad = rows_by_rows(cand_ref[...], ref_moment_ref[...]) / w
-        kernel_cand = cand_plan_ref[...] * jnp.exp(-step_size * grad / top)
-        cand_out[...] = kernel_cand * (rank / jnp.sum(kernel_cand * state_ref[2:3, :], axis=1, keepdims=True))
-        grad = rows_by_rows(ref_ref[...], cand_moment_ref[...]) / w
-        kernel_ref = ref_plan_ref[...] * jnp.exp(-step_size * grad / top)
-        ref_out[...] = kernel_ref * (rank / jnp.sum(kernel_ref * state_ref[3:4, :], axis=1, keepdims=True))
-
-    rows_cand, rows_ref = call(
-        scaled_rows, [(cand_rows, rank), (ref_rows, rank)],
-        cand_moment, ref_moment, state, cand_factor, cand_plan, ref_factor, ref_plan, weights_row,
-    )
-
-    def finish(mass_ref, state_ref, rows_cand_ref, rows_ref_ref, cand_out, ref_out, w_out):
-        new_weights, scale_cand, scale_ref = update(mass_ref, state_ref)
-        cand_out[...] = rows_cand_ref[...] * scale_cand
-        ref_out[...] = rows_ref_ref[...] * scale_ref
-        w_out[...] = new_weights
+        kernel = full_cand[...]
+        row = rank / jnp.sum(kernel * state_ref[2:3, :], axis=1, keepdims=True)
+        cand_done[...] = row * kernel * scale_cand
+        stores = [pltpu.make_async_copy(cand_done, cand_out, sems.at[0])]
+        stores[0].start()
+        w_done[...] = new_weights
+        stores += [pltpu.make_async_copy(w_done, w_out, sems.at[1])]
+        stores[1].start()
+        grad = rows_by_rows(split(ref_ref[...]), cand_moment[...]) / w_ref[...]
+        kernel = ref_plan_ref[...] * jnp.exp(-step_size * grad / top)
+        row = rank / jnp.sum(kernel * state_ref[3:4, :], axis=1, keepdims=True)
+        ref_done[...] = row * kernel * scale_ref
+        stores += [pltpu.make_async_copy(ref_done, ref_out, sems.at[2])]
+        stores[2].start()
+        for c in stores:
+            c.wait()
 
     new_cand_plan, new_ref_plan, new_weights = call(
-        finish, [(cand_rows, rank), (ref_rows, rank), (1, rank)], mass, state, rows_cand, rows_ref
+        finish,
+        [(cand_rows, rank), (ref_rows, rank), (1, rank)],
+        mass, cand_moment, state, full_cand, ref_factor, ref_plan, weights_row,
+        scratch=[(cand_rows, rank), (ref_rows, rank), (1, rank), dma((3,))],
+        slow_outs=(0, 1, 2),
+        room=8,
     )
     return new_cand_plan, new_ref_plan, new_weights.reshape(rank)
 

time: 74.7 us -> 69.5 us (0.930)
  local copies, waits for them, and re-layouts: 9.77 us -> 0.02 us
  blocking collectives: 34.3 us -> 43.4 us
  starting transfers between devices: 12.4 us -> 9.67 us
  waiting for transfers between devices: 10.3 us -> 8.36 us
    unnamed x34 -> x8, local copies, waits for them, and re-layouts: 9.77 us -> 0.02 us
    all_to_all x2 -> x3, blocking collectives: 18 us -> 27 us  [on_device_tiled(): mass = lax.all_to_all(out, ('chip', 'core', 'ref'), 0, 0)]
    all_to_all x2 -> x1, starting transfers between devices: 7.77 us -> 5.21 us  [on_device_tiled(): pieces = lax.all_to_all(to_plane, ('chip', 'core'), 0, 0)]
    all_to_all x2 -> x1, waiting for transfers between devices: 1.74 us -> 0.01 us  [on_device_tiled(): pieces = lax.all_to_all(to_plane, ('chip', 'core'), 0, 0)]
    pallas_call x9 -> x7, Pallas kernels: 6.49 us -> 7.04 us  [call(): pl.pallas_call(body, out_shape=[pltpu.HBM(s, f32) if i in slow_outs else...]
  transfers between devices with their start and end apart: 7 -> 6, of which waited for: 5 -> 4; matrix products, arithmetic and copies ran while one was open for 0% -> 0% of each run, Pallas kernels for 2% -> 0%
where the time goes in v3:
time: 69.5 us; the launch traced here: 69.2 us
  blocking collectives  43.4 us (62%)
  starting transfers between devices  9.67 us (14%)
  waiting for transfers between devices  8.36 us (12%)
  Pallas kernels  7.04 us (10%)
  between operations  0.7 us (1%)
    all_to_all x3, blocking collectives, on_device_tiled(): mass = lax.all_to_all(out, ('chip', 'core', 'ref'), 0, 0)  27 us
    all_to_all x1, blocking collectives, on_device_tiled(): got = lax.all_to_all(to_all, ('chip', 'ref'), 0, 0)  16.4 us
    pallas_call x7, Pallas kernels, call(): pl.pallas_call(body, out_shape=[pltpu.HBM(s, f32) if i in slow_outs else...  7.04 us
    ppermute x3, waiting for transfers between devices, on_device_tiled(): lax.ppermute(blocks[k], 'ref', pairs[k - 1])  5.49 us
    all_to_all x1, starting transfers between devices, on_device_tiled(): pieces = lax.all_to_all(to_plane, ('chip', 'core'), 0, 0)  5.21 us
    ppermute x3, starting transfers between devices, on_device_tiled(): lax.ppermute(blocks[k], 'ref', pairs[k - 1])  4.39 us
    ppermute x2, waiting for transfers between devices, swap_core(): return lax.ppermute(array, 'core', [(0, 1), (1, 0)])  2.87 us
  transfers between devices with their start and end apart: 6, of which 4 were waited for; matrix products, arithmetic and copies ran while one was open for 0% of the time, Pallas kernels for 0%

profile of v3, /device:TPU:0, one launch (start us, length us, event | category | flops | bytes accessed | tf_op | source)
XLA Modules:
  0.0 69.2 jit_solution(16292866696935123975)
XLA Ops:
  0.6 0.0 copy-start.3
  0.6 3.3 %shard_map.76 = (f32[8,32,256]{2,1,0:T(8,128)}, bf16[1024,512]{1,0:T(8,128)(2,1)S(1)}, bf16[1024,512]{1,0:T(8,128)(2,1)S(1)}, bf16[256,512]{1,0:T(8,128)(2,1)S(1...) custom-call(f32[1024,512]{1,0:T(8,128)} %cand_hbm.1, ...), custom_call_target="tpu_custom_call" | custom-call | tf_op jit(solution)/shard_map/pallas_call | solution.py:184
  4.0 5.2 %all-to-all-start = ((f32[8,32,256]{2,1,0:T(8,128)}), f32[8,32,256]{2,1,0:T(8,128)S(1)}, u32[]{:S(2)}, u32[]{:S(2)}) async-start(f32[8,32,256]{2,1,0:T(8,128)} %get-tuple-element.25), calls=%async_computation | async-start | bytes 524288 | tf_op jit(solution)/shard_map/all_to_all | solution.py:294
  9.2 1.6 %collective-permute-start = (f32[32,256]{1,0:T(8,128)S(1)}, f32[32,256]{1,0:T(8,128)S(1)}, u32[]{:S(2)}, u32[]{:S(2)}) collective-permute-start(f32[32,256]{1,0:T(8,128)S(1)} %get-tuple-element.27), channel_id=1, source_target_pairs={{0,1},{1,0},{2,3},{3,2},{4,5},{5,4},{6,7},{7,6},{8,9},{9,8},{10,11... | collective-permute-start | bytes 98312 | tf_op jit(solution)/shard_map/ppermute | solution.py:296
  10.8 2.6 %collective-permute-start.1 = (f32[32,256]{1,0:T(8,128)S(1)}, f32[32,256]{1,0:T(8,128)S(1)}, u32[]{:S(2)}, u32[]{:S(2)}) collective-permute-start(f32[32,256]{1,0:T(8,128)S(1)} %get-tuple-element.28), channel_id=1, source_target_pairs={{0,2},{1,3},{2,0},{3,1},{4,6},{5,7},{6,4},{7,5},{8,10},{9,11},{10,... | collective-permute-start | bytes 98312 | tf_op jit(solution)/shard_map/ppermute | solution.py:296
  13.4 0.2 collective-permute-start.2
  13.6 0.0 collective-permute-done.rest_1_
  13.6 2.5 %collective-permute-done.1.rest_2_ = f32[32,256]{1,0:T(8,128)S(1)} collective-permute-done((f32[32,256]{1,0:T(8,128)S(1)}, f32[32,256]{1,0:T(8,128)S(1)}, u32[]{:S(2)}, u32[]{:S(2)}) %collective-permute-start.1) | collective-permute-done | bytes 32800 | tf_op jit(solution)/shard_map/ppermute | solution.py:296
  16.1 3.0 %collective-permute-done.2.rest_3_ = f32[32,256]{1,0:T(8,128)S(1)} collective-permute-done((f32[32,256]{1,0:T(8,128)S(1)}, f32[32,256]{1,0:T(8,128)S(1)}, u32[]{:S(2)}, u32[]{:S(2)}) %collective-permute-start.2) | collective-permute-done | bytes 32800 | tf_op jit(solution)/shard_map/ppermute | solution.py:296
  19.1 0.0 all-to-all-done.pieces_ref
  19.1 0.0 copy-start.1
  19.1 0.0 copy-start.2
  19.1 0.1 collective-permute-start.3
  19.2 1.2 %collective-permute-done.3.other_ref = f32[64,256]{1,0:T(8,128)S(1)} collective-permute-done((f32[64,256]{1,0:T(8,128)S(1)}, f32[64,256]{1,0:T(8,128)S(1)}, u32[]{:S(2)}, u32[]{:S(2)}) %collective-permute-start.3) | collective-permute-done | bytes 65568 | tf_op jit(solution)/shard_map/ppermute | solution.py:38
  20.4 0.0 copy-done.3
  20.4 0.9 %shard_map.78 = f32[16,40,128]{2,1,0:T(8,128)S(1)} custom-call(f32[64,256]{1,0:T(8,128)S(1)} %shard_map.77.mine_ref, f32[64,256]{1,0:T(8,128)S(1)} %collective-permute-done.3.other_ref, bf16[1024,512]{1,0:T(8,128)(2,1)S(1)} %get-tuple-element.30.cand_high, bf16[1024,512]{1,0:T(8,128)(2,1)S(1)} %get-tuple-element.31.cand_low, ...), custom_call_target="tpu_custom_call" | custom-call | tf_op jit(solution)/shard_map/pallas_call | solution.py:184
  21.4 16.4 %all_to_all.25.got_ref = f32[16,40,128]{2,1,0:T(8,128)S(1)} all-to-all(f32[16,40,128]{2,1,0:T(8,128)S(1)} %shard_map.78), channel_id=1, replica_groups=mesh['chip'=4,'core'=2,'ref'=4] {'chip','ref'}, dimensions={0} | all-to-all | bytes 655360 | tf_op jit(solution)/shard_map/all_to_all | solution.py:357
  37.8 0.0 copy-start
  37.8 0.0 collective-permute-start.4
  37.8 1.6 %collective-permute-done.4.got_other_ref = f32[16,40,128]{2,1,0:T(8,128)S(1)} collective-permute-done((f32[16,40,128]{2,1,0:T(8,128)S(1)}, f32[16,40,128]{2,1,0:T(8,128)S(1)}, u32[]{:S(2)}, u32[]{:S(2)}) %collective-permute-start.4) | collective-permute-done | bytes 327712 | tf_op jit(solution)/shard_map/ppermute | solution.py:38
  39.4 0.0 copy-done.1
  39.4 0.0 copy-done.2
  39.4 1.0 %shard_map.79 = (f32[128,512]{1,0:T(8,128)S(1)}, f32[1024,128]{1,0:T(8,128)S(1)}, f32[8,128]{1,0:T(8,128)S(1)}, f32[256,128]{1,0:T(8,128)S(1)}, f32[64,128]{1,0:T(8,128)S(1)}, /*index=5*/f32[32,2,128]{2,1,0:T(2,128)S(1)}) custom-call(f32[16,40,128]{2,1,0:T(8,128)S(1)} %all_to_all.25.got_ref, f32[16,40,128]{2,1,0:T(8,128)S(1)} %collective-permute-done.4.got_other_ref, ...), custom_call_target="tpu_custom_call" | custom-call | tf_op jit(solution)/shard_map/pallas_call | solution.py:184
  40.4 9.0 %all_to_all.26.mass_ref = f32[32,2,128]{2,1,0:T(2,128)S(1)} all-to-all(f32[32,2,128]{2,1,0:T(2,128)S(1)} %get-tuple-element.34), channel_id=1, replica_groups=mesh['chip'=4,'core'=2,'ref'=4] {'chip','core','ref'}, dimensions={0} | all-to-all | bytes 65536 | tf_op jit(solution)/shard_map/all_to_all | solution.py:435
  49.4 0.2 shard_map.80
  49.6 9.0 %all_to_all.27.mass_ref = f32[32,2,128]{2,1,0:T(2,128)S(1)} all-to-all(f32[32,2,128]{2,1,0:T(2,128)S(1)} %get-tuple-element.38), channel_id=1, replica_groups=mesh['chip'=4,'core'=2,'ref'=4] {'chip','core','ref'}, dimensions={0} | all-to-all | bytes 65536 | tf_op jit(solution)/shard_map/all_to_all | solution.py:435
  58.6 0.2 shard_map.81
  58.8 9.0 %all_to_all.28.mass_ref = f32[32,2,128]{2,1,0:T(2,128)S(1)} all-to-all(f32[32,2,128]{2,1,0:T(2,128)S(1)} %get-tuple-element.40), channel_id=1, replica_groups=mesh['chip'=4,'core'=2,'ref'=4] {'chip','core','ref'}, dimensions={0} | all-to-all | bytes 65536 | tf_op jit(solution)/shard_map/all_to_all | solution.py:437
  67.8 0.0 copy-done
  67.8 1.4 %shard_map.82 = (f32[1024,128]{1,0:T(8,128)}, f32[512,128]{1,0:T(8,128)}, f32[1,128]{1,0:T(1,128)}) custom-call(f32[32,2,128]{2,1,0:T(2,128)S(1)} %all_to_all.28.mass_ref, f32[128,512]{1,0:T(8,128)S(1)} %get-tuple-element.41.cand_moment, f32[8,128]{1,0:T(8,128)S(1)} %get-tuple-element.42.state_ref, f32[1024,128]{1,0:T(8,128)S(1)} %get-tuple-element.43.full_cand, ...), custom_call_target="tpu_custom_call" | custom-call | tf_op jit(solution)/shard_map/pallas_call | solution.py:184
  (1 shorter events, 0.0 us)
Async XLA Ops:
  0.6 19.8 %copy-start.3 = (f32[128]{0:T(128)S(1)}, f32[128]{0:T(128)}, u32[]{:S(2)}) copy-start(f32[128]{0:T(128)} %param.9) | copy-start | bytes 1540
  4.0 15.1 %all-to-all-start = ((f32[8,32,256]{2,1,0:T(8,128)}), f32[8,32,256]{2,1,0:T(8,128)S(1)}, u32[]{:S(2)}, u32[]{:S(2)}) async-start(f32[8,32,256]{2,1,0:T(8,128)} %get-tuple-element.25), calls=%async_computation | async-start | bytes 524288 | tf_op jit(solution)/shard_map/all_to_all | solution.py:294
  9.2 4.4 %collective-permute-start = (f32[32,256]{1,0:T(8,128)S(1)}, f32[32,256]{1,0:T(8,128)S(1)}, u32[]{:S(2)}, u32[]{:S(2)}) collective-permute-start(f32[32,256]{1,0:T(8,128)S(1)} %get-tuple-element.27), channel_id=1, source_target_pairs={{0,1},{1,0},{2,3},{3,2},{4,5},{5,4},{6,7},{7,6},{8,9},{9,8},{10,11... | collective-permute-start | bytes 98312 | tf_op jit(solution)/shard_map/ppermute | solution.py:296
  10.8 5.3 %collective-permute-start.1 = (f32[32,256]{1,0:T(8,128)S(1)}, f32[32,256]{1,0:T(8,128)S(1)}, u32[]{:S(2)}, u32[]{:S(2)}) collective-permute-start(f32[32,256]{1,0:T(8,128)S(1)} %get-tuple-element.28), channel_id=1, source_target_pairs={{0,2},{1,3},{2,0},{3,1},{4,6},{5,7},{6,4},{7,5},{8,10},{9,11},{10,... | collective-permute-start | bytes 98312 | tf_op jit(solution)/shard_map/ppermute | solution.py:296
  13.4 5.7 %collective-permute-start.2 = (f32[32,256]{1,0:T(8,128)S(1)}, f32[32,256]{1,0:T(8,128)S(1)}, u32[]{:S(2)}, u32[]{:S(2)}) collective-permute-start(f32[32,256]{1,0:T(8,128)S(1)} %get-tuple-element.29), channel_id=1, source_target_pairs={{0,3},{1,2},{2,1},{3,0},{4,7},{5,6},{6,5},{7,4},{8,11},{9,10},{10,... | collective-permute-start | bytes 98312 | tf_op jit(solution)/shard_map/ppermute | solution.py:296
  19.1 20.3 %copy-start.1 = (f32[512,128]{1,0:T(8,128)S(1)}, f32[512,128]{1,0:T(8,128)}, u32[]{:S(2)}) copy-start(f32[512,128]{1,0:T(8,128)} %ref_plan_ref.3) | copy-start | bytes 786436
  19.1 20.3 %copy-start.2 = (f32[1024,128]{1,0:T(8,128)S(1)}, f32[1024,128]{1,0:T(8,128)}, u32[]{:S(2)}) copy-start(f32[1024,128]{1,0:T(8,128)} %cand_plan_ref.1) | copy-start | bytes 1572868
  19.1 1.3 %collective-permute-start.3 = (f32[64,256]{1,0:T(8,128)S(1)}, f32[64,256]{1,0:T(8,128)S(1)}, u32[]{:S(2)}, u32[]{:S(2)}) collective-permute-start(f32[64,256]{1,0:T(8,128)S(1)} %shard_map.77.mine_ref), channel_id=1, source_target_pairs={{0,4},{4,0},{1,5},{5,1},{2,6},{6,2},{3,7},{7,3},{8,12},{12,8},{9,1... | collective-permute-start | bytes 196616 | tf_op jit(solution)/shard_map/ppermute | solution.py:38
  37.8 30.0 %copy-start = (f32[512,512]{1,0:T(8,128)S(1)}, f32[512,512]{1,0:T(8,128)}, u32[]{:S(2)}) copy-start(f32[512,512]{1,0:T(8,128)} %ref_ref.1) | copy-start | bytes 3145732
  37.8 1.6 %collective-permute-start.4 = (f32[16,40,128]{2,1,0:T(8,128)S(1)}, f32[16,40,128]{2,1,0:T(8,128)S(1)}, u32[]{:S(2)}, u32[]{:S(2)}) collective-permute-start(f32[16,40,128]{2,1,0:T(8,128)S(1)} %all_to_all.25.got_ref), channel_id=1, source_target_pairs={{0,4},{4,0},{1,5},{5,1},{2,6},{6,2},{3,7},{7,3},{8,12},{12,8},{9,1... | collective-permute-start | bytes 983048 | tf_op jit(solution)/shard_map/ppermute | solution.py:38

commit v4 on v3

--- a/solution.py
+++ b/solution.py
@@ -146,7 +146,7 @@
 
 
 ORDER = 1
-STEPS = 2
+STEPS = 4
 bf16 = jnp.bfloat16
 
 
@@ -162,8 +162,9 @@
 def rows_by_cols(left, right):
     lh, ll = split(left)
     rh, rl = split(right)
-    nn = ((1,), (0,))
-    return mxu(lh, rh, nn) + (mxu(lh, rl, nn) + mxu(ll, rh, nn))
+    m, nn = left.shape[0], ((1,), (0,))
+    tall = mxu(jnp.concatenate([lh, ll], axis=0), rh, nn)
+    return tall[:m] + (tall[m:] + mxu(lh, rl, nn))
 
 
 def rows_by_rows(left, right):
@@ -238,15 +239,16 @@
         out, cand_high, cand_low, share_high, share_low, *rest,
     ):
         blocks = rest[:refs]
-        cand, cand_plan, ref_in, ref_plan, whole, ref_whole, sems, ref_sems, out_sems = rest[refs:]
+        cand, cand_plan, ref_in, ref_plan, whole, ref_whole, sems, ref_sems, out_sem = rest[refs:]
         core, ref = lax.axis_index("core"), lax.axis_index("ref")
         loads = copies(
             [(cand_plan_hbm, cand_plan)]
             + [(cand_hbm.at[pl.ds(i * step, step)], cand.at[pl.ds(i * step, step)]) for i in range(steps)],
             sems,
         )
+        ref_loads = []
         loads[0].wait()
-        plan_high, plan_low = split(cand_plan[...].T)
+        plan = jnp.concatenate(split(cand_plan[...].T), axis=0)
         nn = ((1,), (0,))
         total = None
         for i in range(steps):
@@ -256,26 +258,29 @@
             rows = slice(i * step, (i + 1) * step)
             high, low = split(cand[rows, :])
             cand_high[rows, :], cand_low[rows, :] = high, low
-            part = mxu(plan_high[:, rows], high, nn) + (
-                mxu(plan_high[:, rows], low, nn) + mxu(plan_low[:, rows], high, nn)
-            )
+            tall = mxu(plan[:, rows], high, nn)
+            part = tall[:rank] + (tall[rank:] + mxu(plan[:rank, rows], low, nn))
             total = part if total is None else total + part
         total = total / cand_total
         for i in range(chips):
             for j in range(cores):
                 whole[i * cores + j] = total[i * ca : (i + 1) * ca, j * half : (j + 1) * half]
-        stores = copies([(whole, out)], out_sems)
+        store = pltpu.make_async_copy(whole, out, out_sem)
+        store.start()
+
         for c in ref_loads:
             c.wait()
-        here = ref_in[:, pl.ds(pl.multiple_of(core * half, half), half)]
-        ref_whole[...] = rows_by_cols(ref_plan[...].T, here) / ref_total
-        for k in range(refs):
-            to = ref ^ k if xor else (ref + k) % refs
-            blocks[k][...] = ref_whole[pl.ds(pl.multiple_of(to * ra, ra), ra), :]
-        share = ref_in[pl.ds(pl.multiple_of(core * share_rows, share_rows), share_rows), :]
-        share_high[...], share_low[...] = split(share)
-        for c in stores:
-            c.wait()
+        @pl.when(core < cores)
+        def _():
+            here = ref_in[:, pl.ds(pl.multiple_of(core * half, half), half)]
+            ref_whole[...] = rows_by_cols(ref_plan[...].T, here) / ref_total
+            for k in range(refs):
+                to = ref ^ k if xor else (ref + k) % refs
+                blocks[k][...] = ref_whole[pl.ds(pl.multiple_of(to * ra, ra), ra), :]
+            share = ref_in[pl.ds(pl.multiple_of(core * share_rows, share_rows), share_rows), :]
+            share_high[...], share_low[...] = split(share)
+
+        store.wait()
 
     to_plane, cand_high, cand_low, share_high, share_low, *blocks = call(
         parts,
@@ -284,7 +289,7 @@
         cand_factor, cand_plan, ref_factor, ref_plan,
         scratch=[
             (cand_rows, width), (cand_rows, rank), (ref_rows, width), (ref_rows, rank), (chips * cores, ca, half),
-            (rank, half), dma((steps + 1,)), dma((2,)), dma((1,)),
+            (rank, half), dma((steps + 1,)), dma((2,)), dma(()),
         ],
         slow=(0, 1, 2, 3),
         slow_outs=(0,),
@@ -309,52 +314,68 @@
     (mine,) = call(own_blocks, [(ca + ra, half)], pieces, *blocks)
     other = swap_core(mine, cores)
 
+    def columns_at(moment, at, columns, padded):
+        padded[...] = jnp.zeros_like(padded)
+        padded[pl.ds(pl.multiple_of(at * columns, columns), columns), :] = moment
+        return padded[...]
+
+    def own_lanes(factor, core):
+        return factor[:, pl.ds(pl.multiple_of(core * half, half), half)]
+
+    def half_columns(mine_ref, cand_high, cand_low, share_high, share_low, cand_out, share_out, padded):
+        chip, core, ref = (lax.axis_index(a) for a in ("chip", "core", "ref"))
+        moment = columns_at(mine_ref[ca:, :], ref, ra, padded)
+        cand_out[...] = rows_by_rows((own_lanes(cand_high, core), own_lanes(cand_low, core)), moment)
+        moment = columns_at(mine_ref[:ca, :], chip, ca, padded)
+        share_out[...] = rows_by_rows((own_lanes(share_high, core), own_lanes(share_low, core)), moment)
+
+    cand_cols_part, share_cols_part = call(
+        half_columns,
+        [(cand_rows, rank), (share_rows, rank)],
+        mine, cand_high, cand_low, share_high, share_low,
+        scratch=[(rank, half)],
+        room=12,
+    )
+
     def column_tops(
-        mine_ref, other_ref, cand_high, cand_low, share_high, share_low, w_ref, out, ref_cols, cand_cols
+        mine_ref, other_ref, cand_high, cand_low, share_high, share_low, cand_part, share_part, w_ref, out, padded
     ):
         chip, core, ref = (lax.axis_index(a) for a in ("chip", "core", "ref"))
-        here, there = mine_ref[...], other_ref[...]
-        low = jnp.where(core == 0, here, there)
-        high = jnp.where(core == 0, there, here)
-        ref_cols[...] = jnp.zeros_like(ref_cols)
-        cand_cols[...] = jnp.zeros_like(cand_cols)
-        at_ref = pl.ds(pl.multiple_of(ref * ra, ra), ra)
-        at_cand = pl.ds(pl.multiple_of(chip * ca, ca), ca)
-        ref_cols[at_ref, :half] = low[ca:]
-        ref_cols[at_ref, half:] = high[ca:]
-        cand_cols[at_cand, :half] = low[:ca]
-        cand_cols[at_cand, half:] = high[:ca]
         w = w_ref[...]
-        grad_cand = rows_by_rows((cand_high[...], cand_low[...]), ref_cols[...])
-        grad_ref = rows_by_rows((share_high[...], share_low[...]), cand_cols[...])
+        moment = columns_at(other_ref[ca:, :], ref, ra, padded)
+        factor = (own_lanes(cand_high, 1 - core), own_lanes(cand_low, 1 - core))
+        grad_cand = cand_part[...] + rows_by_rows(factor, moment)
+        moment = columns_at(other_ref[:ca, :], chip, ca, padded)
+        factor = (own_lanes(share_high, 1 - core), own_lanes(share_low, 1 - core))
+        grad_ref = share_part[...] + rows_by_rows(factor, moment)
         tall = jnp.maximum(
             jnp.max(jnp.abs(grad_cand), axis=0, keepdims=True), jnp.max(jnp.abs(grad_ref), axis=0, keepdims=True)
         )
-        top = jnp.broadcast_to(tall / w, (8, rank))
         cand_piece = mine_ref[pl.ds(pl.multiple_of(ref * cb, cb), cb), :]
         ref_piece = mine_ref[pl.ds(pl.multiple_of(ca + chip * rb, rb), rb), :]
+        tiles = [p[:, lane * 128 : (lane + 1) * 128] for p in (cand_piece, ref_piece) for lane in range(lanes)]
+        piece = jnp.concatenate(tiles + [tall / w], axis=0)
         for to in range(chips * refs):
-            for lane in range(lanes):
-                at = slice(lane * 128, (lane + 1) * 128)
-                out[to, lane * cb : (lane + 1) * cb, :] = cand_piece[:, at]
-                out[to, lanes * cb + lane * rb : lanes * cb + (lane + 1) * rb, :] = ref_piece[:, at]
-            out[to, lanes * (cb + rb) :, :] = top
-
-    tall_piece = lanes * (cb + rb) + 8
+            out[to * tall_piece : (to + 1) * tall_piece, :] = piece
+
+    tall_piece = lanes * (cb + rb) + 1
     (to_all,) = call(
         column_tops,
-        [(chips * refs, tall_piece, 128)],
+        [(chips * refs * tall_piece, 128)],
         mine,
         other,
         cand_high,
         cand_low,
         share_high,
         share_low,
+        cand_cols_part,
+        share_cols_part,
         weights_row,
-        scratch=[(rank, width), (rank, width)],
+        scratch=[(rank, half)],
         room=12,
     )
-    got = lax.all_to_all(to_all, ("chip", "ref"), 0, 0)
+    to_all = to_all.reshape(chips * refs, tall_piece, 1, 128)
+    got = lax.all_to_all(to_all, ("chip", "ref"), 0, 0).reshape(-1, 128)
     got_other = swap_core(got, cores)
 
     def mass_part(kernel_cand, kernel_ref, scale_cand, scale_ref, out):
@@ -365,43 +386,70 @@
         both = jnp.concatenate([mass_cand, mass_ref], axis=0)
         out[...] = jnp.broadcast_to(both[None], (everyone, 2, rank))
 
-    def first_kernels(
-        got_ref, got_other_ref, cand_high, cand_low, cand_plan_ref, share_high, share_low, ref_plan_ref, w_ref,
-        cand_moment, full_cand, state, sub_cand, sub_ref, out, ref_moment,
-    ):
-        chip, core, ref = (lax.axis_index(a) for a in ("chip", "core", "ref"))
+    def assemble(pieces_ref, cand_half, ref_half):
         tops = None
         for i in range(chips):
             for k in range(refs):
-                here, there = got_ref[i * refs + k], got_other_ref[i * refs + k]
-                low = jnp.where(core == 0, here, there)
-                high = jnp.where(core == 0, there, here)
-                for part, side in enumerate((low, high)):
-                    for lane in range(lanes):
-                        at = slice(part * half + lane * 128, part * half + (lane + 1) * 128)
-                        row = i * ca + k * cb
-                        cand_moment[row : row + cb, at] = side[lane * cb : (lane + 1) * cb]
-                        row = k * ra + i * rb
-                        start = lanes * cb + lane * rb
-                        ref_moment[row : row + rb, at] = side[start : start + rb]
-                    top = side[lanes * (cb + rb) :]
-                    tops = top if tops is None else jnp.maximum(tops, top)
+                start = (i * refs + k) * tall_piece
+                piece = pieces_ref[start : start + tall_piece, :]
+                for lane in range(lanes):
+                    at = slice(lane * 128, (lane + 1) * 128)
+                    row, start = i * ca + k * cb, lane * cb
+                    cand_half[row : row + cb, at] = piece[start : start + cb]
+                    row, start = k * ra + i * rb, lanes * cb + lane * rb
+                    ref_half[row : row + rb, at] = piece[start : start + rb]
+                top = piece[tall_piece - 1 :]
+                tops = top if tops is None else jnp.maximum(tops, top)
+        product = cand_half[...] * ref_half[...]
+        folded = product[:, :128]
+        for lane in range(1, lanes):
+            folded = folded + product[:, lane * 128 : (lane + 1) * 128]
+        return tops, jnp.sum(folded.T, axis=0, keepdims=True)
+
+    def half_kernels(
+        got_ref, cand_high, cand_low, share_high, share_low, cand_half, cand_out, share_out, rows_out, ref_half
+    ):
+        chip, core = lax.axis_index("chip"), lax.axis_index("core")
+        tops, inner = assemble(got_ref, cand_half, ref_half)
+        rows_out[0:1, :] = tops
+        rows_out[1:2, :] = inner
+        cand_out[...] = rows_by_rows((own_lanes(cand_high, core), own_lanes(cand_low, core)), ref_half[...])
+        at = pl.ds(pl.multiple_of(chip * ref_sub, ref_sub), ref_sub)
+        lane = pl.ds(pl.multiple_of(core * half, half), half)
+        share_out[...] = rows_by_rows((share_high[at, lane], share_low[at, lane]), cand_half[...])
+
+    cand_half, cand_part, share_part, rows_part = call(
+        half_kernels,
+        [(rank, half), (cand_rows, rank), (ref_sub, rank), (8, rank)],
+        got, cand_high, cand_low, share_high, share_low,
+        scratch=[(rank, half)],
+        room=12,
+    )
+
+    def first_kernels(
+        got_ref, cand_high, cand_low, cand_plan_ref, share_high, share_low, ref_plan_ref, w_ref,
+        cand_half, cand_part, share_part, rows_part,
+        cand_moment, full_cand, state, sub_cand, sub_ref, out, other_half, ref_half,
+    ):
+        chip, core, ref = (lax.axis_index(a) for a in ("chip", "core", "ref"))
+        tops, inner = assemble(got_ref, other_half, ref_half)
+        tops = jnp.maximum(tops, rows_part[0:1, :])
+        cand_moment[:, :half] = jnp.where(core == 0, cand_half[...], other_half[...])
+        cand_moment[:, half:] = jnp.where(core == 0, other_half[...], cand_half[...])
         w = w_ref[...]
-        product = cand_moment[...] * ref_moment[...]
-        folded = product[:, :128]
-        for lane in range(1, width // 128):
-            folded = folded + product[:, lane * 128 : (lane + 1) * 128]
-        grad_weights = -jnp.sum(folded.T, axis=0, keepdims=True) / (w * w)
-        top = jnp.maximum(jnp.max(tops[:1], axis=1, keepdims=True), largest(grad_weights)) + tiny_value
+        grad_weights = -(inner + rows_part[1:2, :]) / (w * w)
+        top = jnp.maximum(jnp.max(tops, axis=1, keepdims=True), largest(grad_weights)) + tiny_value
         kernel_weights = w * jnp.exp(-step_size * grad_weights / top)
         state[0:1, :] = kernel_weights
         state[1:2, :] = jnp.broadcast_to(top, (1, rank))
         state[2:8, :] = jnp.ones((6, rank), f32)
-        grad = rows_by_rows((cand_high[...], cand_low[...]), ref_moment[...]) / w
+        factor = (own_lanes(cand_high, 1 - core), own_lanes(cand_low, 1 - core))
+        grad = (cand_part[...] + rows_by_rows(factor, ref_half[...])) / w
         full_cand[...] = cand_plan_ref[...] * jnp.exp(-step_size * grad / top)
         kernel_cand = full_cand[pl.ds(pl.multiple_of(ref * cand_sub, cand_sub), cand_sub), :]
         at = pl.ds(pl.multiple_of(chip * ref_sub, ref_sub), ref_sub)
-        grad = rows_by_rows((share_high[at, :], share_low[at, :]), cand_moment[...]) / w
+        lane = pl.ds(pl.multiple_of((1 - core) * half, half), half)
+        grad = (share_part[...] + rows_by_rows((share_high[at, lane], share_low[at, lane]), other_half[...])) / w
         at = pl.ds(pl.multiple_of(core * share_rows + chip * ref_sub, ref_sub), ref_sub)
         kernel_ref = ref_plan_ref[at, :] * jnp.exp(-step_size * grad / top)
         sub_cand[...] = kernel_cand
@@ -412,8 +460,9 @@
     cand_moment, full_cand, state, sub_cand, sub_ref, out = call(
         first_kernels,
         [(rank, width), (cand_rows, rank), (8, rank), (cand_sub, rank), (ref_sub, rank), (everyone, 2, rank)],
-        got, got_other, cand_high, cand_low, cand_plan, share_high, share_low, ref_plan, weights_row,
-        scratch=[(rank, width)],
+        got_other, cand_high, cand_low, cand_plan, share_high, share_low, ref_plan, weights_row,
+        cand_half, cand_part, share_part, rows_part,
+        scratch=[(rank, half), (rank, half)],
         room=12,
     )
 

time: 69.5 us -> 67.5 us (0.971)
  blocking collectives: 43.4 us -> 42.3 us
  waiting for transfers between devices: 8.36 us -> 7.27 us
    all_to_all x1, blocking collectives: 16.4 us -> 15.3 us  [on_device_tiled(): got = lax.all_to_all(to_all, ('chip', 'ref'), 0, 0).reshape(-1, 128)]
    ppermute x2, waiting for transfers between devices: 2.87 us -> 1.78 us  [swap_core(): return lax.ppermute(array, 'core', [(0, 1), (1, 0)])]
    pallas_call x7 -> x9, Pallas kernels: 7.04 us -> 7.2 us  [call(): pl.pallas_call(body, out_shape=[pltpu.HBM(s, f32) if i in slow_outs else...]
  transfers between devices with their start and end apart: 6 -> 6, of which waited for: 4 -> 4; matrix products, arithmetic and copies ran while one was open for 0% -> 0% of each run, Pallas kernels for 0% -> 1%
where the time goes in v4:
time: 67.5 us; the launch traced here: 67.2 us
  blocking collectives  42.3 us (63%)
  starting transfers between devices  9.67 us (14%)
  waiting for transfers between devices  7.27 us (11%)
  Pallas kernels  7.2 us (11%)
  between operations  0.72 us (1%)
    all_to_all x3, blocking collectives, on_device_tiled(): mass = lax.all_to_all(out, ('chip', 'core', 'ref'), 0, 0)  27 us
    all_to_all x1, blocking collectives, on_device_tiled(): got = lax.all_to_all(to_all, ('chip', 'ref'), 0, 0).reshape(-1, 128)  15.3 us
    pallas_call x9, Pallas kernels, call(): pl.pallas_call(body, out_shape=[pltpu.HBM(s, f32) if i in slow_outs else...  7.2 us
    ppermute x3, waiting for transfers between devices, on_device_tiled(): lax.ppermute(blocks[k], 'ref', pairs[k - 1])  5.49 us
    all_to_all x1, starting transfers between devices, on_device_tiled(): pieces = lax.all_to_all(to_plane, ('chip', 'core'), 0, 0)  5.21 us
    ppermute x3, starting transfers between devices, on_device_tiled(): lax.ppermute(blocks[k], 'ref', pairs[k - 1])  4.39 us
    ppermute x2, waiting for transfers between devices, swap_core(): return lax.ppermute(array, 'core', [(0, 1), (1, 0)])  1.78 us
  transfers between devices with their start and end apart: 6, of which 4 were waited for; matrix products, arithmetic and copies ran while one was open for 0% of the time, Pallas kernels for 1%

profile of v4, /device:TPU:0, one launch (start us, length us, event | category | flops | bytes accessed | tf_op | source)
XLA Modules:
  0.0 67.2 jit_solution(9952937185767011135)
XLA Ops:
  0.6 3.2 %shard_map.76 = (f32[8,32,256]{2,1,0:T(8,128)}, bf16[1024,512]{1,0:T(8,128)(2,1)S(1)}, bf16[1024,512]{1,0:T(8,128)(2,1)S(1)}, bf16[256,512]{1,0:T(8,128)(2,1)S(1...) custom-call(f32[1024,512]{1,0:T(8,128)} %cand_hbm.1, ...), custom_call_target="tpu_custom_call" | custom-call | tf_op jit(solution)/shard_map/pallas_call | solution.py:185
  3.8 0.0 copy-start.3
  3.8 5.2 %all-to-all-start = ((f32[8,32,256]{2,1,0:T(8,128)}), f32[8,32,256]{2,1,0:T(8,128)S(1)}, u32[]{:S(2)}, u32[]{:S(2)}) async-start(f32[8,32,256]{2,1,0:T(8,128)} %get-tuple-element.31), calls=%async_computation | async-start | bytes 524288 | tf_op jit(solution)/shard_map/all_to_all | solution.py:299
  9.0 1.6 %collective-permute-start = (f32[32,256]{1,0:T(8,128)S(1)}, f32[32,256]{1,0:T(8,128)S(1)}, u32[]{:S(2)}, u32[]{:S(2)}) collective-permute-start(f32[32,256]{1,0:T(8,128)S(1)} %get-tuple-element.33), channel_id=1, source_target_pairs={{0,1},{1,0},{2,3},{3,2},{4,5},{5,4},{6,7},{7,6},{8,9},{9,8},{10,11... | collective-permute-start | bytes 98312 | tf_op jit(solution)/shard_map/ppermute | solution.py:301
  10.6 2.6 %collective-permute-start.1 = (f32[32,256]{1,0:T(8,128)S(1)}, f32[32,256]{1,0:T(8,128)S(1)}, u32[]{:S(2)}, u32[]{:S(2)}) collective-permute-start(f32[32,256]{1,0:T(8,128)S(1)} %get-tuple-element.34), channel_id=1, source_target_pairs={{0,2},{1,3},{2,0},{3,1},{4,6},{5,7},{6,4},{7,5},{8,10},{9,11},{10,... | collective-permute-start | bytes 98312 | tf_op jit(solution)/shard_map/ppermute | solution.py:301
  13.2 0.2 collective-permute-start.2
  13.4 0.0 collective-permute-done.rest_1_
  13.4 2.5 %collective-permute-done.1.rest_2_ = f32[32,256]{1,0:T(8,128)S(1)} collective-permute-done((f32[32,256]{1,0:T(8,128)S(1)}, f32[32,256]{1,0:T(8,128)S(1)}, u32[]{:S(2)}, u32[]{:S(2)}) %collective-permute-start.1) | collective-permute-done | bytes 32800 | tf_op jit(solution)/shard_map/ppermute | solution.py:301
  16.0 3.0 %collective-permute-done.2.rest_3_ = f32[32,256]{1,0:T(8,128)S(1)} collective-permute-done((f32[32,256]{1,0:T(8,128)S(1)}, f32[32,256]{1,0:T(8,128)S(1)}, u32[]{:S(2)}, u32[]{:S(2)}) %collective-permute-start.2) | collective-permute-done | bytes 32800 | tf_op jit(solution)/shard_map/ppermute | solution.py:301
  18.9 0.0 all-to-all-done.pieces_ref
  18.9 0.1 collective-permute-start.3
  19.0 0.5 shard_map.78
  19.6 0.7 %collective-permute-done.3.other_ref = f32[64,256]{1,0:T(8,128)S(1)} collective-permute-done((f32[64,256]{1,0:T(8,128)S(1)}, f32[64,256]{1,0:T(8,128)S(1)}, u32[]{:S(2)}, u32[]{:S(2)}) %collective-permute-start.3) | collective-permute-done | bytes 65568 | tf_op jit(solution)/shard_map/ppermute | solution.py:38
  20.3 0.0 copy-done.3
  20.3 0.6 shard_map.79
  20.8 0.0 copy-start.1
  20.8 0.0 copy-start.2
  20.9 15.3 %all_to_all.25 = f32[16,33,1,128]{3,2,1,0:T(1,128)S(1)} all-to-all(f32[16,33,1,128]{3,2,1,0:T(1,128)S(1)} %bitcast.6), channel_id=1, replica_groups=mesh['chip'=4,'core'=2,'ref'=4] {'chip','ref'}, dimensions={0} | all-to-all | bytes 540672 | tf_op jit(solution)/shard_map/all_to_all | solution.py:378
  36.2 0.0 collective-permute-start.4
  36.2 0.5 shard_map.80
  36.6 1.1 %collective-permute-done.4.got_ref = f32[528,128]{1,0:T(8,128)S(1)} collective-permute-done((f32[528,128]{1,0:T(8,128)S(1)}, f32[528,128]{1,0:T(8,128)S(1)}, u32[]{:S(2)}, u32[]{:S(2)}) %collective-permute-start.4) | collective-permute-done | bytes 270368 | tf_op jit(solution)/shard_map/ppermute | solution.py:38
  37.7 0.0 copy-done.1
  37.7 0.0 copy-done.2
  37.7 0.0 copy-start
  37.7 0.7 shard_map.81
  38.4 9.0 %all_to_all.26.mass_ref = f32[32,2,128]{2,1,0:T(2,128)S(1)} all-to-all(f32[32,2,128]{2,1,0:T(2,128)S(1)} %get-tuple-element.46), channel_id=1, replica_groups=mesh['chip'=4,'core'=2,'ref'=4] {'chip','core','ref'}, dimensions={0} | all-to-all | bytes 65536 | tf_op jit(solution)/shard_map/all_to_all | solution.py:484
  47.4 0.2 shard_map.82
  47.6 9.0 %all_to_all.27.mass_ref = f32[32,2,128]{2,1,0:T(2,128)S(1)} all-to-all(f32[32,2,128]{2,1,0:T(2,128)S(1)} %get-tuple-element.50), channel_id=1, replica_groups=mesh['chip'=4,'core'=2,'ref'=4] {'chip','core','ref'}, dimensions={0} | all-to-all | bytes 65536 | tf_op jit(solution)/shard_map/all_to_all | solution.py:484
  56.6 0.2 shard_map.83
  56.8 9.0 %all_to_all.28.mass_ref = f32[32,2,128]{2,1,0:T(2,128)S(1)} all-to-all(f32[32,2,128]{2,1,0:T(2,128)S(1)} %get-tuple-element.52), channel_id=1, replica_groups=mesh['chip'=4,'core'=2,'ref'=4] {'chip','core','ref'}, dimensions={0} | all-to-all | bytes 65536 | tf_op jit(solution)/shard_map/all_to_all | solution.py:486
  65.8 0.0 copy-done
  65.8 1.4 %shard_map.84 = (f32[1024,128]{1,0:T(8,128)}, f32[512,128]{1,0:T(8,128)}, f32[1,128]{1,0:T(1,128)}) custom-call(f32[32,2,128]{2,1,0:T(2,128)S(1)} %all_to_all.28.mass_ref, f32[128,512]{1,0:T(8,128)S(1)} %get-tuple-element.53.cand_moment, f32[8,128]{1,0:T(8,128)S(1)} %get-tuple-element.54.state_ref, f32[1024,128]{1,0:T(8,128)S(1)} %get-tuple-element.55.full_cand, ...), custom_call_target="tpu_custom_call" | custom-call | tf_op jit(solution)/shard_map/pallas_call | solution.py:185
  (1 shorter events, 0.0 us)
Async XLA Ops:
  3.8 16.5 %copy-start.3 = (f32[128]{0:T(128)S(1)}, f32[128]{0:T(128)}, u32[]{:S(2)}) copy-start(f32[128]{0:T(128)} %param.9) | copy-start | bytes 1540
  3.8 15.1 %all-to-all-start = ((f32[8,32,256]{2,1,0:T(8,128)}), f32[8,32,256]{2,1,0:T(8,128)S(1)}, u32[]{:S(2)}, u32[]{:S(2)}) async-start(f32[8,32,256]{2,1,0:T(8,128)} %get-tuple-element.31), calls=%async_computation | async-start | bytes 524288 | tf_op jit(solution)/shard_map/all_to_all | solution.py:299
  9.0 4.4 %collective-permute-start = (f32[32,256]{1,0:T(8,128)S(1)}, f32[32,256]{1,0:T(8,128)S(1)}, u32[]{:S(2)}, u32[]{:S(2)}) collective-permute-start(f32[32,256]{1,0:T(8,128)S(1)} %get-tuple-element.33), channel_id=1, source_target_pairs={{0,1},{1,0},{2,3},{3,2},{4,5},{5,4},{6,7},{7,6},{8,9},{9,8},{10,11... | collective-permute-start | bytes 98312 | tf_op jit(solution)/shard_map/ppermute | solution.py:301
  10.6 5.3 %collective-permute-start.1 = (f32[32,256]{1,0:T(8,128)S(1)}, f32[32,256]{1,0:T(8,128)S(1)}, u32[]{:S(2)}, u32[]{:S(2)}) collective-permute-start(f32[32,256]{1,0:T(8,128)S(1)} %get-tuple-element.34), channel_id=1, source_target_pairs={{0,2},{1,3},{2,0},{3,1},{4,6},{5,7},{6,4},{7,5},{8,10},{9,11},{10,... | collective-permute-start | bytes 98312 | tf_op jit(solution)/shard_map/ppermute | solution.py:301
  13.2 5.7 %collective-permute-start.2 = (f32[32,256]{1,0:T(8,128)S(1)}, f32[32,256]{1,0:T(8,128)S(1)}, u32[]{:S(2)}, u32[]{:S(2)}) collective-permute-start(f32[32,256]{1,0:T(8,128)S(1)} %get-tuple-element.35), channel_id=1, source_target_pairs={{0,3},{1,2},{2,1},{3,0},{4,7},{5,6},{6,5},{7,4},{8,11},{9,10},{10,... | collective-permute-start | bytes 98312 | tf_op jit(solution)/shard_map/ppermute | solution.py:301
  18.9 1.3 %collective-permute-start.3 = (f32[64,256]{1,0:T(8,128)S(1)}, f32[64,256]{1,0:T(8,128)S(1)}, u32[]{:S(2)}, u32[]{:S(2)}) collective-permute-start(f32[64,256]{1,0:T(8,128)S(1)} %shard_map.77.mine_ref), channel_id=1, source_target_pairs={{0,4},{4,0},{1,5},{5,1},{2,6},{6,2},{3,7},{7,3},{8,12},{12,8},{9,1... | collective-permute-start | bytes 196616 | tf_op jit(solution)/shard_map/ppermute | solution.py:38
  20.8 16.9 %copy-start.1 = (f32[512,128]{1,0:T(8,128)S(1)}, f32[512,128]{1,0:T(8,128)}, u32[]{:S(2)}) copy-start(f32[512,128]{1,0:T(8,128)} %ref_plan_ref.3) | copy-start | bytes 786436
  20.8 16.9 %copy-start.2 = (f32[1024,128]{1,0:T(8,128)S(1)}, f32[1024,128]{1,0:T(8,128)}, u32[]{:S(2)}) copy-start(f32[1024,128]{1,0:T(8,128)} %cand_plan_ref.1) | copy-start | bytes 1572868
  36.2 1.5 %collective-permute-start.4 = (f32[528,128]{1,0:T(8,128)S(1)}, f32[528,128]{1,0:T(8,128)S(1)}, u32[]{:S(2)}, u32[]{:S(2)}) collective-permute-start(f32[528,128]{1,0:T(8,128)S(1)} %bitcast.4), channel_id=1, source_target_pairs={{0,4},{4,0},{1,5},{5,1},{2,6},{6,2},{3,7},{7,3},{8,12},{12,8},{9,1... | collective-permute-start | bytes 811016 | tf_op jit(solution)/shard_map/ppermute | solution.py:38
  37.7 28.1 %copy-start = (f32[512,512]{1,0:T(8,128)S(1)}, f32[512,512]{1,0:T(8,128)}, u32[]{:S(2)}) copy-start(f32[512,512]{1,0:T(8,128)} %ref_ref.1) | copy-start | bytes 3145732

commit v5 on v4

--- a/solution.py
+++ b/solution.py
@@ -221,6 +221,10 @@
     ca, ra = rank // chips, rank // refs
     cb, rb = ca // refs, ra // chips
     lanes = half // 128
+    block_rows = lanes * ca
+    few = -(-block_rows // (refs + 1))
+    last = few * (refs - 1)
+    tall_piece = 2 * few + 1
     cand_sub = cand_rows // refs
     ref_sub = ref_rows // (chips * cores)
     everyone = chips * cores * refs
@@ -338,7 +342,7 @@
     )
 
     def column_tops(
-        mine_ref, other_ref, cand_high, cand_low, share_high, share_low, cand_part, share_part, w_ref, out, padded
+        mine_ref, other_ref, cand_high, cand_low, share_high, share_low, cand_part, share_part, w_ref, out, padded, rows
     ):
         chip, core, ref = (lax.axis_index(a) for a in ("chip", "core", "ref"))
         w = w_ref[...]
@@ -351,14 +355,25 @@
         tall = jnp.maximum(
             jnp.max(jnp.abs(grad_cand), axis=0, keepdims=True), jnp.max(jnp.abs(grad_ref), axis=0, keepdims=True)
         )
-        cand_piece = mine_ref[pl.ds(pl.multiple_of(ref * cb, cb), cb), :]
-        ref_piece = mine_ref[pl.ds(pl.multiple_of(ca + chip * rb, rb), rb), :]
-        tiles = [p[:, lane * 128 : (lane + 1) * 128] for p in (cand_piece, ref_piece) for lane in range(lanes)]
-        piece = jnp.concatenate(tiles + [tall / w], axis=0)
-        for to in range(chips * refs):
-            out[to * tall_piece : (to + 1) * tall_piece, :] = piece
-
-    tall_piece = lanes * (cb + rb) + 1
+        for lane in range(lanes):
+            at = slice(lane * 128, (lane + 1) * 128)
+            rows[lane * ca : (lane + 1) * ca, :] = mine_ref[:ca, at]
+            rows[block_rows + lane * ra : block_rows + (lane + 1) * ra, :] = mine_ref[ca:, at]
+        top = tall / w
+        for e in range(chips):
+            for d in range(refs):
+                to = lax.rem(chip + chips - e, chips) * refs + lax.rem(ref + refs - d, refs)
+                if e and d:
+                    part = [rows[few * (d - 1) : few * d, :]]
+                    part += [rows[block_rows + few * (e - 1) : block_rows + few * e, :]]
+                elif e:
+                    part = [rows[last:block_rows, :]]
+                else:
+                    part = [rows[block_rows + last : 2 * block_rows, :]]
+                short = 2 * few - sum(p.shape[0] for p in part)
+                part += [jnp.zeros((short, rank), f32)] if short else []
+                out[pl.ds(to * tall_piece, tall_piece), :] = jnp.concatenate(part + [top], axis=0)
+
     (to_all,) = call(
         column_tops,
         [(chips * refs * tall_piece, 128)],
@@ -371,7 +386,7 @@
         cand_cols_part,
         share_cols_part,
         weights_row,
-        scratch=[(rank, half)],
+        scratch=[(rank, half), (2 * block_rows, 128)],
         room=12,
     )
     to_all = to_all.reshape(chips * refs, tall_piece, 1, 128)
@@ -386,20 +401,33 @@
         both = jnp.concatenate([mass_cand, mass_ref], axis=0)
         out[...] = jnp.broadcast_to(both[None], (everyone, 2, rank))
 
-    def assemble(pieces_ref, cand_half, ref_half):
-        tops = None
-        for i in range(chips):
-            for k in range(refs):
-                start = (i * refs + k) * tall_piece
-                piece = pieces_ref[start : start + tall_piece, :]
-                for lane in range(lanes):
-                    at = slice(lane * 128, (lane + 1) * 128)
-                    row, start = i * ca + k * cb, lane * cb
-                    cand_half[row : row + cb, at] = piece[start : start + cb]
-                    row, start = k * ra + i * rb, lanes * cb + lane * rb
-                    ref_half[row : row + rb, at] = piece[start : start + rb]
-                top = piece[tall_piece - 1 :]
-                tops = top if tops is None else jnp.maximum(tops, top)
+    def assemble(pieces_ref, own_ref, cand_half, ref_half, rows):
+        chip, ref = lax.axis_index("chip"), lax.axis_index("ref")
+
+        def piece(e, d, start, count):
+            at = lax.rem(chip + e, chips) * refs + lax.rem(ref + d, refs)
+            return pieces_ref[pl.ds(at * tall_piece + start, count), :]
+
+        def spread(half_ref, at, columns):
+            at = pl.ds(pl.multiple_of(at * columns, columns), columns)
+            for lane in range(lanes):
+                half_ref[at, lane * 128 : (lane + 1) * 128] = rows[lane * columns : (lane + 1) * columns, :]
+
+        cand_half[pl.ds(pl.multiple_of(chip * ca, ca), ca), :] = own_ref[:ca, :]
+        ref_half[pl.ds(pl.multiple_of(ref * ra, ra), ra), :] = own_ref[ca:, :]
+        for e in range(1, chips):
+            rows[last:, :] = piece(e, 0, 0, block_rows - last)
+            for d in range(1, refs):
+                rows[few * (d - 1) : few * d, :] = piece(e, d, 0, few)
+            spread(cand_half, lax.rem(chip + e, chips), ca)
+        for d in range(1, refs):
+            rows[last:, :] = piece(0, d, 0, block_rows - last)
+            for e in range(1, chips):
+                rows[few * (e - 1) : few * e, :] = piece(e, d, few, few)
+            spread(ref_half, lax.rem(ref + d, refs), ra)
+        tops = pieces_ref[tall_piece - 1 : tall_piece, :]
+        for i in range(1, chips * refs):
+            tops = jnp.maximum(tops, pieces_ref[(i + 1) * tall_piece - 1 : (i + 1) * tall_piece, :])
         product = cand_half[...] * ref_half[...]
         folded = product[:, :128]
         for lane in range(1, lanes):
@@ -407,10 +435,11 @@
         return tops, jnp.sum(folded.T, axis=0, keepdims=True)
 
     def half_kernels(
-        got_ref, cand_high, cand_low, share_high, share_low, cand_half, cand_out, share_out, rows_out, ref_half
+        got_ref, own_ref, cand_high, cand_low, share_high, share_low,
+        cand_half, cand_out, share_out, rows_out, ref_half, rows,
     ):
         chip, core = lax.axis_index("chip"), lax.axis_index("core")
-        tops, inner = assemble(got_ref, cand_half, ref_half)
+        tops, inner = assemble(got_ref, own_ref, cand_half, ref_half, rows)
         rows_out[0:1, :] = tops
         rows_out[1:2, :] = inner
         cand_out[...] = rows_by_rows((own_lanes(cand_high, core), own_lanes(cand_low, core)), ref_half[...])
@@ -421,18 +450,18 @@
     cand_half, cand_part, share_part, rows_part = call(
         half_kernels,
         [(rank, half), (cand_rows, rank), (ref_sub, rank), (8, rank)],
-        got, cand_high, cand_low, share_high, share_low,
-        scratch=[(rank, half)],
+        got, mine, cand_high, cand_low, share_high, share_low,
+        scratch=[(rank, half), (block_rows, 128)],
         room=12,
     )
 
     def first_kernels(
-        got_ref, cand_high, cand_low, cand_plan_ref, share_high, share_low, ref_plan_ref, w_ref,
+        got_ref, own_ref, cand_high, cand_low, cand_plan_ref, share_high, share_low, ref_plan_ref, w_ref,
         cand_half, cand_part, share_part, rows_part,
-        cand_moment, full_cand, state, sub_cand, sub_ref, out, other_half, ref_half,
+        cand_moment, full_cand, state, sub_cand, sub_ref, out, other_half, ref_half, rows,
     ):
         chip, core, ref = (lax.axis_index(a) for a in ("chip", "core", "ref"))
-        tops, inner = assemble(got_ref, other_half, ref_half)
+        tops, inner = assemble(got_ref, own_ref, other_half, ref_half, rows)
         tops = jnp.maximum(tops, rows_part[0:1, :])
         cand_moment[:, :half] = jnp.where(core == 0, cand_half[...], other_half[...])
         cand_moment[:, half:] = jnp.where(core == 0, other_half[...], cand_half[...])
@@ -460,9 +489,9 @@
     cand_moment, full_cand, state, sub_cand, sub_ref, out = call(
         first_kernels,
         [(rank, width), (cand_rows, rank), (8, rank), (cand_sub, rank), (ref_sub, rank), (everyone, 2, rank)],
-        got_other, cand_high, cand_low, cand_plan, share_high, share_low, ref_plan, weights_row,
+        got_other, other, cand_high, cand_low, cand_plan, share_high, share_low, ref_plan, weights_row,
         cand_half, cand_part, share_part, rows_part,
-        scratch=[(rank, half), (rank, half)],
+        scratch=[(rank, half), (rank, half), (block_rows, 128)],
         room=12,
     )
 
@@ -523,7 +552,7 @@
     chips, cores, refs = (lax.axis_size(a) for a in ("chip", "core", "ref"))
     rank, width = args[4].shape[0], args[0].shape[1]
     rows = (args[0].shape[0] // refs, args[1].shape[0] // (chips * cores))
-    tiled = cores == 2 and rank == 128 and rank % (8 * chips * refs) == 0 and width % (128 * cores) == 0
+    tiled = cores == 2 and chips == refs and rank == 128 and rank % (8 * chips * refs) == 0 and width % (128 * cores) == 0
     tiled = tiled and all(n % 8 == 0 for n in rows)
     return (on_device_tiled if tiled else on_device_any)(*args)
 

time: 67.5 us -> 66.5 us (0.985)
  blocking collectives: 42.3 us -> 41.2 us
    all_to_all x1, blocking collectives: 15.3 us -> 14.2 us  [on_device_tiled(): got = lax.all_to_all(to_all, ('chip', 'ref'), 0, 0).reshape(-1, 128)]
  transfers between devices with their start and end apart: 6 -> 6, of which waited for: 4 -> 4; matrix products, arithmetic and copies ran while one was open for 0% -> 0% of each run, Pallas kernels for 1% -> 2%
where the time goes in v5:
time: 66.5 us; the launch traced here: 66.1 us
  blocking collectives  41.2 us (62%)
  starting transfers between devices  9.67 us (15%)
  Pallas kernels  7.36 us (11%)
  waiting for transfers between devices  7.13 us (11%)
  between operations  0.72 us (1%)
    all_to_all x3, blocking collectives, on_device_tiled(): mass = lax.all_to_all(out, ('chip', 'core', 'ref'), 0, 0)  27 us
    all_to_all x1, blocking collectives, on_device_tiled(): got = lax.all_to_all(to_all, ('chip', 'ref'), 0, 0).reshape(-1, 128)  14.2 us
    pallas_call x9, Pallas kernels, call(): pl.pallas_call(body, out_shape=[pltpu.HBM(s, f32) if i in slow_outs else...  7.36 us
    ppermute x3, waiting for transfers between devices, on_device_tiled(): lax.ppermute(blocks[k], 'ref', pairs[k - 1])  5.49 us
    all_to_all x1, starting transfers between devices, on_device_tiled(): pieces = lax.all_to_all(to_plane, ('chip', 'core'), 0, 0)  5.21 us
    ppermute x3, starting transfers between devices, on_device_tiled(): lax.ppermute(blocks[k], 'ref', pairs[k - 1])  4.39 us
    ppermute x2, waiting for transfers between devices, swap_core(): return lax.ppermute(array, 'core', [(0, 1), (1, 0)])  1.64 us
  transfers between devices with their start and end apart: 6, of which 4 were waited for; matrix products, arithmetic and copies ran while one was open for 0% of the time, Pallas kernels for 2%

profile of v5, /device:TPU:0, one launch (start us, length us, event | category | flops | bytes accessed | tf_op | source)
XLA Modules:
  0.0 66.1 jit_solution(8350641351390880148)
XLA Ops:
  0.6 3.2 %shard_map.76 = (f32[8,32,256]{2,1,0:T(8,128)}, bf16[1024,512]{1,0:T(8,128)(2,1)S(1)}, bf16[1024,512]{1,0:T(8,128)(2,1)S(1)}, bf16[256,512]{1,0:T(8,128)(2,1)S(1...) custom-call(f32[1024,512]{1,0:T(8,128)} %cand_hbm.1, ...), custom_call_target="tpu_custom_call" | custom-call | tf_op jit(solution)/shard_map/pallas_call | solution.py:185
  3.8 0.0 copy-start.3
  3.8 5.2 %all-to-all-start = ((f32[8,32,256]{2,1,0:T(8,128)}), f32[8,32,256]{2,1,0:T(8,128)S(1)}, u32[]{:S(2)}, u32[]{:S(2)}) async-start(f32[8,32,256]{2,1,0:T(8,128)} %get-tuple-element.31), calls=%async_computation | async-start | bytes 524288 | tf_op jit(solution)/shard_map/all_to_all | solution.py:303
  9.0 1.6 %collective-permute-start = (f32[32,256]{1,0:T(8,128)S(1)}, f32[32,256]{1,0:T(8,128)S(1)}, u32[]{:S(2)}, u32[]{:S(2)}) collective-permute-start(f32[32,256]{1,0:T(8,128)S(1)} %get-tuple-element.33), channel_id=1, source_target_pairs={{0,1},{1,0},{2,3},{3,2},{4,5},{5,4},{6,7},{7,6},{8,9},{9,8},{10,11... | collective-permute-start | bytes 98312 | tf_op jit(solution)/shard_map/ppermute | solution.py:305
  10.6 2.6 %collective-permute-start.1 = (f32[32,256]{1,0:T(8,128)S(1)}, f32[32,256]{1,0:T(8,128)S(1)}, u32[]{:S(2)}, u32[]{:S(2)}) collective-permute-start(f32[32,256]{1,0:T(8,128)S(1)} %get-tuple-element.34), channel_id=1, source_target_pairs={{0,2},{1,3},{2,0},{3,1},{4,6},{5,7},{6,4},{7,5},{8,10},{9,11},{10,... | collective-permute-start | bytes 98312 | tf_op jit(solution)/shard_map/ppermute | solution.py:305
  13.2 0.2 collective-permute-start.2
  13.4 0.0 collective-permute-done.rest_1_
  13.4 2.5 %collective-permute-done.1.rest_2_ = f32[32,256]{1,0:T(8,128)S(1)} collective-permute-done((f32[32,256]{1,0:T(8,128)S(1)}, f32[32,256]{1,0:T(8,128)S(1)}, u32[]{:S(2)}, u32[]{:S(2)}) %collective-permute-start.1) | collective-permute-done | bytes 32800 | tf_op jit(solution)/shard_map/ppermute | solution.py:305
  16.0 3.0 %collective-permute-done.2.rest_3_ = f32[32,256]{1,0:T(8,128)S(1)} collective-permute-done((f32[32,256]{1,0:T(8,128)S(1)}, f32[32,256]{1,0:T(8,128)S(1)}, u32[]{:S(2)}, u32[]{:S(2)}) %collective-permute-start.2) | collective-permute-done | bytes 32800 | tf_op jit(solution)/shard_map/ppermute | solution.py:305
  18.9 0.0 all-to-all-done.pieces_ref
  18.9 0.1 collective-permute-start.3
  19.0 0.5 shard_map.78
  19.6 0.7 %collective-permute-done.3.other_ref.own_ref = f32[64,256]{1,0:T(8,128)S(1)} collective-permute-done((f32[64,256]{1,0:T(8,128)S(1)}, f32[64,256]{1,0:T(8,128)S(1)}, u32[]{:S(2)}, u32[]{:S(2)}) %collective-permute-start.3) | collective-permute-done | bytes 65568 | tf_op jit(solution)/shard_map/ppermute | solution.py:38
  20.3 0.0 copy-done.3
  20.3 0.6 shard_map.79
  20.8 0.0 copy-start.1
  20.9 0.0 copy-start.2
  20.9 14.2 %all_to_all.25 = f32[16,27,1,128]{3,2,1,0:T(1,128)S(1)} all-to-all(f32[16,27,1,128]{3,2,1,0:T(1,128)S(1)} %bitcast.6), channel_id=1, replica_groups=mesh['chip'=4,'core'=2,'ref'=4] {'chip','ref'}, dimensions={0} | all-to-all | bytes 442368 | tf_op jit(solution)/shard_map/all_to_all | solution.py:393
  35.1 0.0 collective-permute-start.4
  35.1 0.5 shard_map.80
  35.7 0.9 %collective-permute-done.4.got_ref = f32[432,128]{1,0:T(8,128)S(1)} collective-permute-done((f32[432,128]{1,0:T(8,128)S(1)}, f32[432,128]{1,0:T(8,128)S(1)}, u32[]{:S(2)}, u32[]{:S(2)}) %collective-permute-start.4) | collective-permute-done | bytes 221216 | tf_op jit(solution)/shard_map/ppermute | solution.py:38
  36.6 0.0 copy-done.1
  36.6 0.0 copy-done.2
  36.6 0.0 copy-start
  36.6 0.7 %shard_map.81 = (f32[128,512]{1,0:T(8,128)S(1)}, f32[1024,128]{1,0:T(8,128)S(1)}, f32[8,128]{1,0:T(8,128)S(1)}, f32[256,128]{1,0:T(8,128)S(1)}, f32[64,128]{1,0:T(8,128)S(1)}, /*index=5*/f32[32,2,128]{2,1,0:T(2,128)S(1)}) custom-call(f32[432,128]{1,0:T(8,128)S(1)} %collective-permute-done.4.got_ref, f32[64,256]{1,0:T(8,128)S(1)} %collective-permute-done.3.other_ref.own_ref, ...), custom_call_target="tpu_custom_call" | custom-call | tf_op jit(solution)/shard_map/pallas_call | solution.py:185
  37.3 9.0 %all_to_all.26.mass_ref = f32[32,2,128]{2,1,0:T(2,128)S(1)} all-to-all(f32[32,2,128]{2,1,0:T(2,128)S(1)} %get-tuple-element.46), channel_id=1, replica_groups=mesh['chip'=4,'core'=2,'ref'=4] {'chip','core','ref'}, dimensions={0} | all-to-all | bytes 65536 | tf_op jit(solution)/shard_map/all_to_all | solution.py:513
  46.3 0.2 shard_map.82
  46.5 9.0 %all_to_all.27.mass_ref = f32[32,2,128]{2,1,0:T(2,128)S(1)} all-to-all(f32[32,2,128]{2,1,0:T(2,128)S(1)} %get-tuple-element.50), channel_id=1, replica_groups=mesh['chip'=4,'core'=2,'ref'=4] {'chip','core','ref'}, dimensions={0} | all-to-all | bytes 65536 | tf_op jit(solution)/shard_map/all_to_all | solution.py:513
  55.5 0.2 shard_map.83
  55.7 9.0 %all_to_all.28.mass_ref = f32[32,2,128]{2,1,0:T(2,128)S(1)} all-to-all(f32[32,2,128]{2,1,0:T(2,128)S(1)} %get-tuple-element.52), channel_id=1, replica_groups=mesh['chip'=4,'core'=2,'ref'=4] {'chip','core','ref'}, dimensions={0} | all-to-all | bytes 65536 | tf_op jit(solution)/shard_map/all_to_all | solution.py:515
  64.7 0.0 copy-done
  64.7 1.4 %shard_map.84 = (f32[1024,128]{1,0:T(8,128)}, f32[512,128]{1,0:T(8,128)}, f32[1,128]{1,0:T(1,128)}) custom-call(f32[32,2,128]{2,1,0:T(2,128)S(1)} %all_to_all.28.mass_ref, f32[128,512]{1,0:T(8,128)S(1)} %get-tuple-element.53.cand_moment, f32[8,128]{1,0:T(8,128)S(1)} %get-tuple-element.54.state_ref, f32[1024,128]{1,0:T(8,128)S(1)} %get-tuple-element.55.full_cand, ...), custom_call_target="tpu_custom_call" | custom-call | tf_op jit(solution)/shard_map/pallas_call | solution.py:185
  (1 shorter events, 0.0 us)
Async XLA Ops:
  3.8 16.5 %copy-start.3 = (f32[128]{0:T(128)S(1)}, f32[128]{0:T(128)}, u32[]{:S(2)}) copy-start(f32[128]{0:T(128)} %param.9) | copy-start | bytes 1540
  3.8 15.1 %all-to-all-start = ((f32[8,32,256]{2,1,0:T(8,128)}), f32[8,32,256]{2,1,0:T(8,128)S(1)}, u32[]{:S(2)}, u32[]{:S(2)}) async-start(f32[8,32,256]{2,1,0:T(8,128)} %get-tuple-element.31), calls=%async_computation | async-start | bytes 524288 | tf_op jit(solution)/shard_map/all_to_all | solution.py:303
  9.0 4.4 %collective-permute-start = (f32[32,256]{1,0:T(8,128)S(1)}, f32[32,256]{1,0:T(8,128)S(1)}, u32[]{:S(2)}, u32[]{:S(2)}) collective-permute-start(f32[32,256]{1,0:T(8,128)S(1)} %get-tuple-element.33), channel_id=1, source_target_pairs={{0,1},{1,0},{2,3},{3,2},{4,5},{5,4},{6,7},{7,6},{8,9},{9,8},{10,11... | collective-permute-start | bytes 98312 | tf_op jit(solution)/shard_map/ppermute | solution.py:305
  10.6 5.3 %collective-permute-start.1 = (f32[32,256]{1,0:T(8,128)S(1)}, f32[32,256]{1,0:T(8,128)S(1)}, u32[]{:S(2)}, u32[]{:S(2)}) collective-permute-start(f32[32,256]{1,0:T(8,128)S(1)} %get-tuple-element.34), channel_id=1, source_target_pairs={{0,2},{1,3},{2,0},{3,1},{4,6},{5,7},{6,4},{7,5},{8,10},{9,11},{10,... | collective-permute-start | bytes 98312 | tf_op jit(solution)/shard_map/ppermute | solution.py:305
  13.2 5.7 %collective-permute-start.2 = (f32[32,256]{1,0:T(8,128)S(1)}, f32[32,256]{1,0:T(8,128)S(1)}, u32[]{:S(2)}, u32[]{:S(2)}) collective-permute-start(f32[32,256]{1,0:T(8,128)S(1)} %get-tuple-element.35), channel_id=1, source_target_pairs={{0,3},{1,2},{2,1},{3,0},{4,7},{5,6},{6,5},{7,4},{8,11},{9,10},{10,... | collective-permute-start | bytes 98312 | tf_op jit(solution)/shard_map/ppermute | solution.py:305
  18.9 1.3 %collective-permute-start.3 = (f32[64,256]{1,0:T(8,128)S(1)}, f32[64,256]{1,0:T(8,128)S(1)}, u32[]{:S(2)}, u32[]{:S(2)}) collective-permute-start(f32[64,256]{1,0:T(8,128)S(1)} %shard_map.77.mine_ref.own_ref), channel_id=1, source_target_pairs={{0,4},{4,0},{1,5},{5,1},{2,6},{6,2},{3,7},{7,3},{8,12},{12,8},{9,1... | collective-permute-start | bytes 196616 | tf_op jit(solution)/shard_map/ppermute | solution.py:38
  20.8 15.7 %copy-start.1 = (f32[512,128]{1,0:T(8,128)S(1)}, f32[512,128]{1,0:T(8,128)}, u32[]{:S(2)}) copy-start(f32[512,128]{1,0:T(8,128)} %ref_plan_ref.3) | copy-start | bytes 786436
  20.9 15.7 %copy-start.2 = (f32[1024,128]{1,0:T(8,128)S(1)}, f32[1024,128]{1,0:T(8,128)}, u32[]{:S(2)}) copy-start(f32[1024,128]{1,0:T(8,128)} %cand_plan_ref.1) | copy-start | bytes 1572868
  35.1 1.5 %collective-permute-start.4 = (f32[432,128]{1,0:T(8,128)S(1)}, f32[432,128]{1,0:T(8,128)S(1)}, u32[]{:S(2)}, u32[]{:S(2)}) collective-permute-start(f32[432,128]{1,0:T(8,128)S(1)} %bitcast.4), channel_id=1, source_target_pairs={{0,4},{4,0},{1,5},{5,1},{2,6},{6,2},{3,7},{7,3},{8,12},{12,8},{9,1... | collective-permute-start | bytes 663560 | tf_op jit(solution)/shard_map/ppermute | solution.py:38
  36.6 28.1 %copy-start = (f32[512,512]{1,0:T(8,128)S(1)}, f32[512,512]{1,0:T(8,128)}, u32[]{:S(2)}) copy-start(f32[512,512]{1,0:T(8,128)} %ref_ref.1) | copy-start | bytes 3145732

commit v6 on v5

--- a/solution.py
+++ b/solution.py
@@ -145,8 +145,9 @@
     return (new_cand_plan, new_ref_plan, new_weights)
 
 
-ORDER = 1
-STEPS = 4
+load_steps = 4
+ref_order = [2, 3, 1]
+chip_order = [1, 3, 2]
 bf16 = jnp.bfloat16
 
 
@@ -232,33 +233,25 @@
     xor = refs & (refs - 1) == 0
     weights_row = weights[None, :]
 
-    steps = STEPS
+    steps = load_steps
     step = cand_rows // steps
     dma = pltpu.SemaphoreType.DMA
 
     share_rows = ref_rows // cores
 
-    def parts(
-        cand_hbm, cand_plan_hbm, ref_hbm, ref_plan_hbm,
-        out, cand_high, cand_low, share_high, share_low, *rest,
-    ):
-        blocks = rest[:refs]
-        cand, cand_plan, ref_in, ref_plan, whole, ref_whole, sems, ref_sems, out_sem = rest[refs:]
-        core, ref = lax.axis_index("core"), lax.axis_index("ref")
+    def cand_parts(cand_hbm, cand_plan_hbm, keep, send, cand_high, cand_low, cand, cand_plan, sems):
+        core = lax.axis_index("core")
         loads = copies(
             [(cand_plan_hbm, cand_plan)]
             + [(cand_hbm.at[pl.ds(i * step, step)], cand.at[pl.ds(i * step, step)]) for i in range(steps)],
             sems,
         )
-        ref_loads = []
         loads[0].wait()
         plan = jnp.concatenate(split(cand_plan[...].T), axis=0)
         nn = ((1,), (0,))
         total = None
         for i in range(steps):
             loads[1 + i].wait()
-            if i == 0:
-                ref_loads = copies([(ref_plan_hbm, ref_plan), (ref_hbm, ref_in)], ref_sems)
             rows = slice(i * step, (i + 1) * step)
             high, low = split(cand[rows, :])
             cand_high[rows, :], cand_low[rows, :] = high, low
@@ -266,56 +259,64 @@
             part = tall[:rank] + (tall[rank:] + mxu(plan[:rank, rows], low, nn))
             total = part if total is None else total + part
         total = total / cand_total
-        for i in range(chips):
-            for j in range(cores):
-                whole[i * cores + j] = total[i * ca : (i + 1) * ca, j * half : (j + 1) * half]
-        store = pltpu.make_async_copy(whole, out, out_sem)
-        store.start()
-
-        for c in ref_loads:
-            c.wait()
-        @pl.when(core < cores)
-        def _():
-            here = ref_in[:, pl.ds(pl.multiple_of(core * half, half), half)]
-            ref_whole[...] = rows_by_cols(ref_plan[...].T, here) / ref_total
-            for k in range(refs):
-                to = ref ^ k if xor else (ref + k) % refs
-                blocks[k][...] = ref_whole[pl.ds(pl.multiple_of(to * ra, ra), ra), :]
-            share = ref_in[pl.ds(pl.multiple_of(core * share_rows, share_rows), share_rows), :]
-            share_high[...], share_low[...] = split(share)
-
-        store.wait()
-
-    to_plane, cand_high, cand_low, share_high, share_low, *blocks = call(
-        parts,
-        [(chips * cores, ca, half), (cand_rows, width), (cand_rows, width), (share_rows, width), (share_rows, width)]
-        + [(ra, half)] * refs,
-        cand_factor, cand_plan, ref_factor, ref_plan,
-        scratch=[
-            (cand_rows, width), (cand_rows, rank), (ref_rows, width), (ref_rows, rank), (chips * cores, ca, half),
-            (rank, half), dma((steps + 1,)), dma((2,)), dma(()),
-        ],
-        slow=(0, 1, 2, 3),
-        slow_outs=(0,),
-        short_outs=(1, 2, 3, 4),
+        keep[...] = jnp.where(core == 0, total[:, :half], total[:, half:])
+        send[...] = jnp.where(core == 0, total[:, half:], total[:, :half])
+
+    keep, send, cand_high, cand_low = call(
+        cand_parts,
+        [(rank, half)] * 2 + [(cand_rows, width)] * 2,
+        cand_factor, cand_plan,
+        scratch=[(cand_rows, width), (cand_rows, rank), dma((steps + 1,))],
+        slow=(0, 1),
+        short_outs=(2, 3),
         room=16,
     )
-    pieces = lax.all_to_all(to_plane, ("chip", "core"), 0, 0)
-    order = list(range(1, refs))[::ORDER]
+    came = swap_core(send, cores)
+
+    def ref_parts(ref_in, ref_plan_in, share_high, share_low, *rest):
+        blocks, whole = rest[:refs], rest[refs]
+        core, ref = lax.axis_index("core"), lax.axis_index("ref")
+        here = ref_in[:, pl.ds(pl.multiple_of(core * half, half), half)]
+        whole[...] = rows_by_cols(ref_plan_in[...].T, here) / ref_total
+        for k in range(refs):
+            to = ref ^ k if xor else (ref + k) % refs
+            blocks[k][...] = whole[pl.ds(pl.multiple_of(to * ra, ra), ra), :]
+        share = ref_in[pl.ds(pl.multiple_of(core * share_rows, share_rows), share_rows), :]
+        share_high[...], share_low[...] = split(share)
+
+    share_high, share_low, *blocks = call(
+        ref_parts,
+        [(share_rows, width)] * 2 + [(ra, half)] * refs,
+        ref_factor, ref_plan,
+        scratch=[(rank, half)],
+        short_outs=(0, 1),
+        room=8,
+    )
+    order = ref_order if refs == 4 else list(range(1, refs))
     blocks = [blocks[0]] + [lax.ppermute(blocks[k], "ref", pairs[k - 1]) for k in order]
 
-    def own_blocks(pieces_ref, *rest):
+    def chip_blocks(keep_ref, came_ref, *rest):
+        outs, full = rest[:-1], rest[-1]
+        chip = lax.axis_index("chip")
+        full[...] = keep_ref[...] + came_ref[...]
+        for k in range(chips):
+            outs[k][...] = full[pl.ds(pl.multiple_of((chip ^ k) * ca, ca), ca), :]
+
+    cand_blocks = call(chip_blocks, [(ca, half)] * chips, keep, came, scratch=[(rank, half)])
+    chip_pairs = partner_lists(chips)
+    cand_blocks = [cand_blocks[0]] + [
+        lax.ppermute(cand_blocks[k], "chip", chip_pairs[k - 1]) for k in (chip_order if chips == 4 else range(1, chips))
+    ]
+
+    def own_blocks(*rest):
         out = rest[-1]
-        out[:ca, :] = jnp.sum(pieces_ref[...], axis=0)
-        if len(rest) == 2:
-            out[ca:, :] = jnp.sum(rest[0][...], axis=0)
-        else:
-            total = rest[0][...]
-            for other in rest[1:-1]:
-                total = total + other[...]
-            out[ca:, :] = total
-
-    (mine,) = call(own_blocks, [(ca + ra, half)], pieces, *blocks)
+        for start, count, terms in ((0, ca, rest[:chips]), (ca, ra, rest[chips:-1])):
+            total = terms[0][...]
+            for term in terms[1:]:
+                total = total + term[...]
+            out[start : start + count, :] = total
+
+    (mine,) = call(own_blocks, [(ca + ra, half)], *cand_blocks, *blocks)
     other = swap_core(mine, cores)
 
     def columns_at(moment, at, columns, padded):

time: 66.5 us -> 64.9 us (0.976)
  waiting for transfers between devices: 7.13 us -> 5.06 us
  blocking collectives: 41.2 us -> 42.6 us
    all_to_all x1 -> x0, starting transfers between devices: 5.21 us -> none  [on_device_tiled(): pieces = lax.all_to_all(to_plane, ('chip', 'core'), 0, 0)]
    ppermute x3, waiting for transfers between devices: 5.49 us -> 0.59 us  [on_device_tiled(): lax.ppermute(blocks[k], 'ref', pairs[k - 1])]
    ppermute x0 -> x3, starting transfers between devices: none -> 3.55 us  [on_device_tiled(): lax.ppermute(cand_blocks[k], 'chip', chip_pairs[k - 1])]
    ppermute x0 -> x3, waiting for transfers between devices: none -> 2.83 us  [on_device_tiled(): lax.ppermute(cand_blocks[k], 'chip', chip_pairs[k - 1])]
    all_to_all x1, blocking collectives: 14.2 us -> 15.7 us  [on_device_tiled(): got = lax.all_to_all(to_all, ('chip', 'ref'), 0, 0).reshape(-1, 128)]
    ppermute x3, starting transfers between devices: 4.39 us -> 5.24 us  [on_device_tiled(): lax.ppermute(blocks[k], 'ref', pairs[k - 1])]
    pallas_call x9 -> x11, Pallas kernels: 7.36 us -> 6.8 us  [call(): pl.pallas_call(body, out_shape=[pltpu.HBM(s, f32) if i in slow_outs else...]
    ppermute x2 -> x3, waiting for transfers between devices: 1.64 us -> 1.64 us  [swap_core(): return lax.ppermute(array, 'core', [(0, 1), (1, 0)])]
  transfers between devices with their start and end apart: 6 -> 9, of which waited for: 4 -> 5; matrix products, arithmetic and copies ran while one was open for 0% -> 0% of each run, Pallas kernels for 2% -> 2%
where the time goes in v6:
time: 64.9 us; the launch traced here: 64.7 us
  blocking collectives  42.6 us (66%)
  starting transfers between devices  9.43 us (15%)
  Pallas kernels  6.8 us (10%)
  waiting for transfers between devices  5.06 us (8%)
  between operations  0.75 us (1%)
    all_to_all x3, blocking collectives, on_device_tiled(): mass = lax.all_to_all(out, ('chip', 'core', 'ref'), 0, 0)  27 us
    all_to_all x1, blocking collectives, on_device_tiled(): got = lax.all_to_all(to_all, ('chip', 'ref'), 0, 0).reshape(-1, 128)  15.7 us
    pallas_call x11, Pallas kernels, call(): pl.pallas_call(body, out_shape=[pltpu.HBM(s, f32) if i in slow_outs else...  6.8 us
    ppermute x3, starting transfers between devices, on_device_tiled(): lax.ppermute(blocks[k], 'ref', pairs[k - 1])  5.24 us
    ppermute x3, starting transfers between devices, on_device_tiled(): lax.ppermute(cand_blocks[k], 'chip', chip_pairs[k - 1])  3.55 us
    ppermute x3, waiting for transfers between devices, on_device_tiled(): lax.ppermute(cand_blocks[k], 'chip', chip_pairs[k - 1])  2.83 us
    ppermute x3, waiting for transfers between devices, swap_core(): return lax.ppermute(array, 'core', [(0, 1), (1, 0)])  1.64 us
  transfers between devices with their start and end apart: 9, of which 5 were waited for; matrix products, arithmetic and copies ran while one was open for 0% of the time, Pallas kernels for 2%

profile of v6, /device:TPU:0, one launch (start us, length us, event | category | flops | bytes accessed | tf_op | source)
XLA Modules:
  0.0 64.7 jit_solution(17834109408007375113)
XLA Ops:
  0.7 2.2 %shard_map.76 = (f32[128,256]{1,0:T(8,128)S(1)}, f32[128,256]{1,0:T(8,128)S(1)}, bf16[1024,512]{1,0:T(8,128)(2,1)S(1)}, bf16[1024,512]{1,0:T(8,128)(2,1)S(1)}) custom-call(f32[1024,512]{1,0:T(8,128)} %cand_hbm.1, f32[1024,128]{1,0:T(8,128)} %cand_plan_ref.1), custom_call_target="tpu_custom_call" | custom-call | tf_op jit(solution)/shard_map/pallas_call | solution.py:186
  2.9 0.0 copy-start.3
  2.9 0.6 collective-permute-start
  3.5 0.4 shard_map.78
  3.9 3.7 %collective-permute-start.4 = (f32[32,256]{1,0:T(8,128)S(1)}, f32[32,256]{1,0:T(8,128)S(1)}, u32[]{:S(2)}, u32[]{:S(2)}) collective-permute-start(f32[32,256]{1,0:T(8,128)S(1)} %get-tuple-element.43), channel_id=1, source_target_pairs={{0,2},{1,3},{2,0},{3,1},{4,6},{5,7},{6,4},{7,5},{8,10},{9,11},{10,... | collective-permute-start | bytes 98312 | tf_op jit(solution)/shard_map/ppermute | solution.py:296
  7.6 1.4 %collective-permute-start.5 = (f32[32,256]{1,0:T(8,128)S(1)}, f32[32,256]{1,0:T(8,128)S(1)}, u32[]{:S(2)}, u32[]{:S(2)}) collective-permute-start(f32[32,256]{1,0:T(8,128)S(1)} %get-tuple-element.44), channel_id=1, source_target_pairs={{0,3},{1,2},{2,1},{3,0},{4,7},{5,6},{6,5},{7,4},{8,11},{9,10},{10,... | collective-permute-start | bytes 98312 | tf_op jit(solution)/shard_map/ppermute | solution.py:296
  8.9 0.2 collective-permute-start.6
  9.2 1.6 %collective-permute-start.1 = (f32[32,256]{1,0:T(8,128)S(1)}, f32[32,256]{1,0:T(8,128)S(1)}, u32[]{:S(2)}, u32[]{:S(2)}) collective-permute-start(f32[32,256]{1,0:T(8,128)S(1)} %get-tuple-element.39), channel_id=1, source_target_pairs={{0,8},{8,0},{16,24},{24,16},{1,9},{9,1},{17,25},{25,17},{2,10},{10... | collective-permute-start | bytes 98312 | tf_op jit(solution)/shard_map/ppermute | solution.py:308
  10.7 1.5 %collective-permute-start.2 = (f32[32,256]{1,0:T(8,128)S(1)}, f32[32,256]{1,0:T(8,128)S(1)}, u32[]{:S(2)}, u32[]{:S(2)}) collective-permute-start(f32[32,256]{1,0:T(8,128)S(1)} %get-tuple-element.40), channel_id=1, source_target_pairs={{0,24},{8,16},{16,8},{24,0},{1,25},{9,17},{17,9},{25,1},{2,26},{10... | collective-permute-start | bytes 98312 | tf_op jit(solution)/shard_map/ppermute | solution.py:308
  12.2 0.0 collective-permute-done.4.rest_5_
  12.2 0.5 collective-permute-start.3
  12.7 0.5 collective-permute-done.5.rest_6_
  13.3 0.0 collective-permute-done.6.rest_7_
  13.3 0.0 collective-permute-done.1.rest_1_
  13.3 2.2 %collective-permute-done.2.rest_2_ = f32[32,256]{1,0:T(8,128)S(1)} collective-permute-done((f32[32,256]{1,0:T(8,128)S(1)}, f32[32,256]{1,0:T(8,128)S(1)}, u32[]{:S(2)}, u32[]{:S(2)}) %collective-permute-start.2) | collective-permute-done | bytes 32800 | tf_op jit(solution)/shard_map/ppermute | solution.py:308
  15.5 0.6 collective-permute-done.3.rest_3_
  16.2 0.1 collective-permute-start.7
  16.2 0.5 shard_map.80
  16.8 0.7 %collective-permute-done.7.other_ref.own_ref = f32[64,256]{1,0:T(8,128)S(1)} collective-permute-done((f32[64,256]{1,0:T(8,128)S(1)}, f32[64,256]{1,0:T(8,128)S(1)}, u32[]{:S(2)}, u32[]{:S(2)}) %collective-permute-start.7) | collective-permute-done | bytes 65568 | tf_op jit(solution)/shard_map/ppermute | solution.py:38
  17.5 0.6 shard_map.81
  18.1 0.0 copy-start.2
  18.1 15.7 %all_to_all.20 = f32[16,27,1,128]{3,2,1,0:T(1,128)S(1)} all-to-all(f32[16,27,1,128]{3,2,1,0:T(1,128)S(1)} %bitcast.6), channel_id=1, replica_groups=mesh['chip'=4,'core'=2,'ref'=4] {'chip','ref'}, dimensions={0} | all-to-all | bytes 442368 | tf_op jit(solution)/shard_map/all_to_all | solution.py:394
  33.7 0.0 collective-permute-start.8
  33.7 0.5 shard_map.82
  34.3 0.9 %collective-permute-done.8.got_ref = f32[432,128]{1,0:T(8,128)S(1)} collective-permute-done((f32[432,128]{1,0:T(8,128)S(1)}, f32[432,128]{1,0:T(8,128)S(1)}, u32[]{:S(2)}, u32[]{:S(2)}) %collective-permute-start.8) | collective-permute-done | bytes 221216 | tf_op jit(solution)/shard_map/ppermute | solution.py:38
  35.2 0.7 %shard_map.83 = (f32[128,512]{1,0:T(8,128)S(1)}, f32[1024,128]{1,0:T(8,128)S(1)}, f32[8,128]{1,0:T(8,128)S(1)}, f32[256,128]{1,0:T(8,128)S(1)}, f32[64,128]{1,0:T(8,128)S(1)}, /*index=5*/f32[32,2,128]{2,1,0:T(2,128)S(1)}) custom-call(f32[432,128]{1,0:T(8,128)S(1)} %collective-permute-done.8.got_ref, f32[64,256]{1,0:T(8,128)S(1)} %collective-permute-done.7.other_ref.own_ref, ...), custom_call_target="tpu_custom_call" | custom-call | tf_op jit(solution)/shard_map/pallas_call | solution.py:186
  35.9 9.0 %all_to_all.21.mass_ref = f32[32,2,128]{2,1,0:T(2,128)S(1)} all-to-all(f32[32,2,128]{2,1,0:T(2,128)S(1)} %get-tuple-element.56), channel_id=1, replica_groups=mesh['chip'=4,'core'=2,'ref'=4] {'chip','core','ref'}, dimensions={0} | all-to-all | bytes 65536 | tf_op jit(solution)/shard_map/all_to_all | solution.py:514
  44.9 0.2 shard_map.84
  45.1 9.0 %all_to_all.22.mass_ref = f32[32,2,128]{2,1,0:T(2,128)S(1)} all-to-all(f32[32,2,128]{2,1,0:T(2,128)S(1)} %get-tuple-element.60), channel_id=1, replica_groups=mesh['chip'=4,'core'=2,'ref'=4] {'chip','core','ref'}, dimensions={0} | all-to-all | bytes 65536 | tf_op jit(solution)/shard_map/all_to_all | solution.py:514
  54.1 0.2 shard_map.85
  54.3 9.0 %all_to_all.23.mass_ref = f32[32,2,128]{2,1,0:T(2,128)S(1)} all-to-all(f32[32,2,128]{2,1,0:T(2,128)S(1)} %get-tuple-element.62), channel_id=1, replica_groups=mesh['chip'=4,'core'=2,'ref'=4] {'chip','core','ref'}, dimensions={0} | all-to-all | bytes 65536 | tf_op jit(solution)/shard_map/all_to_all | solution.py:516
  63.3 1.4 %shard_map.86 = (f32[1024,128]{1,0:T(8,128)}, f32[512,128]{1,0:T(8,128)}, f32[1,128]{1,0:T(1,128)}) custom-call(f32[32,2,128]{2,1,0:T(2,128)S(1)} %all_to_all.23.mass_ref, f32[128,512]{1,0:T(8,128)S(1)} %get-tuple-element.63.cand_moment, f32[8,128]{1,0:T(8,128)S(1)} %get-tuple-element.64.state_ref, f32[1024,128]{1,0:T(8,128)S(1)} %get-tuple-element.65.full_cand, ...), custom_call_target="tpu_custom_call" | custom-call | tf_op jit(solution)/shard_map/pallas_call | solution.py:186
  (9 shorter events, 0.1 us)
Async XLA Ops:
  0.6 2.8 %copy-start.1 = (f32[512,128]{1,0:T(8,128)S(1)}, f32[512,128]{1,0:T(8,128)}, u32[]{:S(2)}) copy-start(f32[512,128]{1,0:T(8,128)} %ref_plan_ref.3) | copy-start | bytes 786436
  0.6 2.8 %copy-start = (f32[512,512]{1,0:T(8,128)S(1)}, f32[512,512]{1,0:T(8,128)}, u32[]{:S(2)}) copy-start(f32[512,512]{1,0:T(8,128)} %ref_ref.1) | copy-start | bytes 3145732
  2.9 14.6 %copy-start.3 = (f32[128]{0:T(128)S(1)}, f32[128]{0:T(128)}, u32[]{:S(2)}) copy-start(f32[128]{0:T(128)} %param.9) | copy-start | bytes 1540
  2.9 6.3 %collective-permute-start = (f32[128,256]{1,0:T(8,128)S(1)}, f32[128,256]{1,0:T(8,128)S(1)}, u32[]{:S(2)}, u32[]{:S(2)}) collective-permute-start(f32[128,256]{1,0:T(8,128)S(1)} %get-tuple-element.37), channel_id=1, source_target_pairs={{0,4},{4,0},{1,5},{5,1},{2,6},{6,2},{3,7},{7,3},{8,12},{12,8},{9,1... | collective-permute-start | bytes 393224 | tf_op jit(solution)/shard_map/ppermute | solution.py:38
  3.9 8.3 %collective-permute-start.4 = (f32[32,256]{1,0:T(8,128)S(1)}, f32[32,256]{1,0:T(8,128)S(1)}, u32[]{:S(2)}, u32[]{:S(2)}) collective-permute-start(f32[32,256]{1,0:T(8,128)S(1)} %get-tuple-element.43), channel_id=1, source_target_pairs={{0,2},{1,3},{2,0},{3,1},{4,6},{5,7},{6,4},{7,5},{8,10},{9,11},{10,... | collective-permute-start | bytes 98312 | tf_op jit(solution)/shard_map/ppermute | solution.py:296
  7.6 5.7 %collective-permute-start.5 = (f32[32,256]{1,0:T(8,128)S(1)}, f32[32,256]{1,0:T(8,128)S(1)}, u32[]{:S(2)}, u32[]{:S(2)}) collective-permute-start(f32[32,256]{1,0:T(8,128)S(1)} %get-tuple-element.44), channel_id=1, source_target_pairs={{0,3},{1,2},{2,1},{3,0},{4,7},{5,6},{6,5},{7,4},{8,11},{9,10},{10,... | collective-permute-start | bytes 98312 | tf_op jit(solution)/shard_map/ppermute | solution.py:296
  8.9 4.4 %collective-permute-start.6 = (f32[32,256]{1,0:T(8,128)S(1)}, f32[32,256]{1,0:T(8,128)S(1)}, u32[]{:S(2)}, u32[]{:S(2)}) collective-permute-start(f32[32,256]{1,0:T(8,128)S(1)} %get-tuple-element.45), channel_id=1, source_target_pairs={{0,1},{1,0},{2,3},{3,2},{4,5},{5,4},{6,7},{7,6},{8,9},{9,8},{10,11... | collective-permute-start | bytes 98312 | tf_op jit(solution)/shard_map/ppermute | solution.py:296
  9.2 4.1 %collective-permute-start.1 = (f32[32,256]{1,0:T(8,128)S(1)}, f32[32,256]{1,0:T(8,128)S(1)}, u32[]{:S(2)}, u32[]{:S(2)}) collective-permute-start(f32[32,256]{1,0:T(8,128)S(1)} %get-tuple-element.39), channel_id=1, source_target_pairs={{0,8},{8,0},{16,24},{24,16},{1,9},{9,1},{17,25},{25,17},{2,10},{10... | collective-permute-start | bytes 98312 | tf_op jit(solution)/shard_map/ppermute | solution.py:308
  10.7 4.8 %collective-permute-start.2 = (f32[32,256]{1,0:T(8,128)S(1)}, f32[32,256]{1,0:T(8,128)S(1)}, u32[]{:S(2)}, u32[]{:S(2)}) collective-permute-start(f32[32,256]{1,0:T(8,128)S(1)} %get-tuple-element.40), channel_id=1, source_target_pairs={{0,24},{8,16},{16,8},{24,0},{1,25},{9,17},{17,9},{25,1},{2,26},{10... | collective-permute-start | bytes 98312 | tf_op jit(solution)/shard_map/ppermute | solution.py:308
  12.2 3.9 %collective-permute-start.3 = (f32[32,256]{1,0:T(8,128)S(1)}, f32[32,256]{1,0:T(8,128)S(1)}, u32[]{:S(2)}, u32[]{:S(2)}) collective-permute-start(f32[32,256]{1,0:T(8,128)S(1)} %get-tuple-element.41), channel_id=1, source_target_pairs={{0,16},{8,24},{16,0},{24,8},{1,17},{9,25},{17,1},{25,9},{2,18},{10... | collective-permute-start | bytes 98312 | tf_op jit(solution)/shard_map/ppermute | solution.py:308
  16.2 1.3 %collective-permute-start.7 = (f32[64,256]{1,0:T(8,128)S(1)}, f32[64,256]{1,0:T(8,128)S(1)}, u32[]{:S(2)}, u32[]{:S(2)}) collective-permute-start(f32[64,256]{1,0:T(8,128)S(1)} %shard_map.79.mine_ref.own_ref), channel_id=1, source_target_pairs={{0,4},{4,0},{1,5},{5,1},{2,6},{6,2},{3,7},{7,3},{8,12},{12,8},{9,1... | collective-permute-start | bytes 196616 | tf_op jit(solution)/shard_map/ppermute | solution.py:38
  18.1 17.2 %copy-start.2 = (f32[1024,128]{1,0:T(8,128)S(1)}, f32[1024,128]{1,0:T(8,128)}, u32[]{:S(2)}) copy-start(f32[1024,128]{1,0:T(8,128)} %cand_plan_ref.1) | copy-start | bytes 1572868
  33.7 1.5 %collective-permute-start.8 = (f32[432,128]{1,0:T(8,128)S(1)}, f32[432,128]{1,0:T(8,128)S(1)}, u32[]{:S(2)}, u32[]{:S(2)}) collective-permute-start(f32[432,128]{1,0:T(8,128)S(1)} %bitcast.4), channel_id=1, source_target_pairs={{0,4},{4,0},{1,5},{5,1},{2,6},{6,2},{3,7},{7,3},{8,12},{12,8},{9,1... | collective-permute-start | bytes 663560 | tf_op jit(solution)/shard_map/ppermute | solution.py:38

commit v7 on v6

--- a/solution.py
+++ b/solution.py
@@ -146,8 +146,8 @@
 
 
 load_steps = 4
-ref_order = [2, 3, 1]
-chip_order = [1, 3, 2]
+ref_orders = ([2, 3, 1], [3, 1, 2])
+chip_orders = ([3, 2, 1], [1, 3, 2])
 bf16 = jnp.bfloat16
 
 
@@ -220,7 +220,6 @@
     ref_total = ref_rows * refs
     half = width // cores
     ca, ra = rank // chips, rank // refs
-    cb, rb = ca // refs, ra // chips
     lanes = half // 128
     block_rows = lanes * ca
     few = -(-block_rows // (refs + 1))
@@ -229,8 +228,13 @@
     cand_sub = cand_rows // refs
     ref_sub = ref_rows // (chips * cores)
     everyone = chips * cores * refs
-    pairs = partner_lists(refs)
-    xor = refs & (refs - 1) == 0
+    ref_steps = [[0] + (ref_orders[c] if refs == 4 else list(range(1, refs))) for c in range(cores)]
+    chip_steps = [[0] + (chip_orders[c] if chips == 4 else list(range(1, chips))) for c in range(cores)]
+
+    def step_at(steps_of, k, core):
+        first, second = steps_of[0][k], steps_of[1][k]
+        return first if first == second else jnp.where(core == 0, first, second)
+
     weights_row = weights[None, :]
 
     steps = load_steps
@@ -279,7 +283,7 @@
         here = ref_in[:, pl.ds(pl.multiple_of(core * half, half), half)]
         whole[...] = rows_by_cols(ref_plan_in[...].T, here) / ref_total
         for k in range(refs):
-            to = ref ^ k if xor else (ref + k) % refs
+            to = ref ^ step_at(ref_steps, k, core)
             blocks[k][...] = whole[pl.ds(pl.multiple_of(to * ra, ra), ra), :]
         share = ref_in[pl.ds(pl.multiple_of(core * share_rows, share_rows), share_rows), :]
         share_high[...], share_low[...] = split(share)
@@ -292,20 +296,31 @@
         short_outs=(0, 1),
         room=8,
     )
-    order = ref_order if refs == 4 else list(range(1, refs))
-    blocks = [blocks[0]] + [lax.ppermute(blocks[k], "ref", pairs[k - 1]) for k in order]
+    blocks = [blocks[0]] + [
+        lax.ppermute(
+            blocks[k],
+            ("core", "ref"),
+            [(c * refs + i, c * refs + (i ^ ref_steps[c][k])) for c in range(cores) for i in range(refs)],
+        )
+        for k in range(1, refs)
+    ]
 
     def chip_blocks(keep_ref, came_ref, *rest):
         outs, full = rest[:-1], rest[-1]
-        chip = lax.axis_index("chip")
+        chip, core = lax.axis_index("chip"), lax.axis_index("core")
         full[...] = keep_ref[...] + came_ref[...]
         for k in range(chips):
-            outs[k][...] = full[pl.ds(pl.multiple_of((chip ^ k) * ca, ca), ca), :]
+            to = chip ^ step_at(chip_steps, k, core)
+            outs[k][...] = full[pl.ds(pl.multiple_of(to * ca, ca), ca), :]
 
     cand_blocks = call(chip_blocks, [(ca, half)] * chips, keep, came, scratch=[(rank, half)])
-    chip_pairs = partner_lists(chips)
     cand_blocks = [cand_blocks[0]] + [
-        lax.ppermute(cand_blocks[k], "chip", chip_pairs[k - 1]) for k in (chip_order if chips == 4 else range(1, chips))
+        lax.ppermute(
+            cand_blocks[k],
+            ("chip", "core"),
+            [(i * cores + c, (i ^ chip_steps[c][k]) * cores + c) for c in range(cores) for i in range(chips)],
+        )
+        for k in range(1, chips)
     ]
 
     def own_blocks(*rest):

time: 64.9 us -> 64.4 us (level)
  transfers between devices with their start and end apart: 9 -> 9, of which waited for: 5 -> 7; matrix products, arithmetic and copies ran while one was open for 0% -> 0% of each run, Pallas kernels for 2% -> 2%
where the time goes in v7:
time: 64.4 us; the launch traced here: 64.2 us
  blocking collectives  42.2 us (66%)
  starting transfers between devices  9.43 us (15%)
  Pallas kernels  6.81 us (11%)
  waiting for transfers between devices  5.03 us (8%)
  between operations  0.75 us (1%)
    all_to_all x3, blocking collectives, on_device_tiled(): mass = lax.all_to_all(out, ('chip', 'core', 'ref'), 0, 0)  27 us
    all_to_all x1, blocking collectives, on_device_tiled(): got = lax.all_to_all(to_all, ('chip', 'ref'), 0, 0).reshape(-1, 128)  15.2 us
    pallas_call x11, Pallas kernels, call(): pl.pallas_call(body, out_shape=[pltpu.HBM(s, f32) if i in slow_outs else...  6.81 us
    ppermute x3, starting transfers between devices, on_device_tiled(): lax.ppermute(blocks[k], ('core', 'ref'), [(c * refs + i, c * refs + (i ^...  5.24 us
    ppermute x3, starting transfers between devices, on_device_tiled(): lax.ppermute(cand_blocks[k], ('chip', 'core'), [(i * cores + c, (i ^ chip...  3.55 us
    ppermute x3, waiting for transfers between devices, on_device_tiled(): lax.ppermute(cand_blocks[k], ('chip', 'core'), [(i * cores + c, (i ^ chip...  2.68 us
    ppermute x3, waiting for transfers between devices, swap_core(): return lax.ppermute(array, 'core', [(0, 1), (1, 0)])  1.64 us
  transfers between devices with their start and end apart: 9, of which 7 were waited for; matrix products, arithmetic and copies ran while one was open for 0% of the time, Pallas kernels for 2%

profile of v7, /device:TPU:0, one launch (start us, length us, event | category | flops | bytes accessed | tf_op | source)
XLA Modules:
  0.0 64.2 jit_solution(17541797634249406239)
XLA Ops:
  0.7 2.2 %shard_map.76 = (f32[128,256]{1,0:T(8,128)S(1)}, f32[128,256]{1,0:T(8,128)S(1)}, bf16[1024,512]{1,0:T(8,128)(2,1)S(1)}, bf16[1024,512]{1,0:T(8,128)(2,1)S(1)}) custom-call(f32[1024,512]{1,0:T(8,128)} %cand_hbm.1, f32[1024,128]{1,0:T(8,128)} %cand_plan_ref.1), custom_call_target="tpu_custom_call" | custom-call | tf_op jit(solution)/shard_map/pallas_call | solution.py:186
  2.9 0.0 copy-start.3
  2.9 0.6 collective-permute-start
  3.5 0.4 shard_map.78
  3.9 3.7 %collective-permute-start.4 = (f32[32,256]{1,0:T(8,128)S(1)}, f32[32,256]{1,0:T(8,128)S(1)}, u32[]{:S(2)}, u32[]{:S(2)}) collective-permute-start(f32[32,256]{1,0:T(8,128)S(1)} %get-tuple-element.43), channel_id=1, source_target_pairs={{0,2},{1,3},{2,0},{3,1},{4,7},{5,6},{6,5},{7,4},{8,10},{9,11},{10,... | collective-permute-start | bytes 98312 | tf_op jit(solution)/shard_map/ppermute | solution.py:300
  7.6 1.4 %collective-permute-start.5 = (f32[32,256]{1,0:T(8,128)S(1)}, f32[32,256]{1,0:T(8,128)S(1)}, u32[]{:S(2)}, u32[]{:S(2)}) collective-permute-start(f32[32,256]{1,0:T(8,128)S(1)} %get-tuple-element.44), channel_id=1, source_target_pairs={{0,3},{1,2},{2,1},{3,0},{4,5},{5,4},{6,7},{7,6},{8,11},{9,10},{10,... | collective-permute-start | bytes 98312 | tf_op jit(solution)/shard_map/ppermute | solution.py:300
  8.9 0.2 collective-permute-start.6
  9.1 0.0 collective-permute-done.came_ref
  9.2 2.5 %collective-permute-start.1 = (f32[32,256]{1,0:T(8,128)S(1)}, f32[32,256]{1,0:T(8,128)S(1)}, u32[]{:S(2)}, u32[]{:S(2)}) collective-permute-start(f32[32,256]{1,0:T(8,128)S(1)} %get-tuple-element.39), channel_id=1, source_target_pairs={{0,24},{8,16},{16,8},{24,0},{4,12},{12,4},{20,28},{28,20},{1,25},{... | collective-permute-start | bytes 98312 | tf_op jit(solution)/shard_map/ppermute | solution.py:318
  11.7 0.5 collective-permute-start.2
  12.2 0.5 collective-permute-start.3
  12.7 0.6 collective-permute-done.5.rest_6_
  13.3 0.1 collective-permute-done.6.rest_7_
  13.4 0.7 %collective-permute-done.1.rest_1_ = f32[32,256]{1,0:T(8,128)S(1)} collective-permute-done((f32[32,256]{1,0:T(8,128)S(1)}, f32[32,256]{1,0:T(8,128)S(1)}, u32[]{:S(2)}, u32[]{:S(2)}) %collective-permute-start.1) | collective-permute-done | bytes 32800 | tf_op jit(solution)/shard_map/ppermute | solution.py:318
  14.2 1.5 %collective-permute-done.2.rest_2_ = f32[32,256]{1,0:T(8,128)S(1)} collective-permute-done((f32[32,256]{1,0:T(8,128)S(1)}, f32[32,256]{1,0:T(8,128)S(1)}, u32[]{:S(2)}, u32[]{:S(2)}) %collective-permute-start.2) | collective-permute-done | bytes 32800 | tf_op jit(solution)/shard_map/ppermute | solution.py:318
  15.6 0.5 collective-permute-done.3.rest_3_
  16.1 0.1 collective-permute-start.7
  16.2 0.5 shard_map.80
  16.7 0.7 %collective-permute-done.7.other_ref.own_ref = f32[64,256]{1,0:T(8,128)S(1)} collective-permute-done((f32[64,256]{1,0:T(8,128)S(1)}, f32[64,256]{1,0:T(8,128)S(1)}, u32[]{:S(2)}, u32[]{:S(2)}) %collective-permute-start.7) | collective-permute-done | bytes 65568 | tf_op jit(solution)/shard_map/ppermute | solution.py:38
  17.5 0.6 shard_map.81
  18.0 0.0 copy-start.2
  18.0 15.2 %all_to_all.20 = f32[16,27,1,128]{3,2,1,0:T(1,128)S(1)} all-to-all(f32[16,27,1,128]{3,2,1,0:T(1,128)S(1)} %bitcast.6), channel_id=1, replica_groups=mesh['chip'=4,'core'=2,'ref'=4] {'chip','ref'}, dimensions={0} | all-to-all | bytes 442368 | tf_op jit(solution)/shard_map/all_to_all | solution.py:409
  33.3 0.0 collective-permute-start.8
  33.3 0.5 shard_map.82
  33.8 0.9 %collective-permute-done.8.got_ref = f32[432,128]{1,0:T(8,128)S(1)} collective-permute-done((f32[432,128]{1,0:T(8,128)S(1)}, f32[432,128]{1,0:T(8,128)S(1)}, u32[]{:S(2)}, u32[]{:S(2)}) %collective-permute-start.8) | collective-permute-done | bytes 221216 | tf_op jit(solution)/shard_map/ppermute | solution.py:38
  34.7 0.7 %shard_map.83 = (f32[128,512]{1,0:T(8,128)S(1)}, f32[1024,128]{1,0:T(8,128)S(1)}, f32[8,128]{1,0:T(8,128)S(1)}, f32[256,128]{1,0:T(8,128)S(1)}, f32[64,128]{1,0:T(8,128)S(1)}, /*index=5*/f32[32,2,128]{2,1,0:T(2,128)S(1)}) custom-call(f32[432,128]{1,0:T(8,128)S(1)} %collective-permute-done.8.got_ref, f32[64,256]{1,0:T(8,128)S(1)} %collective-permute-done.7.other_ref.own_ref, ...), custom_call_target="tpu_custom_call" | custom-call | tf_op jit(solution)/shard_map/pallas_call | solution.py:186
  35.5 9.0 %all_to_all.21.mass_ref = f32[32,2,128]{2,1,0:T(2,128)S(1)} all-to-all(f32[32,2,128]{2,1,0:T(2,128)S(1)} %get-tuple-element.56), channel_id=1, replica_groups=mesh['chip'=4,'core'=2,'ref'=4] {'chip','core','ref'}, dimensions={0} | all-to-all | bytes 65536 | tf_op jit(solution)/shard_map/all_to_all | solution.py:529
  44.4 0.2 shard_map.84
  44.6 9.0 %all_to_all.22.mass_ref = f32[32,2,128]{2,1,0:T(2,128)S(1)} all-to-all(f32[32,2,128]{2,1,0:T(2,128)S(1)} %get-tuple-element.60), channel_id=1, replica_groups=mesh['chip'=4,'core'=2,'ref'=4] {'chip','core','ref'}, dimensions={0} | all-to-all | bytes 65536 | tf_op jit(solution)/shard_map/all_to_all | solution.py:529
  53.6 0.2 shard_map.85
  53.8 9.0 %all_to_all.23.mass_ref = f32[32,2,128]{2,1,0:T(2,128)S(1)} all-to-all(f32[32,2,128]{2,1,0:T(2,128)S(1)} %get-tuple-element.62), channel_id=1, replica_groups=mesh['chip'=4,'core'=2,'ref'=4] {'chip','core','ref'}, dimensions={0} | all-to-all | bytes 65536 | tf_op jit(solution)/shard_map/all_to_all | solution.py:531
  62.8 1.4 %shard_map.86 = (f32[1024,128]{1,0:T(8,128)}, f32[512,128]{1,0:T(8,128)}, f32[1,128]{1,0:T(1,128)}) custom-call(f32[32,2,128]{2,1,0:T(2,128)S(1)} %all_to_all.23.mass_ref, f32[128,512]{1,0:T(8,128)S(1)} %get-tuple-element.63.cand_moment, f32[8,128]{1,0:T(8,128)S(1)} %get-tuple-element.64.state_ref, f32[1024,128]{1,0:T(8,128)S(1)} %get-tuple-element.65.full_cand, ...), custom_call_target="tpu_custom_call" | custom-call | tf_op jit(solution)/shard_map/pallas_call | solution.py:186
  (9 shorter events, 0.1 us)
Async XLA Ops:
  0.6 2.8 %copy-start.1 = (f32[512,128]{1,0:T(8,128)S(1)}, f32[512,128]{1,0:T(8,128)}, u32[]{:S(2)}) copy-start(f32[512,128]{1,0:T(8,128)} %ref_plan_ref.3) | copy-start | bytes 786436
  0.6 2.8 %copy-start = (f32[512,512]{1,0:T(8,128)S(1)}, f32[512,512]{1,0:T(8,128)}, u32[]{:S(2)}) copy-start(f32[512,512]{1,0:T(8,128)} %ref_ref.1) | copy-start | bytes 3145732
  2.9 14.6 %copy-start.3 = (f32[128]{0:T(128)S(1)}, f32[128]{0:T(128)}, u32[]{:S(2)}) copy-start(f32[128]{0:T(128)} %param.9) | copy-start | bytes 1540
  2.9 6.3 %collective-permute-start = (f32[128,256]{1,0:T(8,128)S(1)}, f32[128,256]{1,0:T(8,128)S(1)}, u32[]{:S(2)}, u32[]{:S(2)}) collective-permute-start(f32[128,256]{1,0:T(8,128)S(1)} %get-tuple-element.37), channel_id=1, source_target_pairs={{0,4},{4,0},{1,5},{5,1},{2,6},{6,2},{3,7},{7,3},{8,12},{12,8},{9,1... | collective-permute-start | bytes 393224 | tf_op jit(solution)/shard_map/ppermute | solution.py:38
  3.9 8.3 %collective-permute-start.4 = (f32[32,256]{1,0:T(8,128)S(1)}, f32[32,256]{1,0:T(8,128)S(1)}, u32[]{:S(2)}, u32[]{:S(2)}) collective-permute-start(f32[32,256]{1,0:T(8,128)S(1)} %get-tuple-element.43), channel_id=1, source_target_pairs={{0,2},{1,3},{2,0},{3,1},{4,7},{5,6},{6,5},{7,4},{8,10},{9,11},{10,... | collective-permute-start | bytes 98312 | tf_op jit(solution)/shard_map/ppermute | solution.py:300
  7.6 5.7 %collective-permute-start.5 = (f32[32,256]{1,0:T(8,128)S(1)}, f32[32,256]{1,0:T(8,128)S(1)}, u32[]{:S(2)}, u32[]{:S(2)}) collective-permute-start(f32[32,256]{1,0:T(8,128)S(1)} %get-tuple-element.44), channel_id=1, source_target_pairs={{0,3},{1,2},{2,1},{3,0},{4,5},{5,4},{6,7},{7,6},{8,11},{9,10},{10,... | collective-permute-start | bytes 98312 | tf_op jit(solution)/shard_map/ppermute | solution.py:300
  8.9 4.5 %collective-permute-start.6 = (f32[32,256]{1,0:T(8,128)S(1)}, f32[32,256]{1,0:T(8,128)S(1)}, u32[]{:S(2)}, u32[]{:S(2)}) collective-permute-start(f32[32,256]{1,0:T(8,128)S(1)} %get-tuple-element.45), channel_id=1, source_target_pairs={{0,1},{1,0},{2,3},{3,2},{4,6},{5,7},{6,4},{7,5},{8,9},{9,8},{10,11... | collective-permute-start | bytes 98312 | tf_op jit(solution)/shard_map/ppermute | solution.py:300
  9.2 5.0 %collective-permute-start.1 = (f32[32,256]{1,0:T(8,128)S(1)}, f32[32,256]{1,0:T(8,128)S(1)}, u32[]{:S(2)}, u32[]{:S(2)}) collective-permute-start(f32[32,256]{1,0:T(8,128)S(1)} %get-tuple-element.39), channel_id=1, source_target_pairs={{0,24},{8,16},{16,8},{24,0},{4,12},{12,4},{20,28},{28,20},{1,25},{... | collective-permute-start | bytes 98312 | tf_op jit(solution)/shard_map/ppermute | solution.py:318
  11.7 3.9 %collective-permute-start.2 = (f32[32,256]{1,0:T(8,128)S(1)}, f32[32,256]{1,0:T(8,128)S(1)}, u32[]{:S(2)}, u32[]{:S(2)}) collective-permute-start(f32[32,256]{1,0:T(8,128)S(1)} %get-tuple-element.40), channel_id=1, source_target_pairs={{0,16},{8,24},{16,0},{24,8},{4,28},{12,20},{20,12},{28,4},{1,17},{... | collective-permute-start | bytes 98312 | tf_op jit(solution)/shard_map/ppermute | solution.py:318
  12.2 3.9 %collective-permute-start.3 = (f32[32,256]{1,0:T(8,128)S(1)}, f32[32,256]{1,0:T(8,128)S(1)}, u32[]{:S(2)}, u32[]{:S(2)}) collective-permute-start(f32[32,256]{1,0:T(8,128)S(1)} %get-tuple-element.41), channel_id=1, source_target_pairs={{0,8},{8,0},{16,24},{24,16},{4,20},{12,28},{20,4},{28,12},{1,9},{9... | collective-permute-start | bytes 98312 | tf_op jit(solution)/shard_map/ppermute | solution.py:318
  16.1 1.3 %collective-permute-start.7 = (f32[64,256]{1,0:T(8,128)S(1)}, f32[64,256]{1,0:T(8,128)S(1)}, u32[]{:S(2)}, u32[]{:S(2)}) collective-permute-start(f32[64,256]{1,0:T(8,128)S(1)} %shard_map.79.mine_ref.own_ref), channel_id=1, source_target_pairs={{0,4},{4,0},{1,5},{5,1},{2,6},{6,2},{3,7},{7,3},{8,12},{12,8},{9,1... | collective-permute-start | bytes 196616 | tf_op jit(solution)/shard_map/ppermute | solution.py:38
  18.0 16.7 %copy-start.2 = (f32[1024,128]{1,0:T(8,128)S(1)}, f32[1024,128]{1,0:T(8,128)}, u32[]{:S(2)}) copy-start(f32[1024,128]{1,0:T(8,128)} %cand_plan_ref.1) | copy-start | bytes 1572868
  33.3 1.5 %collective-permute-start.8 = (f32[432,128]{1,0:T(8,128)S(1)}, f32[432,128]{1,0:T(8,128)S(1)}, u32[]{:S(2)}, u32[]{:S(2)}) collective-permute-start(f32[432,128]{1,0:T(8,128)S(1)} %bitcast.4), channel_id=1, source_target_pairs={{0,4},{4,0},{1,5},{5,1},{2,6},{6,2},{3,7},{7,3},{8,12},{12,8},{9,1... | collective-permute-start | bytes 663560 | tf_op jit(solution)/shard_map/ppermute | solution.py:38
